TPU v7x, 32 devices: a whole 2x2x4 slice. The times are simulated.
32 devices in a mesh: row: 8 (over z, y), col: 4 (over x, core).
Axes of the slice: x: 2, y: 2, z: 4, core: 2. Of those that a mesh axis runs over, the one named last changes fastest.
Arguments:
- stack_embedding: bfloat16 [64, 160, 256], P('row', 'col'), may hold values from -6 to 6
- pair_representation: bfloat16 [160, 160, 128], P('row', 'col'), may hold values from -8 to 8
- mixing_entry_coefficients: bfloat16 [256, 1024], replicated, may hold values from -0.375 to 0.375
- mixing_final_coefficients: bfloat16 [256, 256], replicated, may hold values from -1 to 1
- pair_bias_matrix: bfloat16 [128, 8], replicated, may hold values from -4 to 4
- tensor_side_coefficients: bfloat16 [256, 64], replicated, may hold values from -0.375 to 0.375
- outer_output_weight: bfloat16 [1024, 128], replicated, may hold values from -1 to 1
- triangle_projection_weight: bfloat16 [128, 640], replicated, may hold values from -0.5 to 0.5
- triangle_output_weight: bfloat16 [128, 128], replicated, may hold values from -0.5 to 0.5
Outputs:
- stack_embedding_updated: bfloat16 [64, 160, 256], P('row', 'col')
- pair_state_next: bfloat16 [160, 160, 128], P('row', 'col')
All inputs are finite; a program needn't handle non-finite values.
Results may differ from a plain program's by a relative error of at most 0.015.
Values may be sent and summed in bfloat16 or wider, within the bound.
No kernel may reach another device: no remote copies, remote signals or barrier semaphores. Data moves between devices by JAX's collectives and lax.ppermute only.
A program may use at most 128 MiB of HBM per device.

v0:
```python
import jax
import jax.numpy as jnp
from jax import lax
from jax.sharding import PartitionSpec as P

epsilon = 1e-05


def standardize_features(inputs):
    inputs = inputs.astype(jnp.float32)
    center = inputs - jnp.mean(inputs, axis=-1, keepdims=True)
    spread = jnp.mean(center * center, axis=-1, keepdims=True)
    return center * lax.rsqrt(spread + epsilon)


def shards(
    stack_embedding,
    pair_representation,
    mixing_entry_coefficients,
    mixing_final_coefficients,
    pair_bias_matrix,
    tensor_side_coefficients,
    outer_output_weight,
    triangle_projection_weight,
    triangle_output_weight,
):
    sequences_per_device, residues_per_device, alignment_channels = stack_embedding.shape
    rows_dev = pair_representation.shape[0]
    pair_width = pair_representation.shape[2]
    number_heads = pair_bias_matrix.shape[1]
    head_channels = alignment_channels // number_heads
    outer_width = tensor_side_coefficients.shape[1] // 2
    row_count = lax.axis_size("row")
    seq_total = sequences_per_device * row_count
    row_index = lax.axis_index("row")
    normalized_input = (
        standardize_features(stack_embedding).astype(jnp.bfloat16).reshape(-1, alignment_channels)
    )
    mapped_lines = jnp.dot(
        normalized_input, mixing_entry_coefficients, preferred_element_type=jnp.float32
    )
    stack_probe_vectors = (
        (mapped_lines[:, :alignment_channels] * head_channels ** (-0.5))
        .astype(jnp.bfloat16)
        .reshape(sequences_per_device, residues_per_device, number_heads, head_channels)
    )
    stack_lookup_vectors = (
        mapped_lines[:, alignment_channels : 2 * alignment_channels]
        .astype(jnp.bfloat16)
        .reshape(sequences_per_device, residues_per_device, alignment_channels)
    )
    stack_content_vectors = (
        mapped_lines[:, 2 * alignment_channels : 3 * alignment_channels]
        .astype(jnp.bfloat16)
        .reshape(sequences_per_device, residues_per_device, alignment_channels)
    )
    sigmoid_factors = jax.nn.sigmoid(mapped_lines[:, 3 * alignment_channels :]).reshape(
        sequences_per_device, residues_per_device, alignment_channels
    )
    pair_normed = standardize_features(pair_representation).astype(jnp.bfloat16)
    bias_local = jnp.einsum(
        "ijc,ch->hij", pair_normed, pair_bias_matrix, preferred_element_type=jnp.float32
    ).astype(jnp.bfloat16)
    bias_all = lax.all_gather(bias_local, "row", axis=1, tiled=True)
    bias_query = lax.all_to_all(bias_all, "col", split_axis=1, concat_axis=2, tiled=True)
    best_score = jnp.full(
        (sequences_per_device, number_heads, residues_per_device), -1e30, jnp.float32
    )
    received_keys = lax.all_gather(stack_lookup_vectors, "col", axis=1, tiled=True)
    received_values = lax.all_gather(stack_content_vectors, "col", axis=1, tiled=True)
    key_count = received_keys.shape[1]
    received_keys = received_keys.reshape(
        sequences_per_device, key_count, number_heads, head_channels
    )
    received_values = received_values.reshape(
        sequences_per_device, key_count, number_heads, head_channels
    )
    bias_piece = bias_query.astype(jnp.float32)
    scores = (
        jnp.einsum(
            "yeca,yica->ycei",
            stack_probe_vectors,
            received_keys,
            preferred_element_type=jnp.float32,
        )
        + bias_piece[None]
    )
    next_best = jnp.maximum(best_score, jnp.max(scores, axis=-1))
    weights = jnp.exp(scores - next_best[..., None])
    next_sum = jnp.sum(weights, axis=-1)
    update = jnp.einsum(
        "shqk,skhd->sqhd",
        weights.astype(jnp.bfloat16),
        received_values,
        preferred_element_type=jnp.float32,
    )
    weighted_mixture = (update / jnp.transpose(next_sum, (0, 2, 1))[..., None]).reshape(
        sequences_per_device, residues_per_device, alignment_channels
    )
    scaled_mixture = (sigmoid_factors * weighted_mixture).astype(jnp.bfloat16)
    stack_increment = jnp.dot(
        scaled_mixture.reshape(-1, alignment_channels),
        mixing_final_coefficients,
        preferred_element_type=jnp.float32,
    ).reshape(sequences_per_device, residues_per_device, alignment_channels)
    stack_embedding_updated = (stack_embedding.astype(jnp.float32) + stack_increment).astype(
        jnp.bfloat16
    )
    tensor_standardized = (
        standardize_features(stack_embedding_updated)
        .astype(jnp.bfloat16)
        .reshape(-1, alignment_channels)
    )
    sides = jnp.dot(
        tensor_standardized, tensor_side_coefficients, preferred_element_type=jnp.float32
    ).astype(jnp.bfloat16)
    sides = sides.reshape(sequences_per_device, residues_per_device, 2 * outer_width)
    left_side = sides[..., :outer_width]
    right_side = sides[..., outer_width:]
    left_wide = lax.all_gather(left_side, "col", axis=1, tiled=True)
    left_every, right_all = (
        lax.all_gather(left_wide, "row", axis=0, tiled=True),
        lax.all_gather(right_side, "row", axis=0, tiled=True),
    )
    left_all = lax.dynamic_slice_in_dim(left_every, row_index * rows_dev, rows_dev, 1)
    products = jnp.einsum("sic,sjd->ijcd", left_all, right_all, preferred_element_type=jnp.float32)
    averaged = (products * (1.0 / seq_total)).astype(jnp.bfloat16)
    outer_update = jnp.dot(
        averaged.reshape(-1, outer_width * outer_width),
        outer_output_weight,
        preferred_element_type=jnp.float32,
    )
    pair_mid = (
        pair_representation.astype(jnp.float32)
        + outer_update.reshape(rows_dev, residues_per_device, pair_width)
    ).astype(jnp.bfloat16)
    tri_normed = standardize_features(pair_mid).astype(jnp.bfloat16).reshape(-1, pair_width)
    tri_parts = jnp.dot(
        tri_normed, triangle_projection_weight, preferred_element_type=jnp.float32
    ).reshape(rows_dev, residues_per_device, 5 * pair_width)
    left_edge = (
        jax.nn.sigmoid(tri_parts[..., pair_width : 2 * pair_width]) * tri_parts[..., :pair_width]
    ).astype(jnp.bfloat16)
    right_edge = (
        jax.nn.sigmoid(tri_parts[..., 3 * pair_width : 4 * pair_width])
        * tri_parts[..., 2 * pair_width : 3 * pair_width]
    ).astype(jnp.bfloat16)
    out_gate = jax.nn.sigmoid(tri_parts[..., 4 * pair_width :])
    right_rows = lax.all_gather(right_edge, "row", axis=0, tiled=True)
    right_query = lax.all_to_all(right_rows, "col", split_axis=0, concat_axis=1, tiled=True)
    arrived = lax.all_gather(left_edge, "col", axis=1, tiled=True)
    summed = jnp.einsum("ikc,jkc->ijc", arrived, right_query, preferred_element_type=jnp.float32)
    tri_ln = standardize_features(summed).astype(jnp.bfloat16)
    tri_update = jnp.dot(
        tri_ln.reshape(-1, pair_width), triangle_output_weight, preferred_element_type=jnp.float32
    ).reshape(rows_dev, residues_per_device, pair_width)
    pair_state_next = (pair_mid.astype(jnp.float32) + out_gate * tri_update).astype(jnp.bfloat16)
    return (stack_embedding_updated, pair_state_next)


def solution(mesh):
    return jax.shard_map(
        shards,
        mesh=mesh,
        in_specs=(P("row", "col", None), P("row", "col", None), P(), P(), P(), P(), P(), P(), P()),
        out_specs=(P("row", "col", None), P("row", "col", None)),
        check_vma=False,
    )
```

profile of v0, /device:TPU:0, one launch (start us, length us, event | category | flops | bytes accessed | tf_op | source)
XLA Modules:
  0.0 272.3 jit_solution(17193214005890169909)
XLA Ops:
  9.7 1.4 fusion.12
  11.0 32.7 %all_gather.26 = bf16[8,160,40]{2,0,1:T(8,128)(2,1)S(1)} all-gather(bf16[8,20,40]{2,0,1:T(8,128)(2,1)S(1)} %fusion.12), channel_id=1, replica_groups=mesh['row'=8,'col'=4] {'row'}, dimensions={1}, use_global_device_ids=true | all-gather | bytes 115200 | tf_op jit(solution)/shard_map/all_gather | solution.py:64
  44.8 3.3 %all-to-all-start = ((bf16[4,2,6400]{2,1,0:T(2,128)(2,1)}), bf16[4,2,6400]{2,1,0:T(2,128)(2,1)S(1)}, u32[]{:S(2)}, u32[]{:S(2)}) async-start(bf16[4,2,6400]{2,1,0:T(2,128)(2,1)} %reshape.141), calls=%async_computation | async-start | bytes 204800 | tf_op jit(solution)/shard_map/all_to_all | solution.py:65
  49.1 8.3 %all_gather.24 = bf16[8,160,256]{2,1,0:T(8,128)(2,1)S(1)} all-gather(bf16[8,40,256]{2,1,0:T(8,128)(2,1)S(1)} %bitcast.83), channel_id=1, replica_groups=mesh['row'=8,'col'=4] {'col'}, dimensions={1}, use_global_device_ids=true | all-gather | bytes 819200 | tf_op jit(solution)/shard_map/all_gather | solution.py:70
  57.4 8.4 %all_gather.25 = bf16[8,160,256]{2,1,0:T(8,128)(2,1)} all-gather(bf16[8,40,256]{2,1,0:T(8,128)(2,1)S(1)} %bitcast.82), channel_id=1, replica_groups=mesh['row'=8,'col'=4] {'col'}, dimensions={1}, use_global_device_ids=true | all-gather | bytes 819200 | tf_op jit(solution)/shard_map/all_gather | solution.py:69
  68.3 1.4 copy.53
  71.6 1.4 reshape.130
  73.0 1.7 add_reduce_fusion
  75.8 1.8 fusion.3
  77.6 1.7 copy.71
  83.2 6.2 %all_gather.28 = bf16[8,160,32]{2,0,1:T(8,128)(2,1)S(1)} all-gather(bf16[8,40,32]{2,0,1:T(8,128)(2,1)S(1)} %copy.60), channel_id=1, replica_groups=mesh['row'=8,'col'=4] {'col'}, dimensions={1}, use_global_device_ids=true | all-gather | bytes 102400 | tf_op jit(solution)/shard_map/all_gather | solution.py:120
  89.7 27.1 %all_gather.27 = bf16[64,40,32]{1,0,2:T(8,128)(2,1)S(1)} all-gather(bf16[8,40,32]{1,0,2:T(8,128)(2,1)S(1)} %copy.73), channel_id=1, replica_groups=mesh['row'=8,'col'=4] {'row'}, dimensions={0}, use_global_device_ids=true | all-gather | bytes 184320 | tf_op jit(solution)/shard_map/all_gather | solution.py:123
  116.8 32.9 %all_gather.29 = bf16[64,160,32]{1,2,0:T(8,128)(2,1)S(1)} all-gather(bf16[8,160,32]{1,2,0:T(8,128)(2,1)S(1)} %copy.61), channel_id=1, replica_groups=mesh['row'=8,'col'=4] {'row'}, dimensions={0}, use_global_device_ids=true | all-gather | bytes 737280 | tf_op jit(solution)/shard_map/all_gather | solution.py:122
  150.7 3.9 %fusion = bf16[20,40,32,32]{1,2,0,3:T(8,128)(2,1)} fusion(bf16[64,40,32]{1,0,2:T(8,128)(2,1)S(1)} %all_gather.27, bf16[64,20,32]{0,2,1:T(8,128)(2,1)S(1)} %copy.74), kind=kOutput, calls=%fused_computation.1 | convolution fusion | flops 106496000 | bytes 1884160 | tf_op jit(solution)/shard_map/sic,sjd->ijcd/dot_general | solution.py:126
  154.6 11.2 %copy.63 = bf16[20,40,32,32]{3,2,1,0:T(8,128)(2,1)} copy(bf16[20,40,32,32]{1,2,0,3:T(8,128)(2,1)} %fusion) | data formatting | bytes 3276800 | tf_op jit(solution)/shard_map/convert_element_type | solution.py:127
  165.8 9.1 %dot_general.45 = bf16[20,40,1024]{2,1,0:T(8,128)(2,1)S(1)} reshape(bf16[20,40,32,32]{3,2,1,0:T(8,128)(2,1)} %copy.63) | data formatting | bytes 3276800 | tf_op jit(solution)/shard_map/dot_general | solution.py:128
  178.9 44.9 %all-gather.2.cloned.1.call-done = bf16[160,40,128]{2,1,0:T(8,128)(2,1)} async-done(((bf16[20,40,128]{2,1,0:T(8,128)(2,1)}), bf16[160,40,128]{2,1,0:T(8,128)(2,1)}) %all-gather.2.cloned.1.call-update) | async-done | bytes 1638416 | tf_op jit(solution)/shard_map/all_gather | solution.py:149
  223.8 3.6 %all-to-all-start.1 = ((bf16[160,40,128]{2,1,0:T(8,128)(2,1)}), bf16[160,40,128]{2,1,0:T(8,128)(2,1)S(1)}, u32[]{:S(2)}, u32[]{:S(2)}) async-start(bf16[160,40,128]{2,1,0:T(8,128)(2,1)} %all-gather.2.cloned.1.call-done), calls=%async_computation.1 | async-start | bytes 3276800 | tf_op jit(solution)/shard_map/all_to_all | solution.py:150
  227.4 26.0 %all_gather.31 = bf16[20,160,128]{2,1,0:T(8,128)(2,1)S(1)} all-gather(bf16[20,40,128]{2,1,0:T(8,128)(2,1)} %get-tuple-element.2), channel_id=1, replica_groups=mesh['row'=8,'col'=4] {'col'}, dimensions={1}, use_global_device_ids=true | all-gather | bytes 1024000 | tf_op jit(solution)/shard_map/all_gather | solution.py:151
  253.4 1.9 copy.66
  255.3 1.4 copy.64
  256.7 3.7 %copy.65 = bf16[40,160,128]{1,0,2:T(8,128)(2,1)S(1)} copy(bf16[40,160,128]{2,1,0:T(8,128)(2,1)} %bitcast.76) | data formatting | bytes 3276800 | tf_op jit(solution)/shard_map/all_to_all | solution.py:150
  260.4 2.2 bitcast_reduce_fusion
  263.4 2.0 fusion.8
  (71 shorter events, 19.7 us)
Async XLA Ops:
  7.2 41.5 %copy-start = (bf16[256,1024]{1,0:T(8,128)(2,1)S(1)}, bf16[256,1024]{1,0:T(8,128)(2,1)}, u32[]{:S(2)}) copy-start(bf16[256,1024]{1,0:T(8,128)(2,1)} %param.11) | copy-start | bytes 1572868
  7.2 41.0 %copy-start.2 = (bf16[8,40,256]{2,1,0:T(8,128)(2,1)S(1)}, bf16[8,40,256]{2,1,0:T(8,128)(2,1)}, u32[]{:S(2)}) copy-start(bf16[8,40,256]{2,1,0:T(8,128)(2,1)} %param.9) | copy-start | bytes 491524
  44.8 24.9 %all-to-all-start = ((bf16[4,2,6400]{2,1,0:T(2,128)(2,1)}), bf16[4,2,6400]{2,1,0:T(2,128)(2,1)S(1)}, u32[]{:S(2)}, u32[]{:S(2)}) async-start(bf16[4,2,6400]{2,1,0:T(2,128)(2,1)} %reshape.141), calls=%async_computation | async-start | bytes 204800 | tf_op jit(solution)/shard_map/all_to_all | solution.py:65
  48.1 175.7 %all-gather.2.cloned.1.call-start = ((), (), s32[]{:S(2)}) async-start(), calls=%async_computation.2 | async-start | bytes 1843200 | tf_op jit(solution)/shard_map/all_gather | solution.py:149
  74.6 1.2 copy-start.5
  77.6 3.9 %copy-start.8 = (bf16[256,256]{1,0:T(8,128)(2,1)S(1)}, bf16[256,256]{1,0:T(8,128)(2,1)}, u32[]{:S(2)}) copy-start(bf16[256,256]{1,0:T(8,128)(2,1)} %param.12) | copy-start | bytes 393220
  79.3 3.3 %copy-start.9 = (bf16[256,64]{0,1:T(8,128)(2,1)S(1)}, bf16[256,64]{0,1:T(8,128)(2,1)}, u32[]{:S(2)}) copy-start(bf16[256,64]{0,1:T(8,128)(2,1)} %param.14) | copy-start | bytes 98308
  81.8 0.7 copy-start.4
  165.8 9.1 %copy-start.3 = (bf16[20,40,128]{2,1,0:T(8,128)(2,1)S(1)}, bf16[20,40,128]{2,1,0:T(8,128)(2,1)}, u32[]{:S(2)}) copy-start(bf16[20,40,128]{2,1,0:T(8,128)(2,1)} %param.10) | copy-start | bytes 614404
  165.8 9.1 %copy-start.6 = (bf16[1024,128]{1,0:T(8,128)(2,1)S(1)}, bf16[1024,128]{1,0:T(8,128)(2,1)}, u32[]{:S(2)}) copy-start(bf16[1024,128]{1,0:T(8,128)(2,1)} %param.15) | copy-start | bytes 786436
  174.9 1.0 copy-start.7
  176.6 1.3 copy-start.1
  223.8 31.5 %all-to-all-start.1 = ((bf16[160,40,128]{2,1,0:T(8,128)(2,1)}), bf16[160,40,128]{2,1,0:T(8,128)(2,1)S(1)}, u32[]{:S(2)}, u32[]{:S(2)}) async-start(bf16[160,40,128]{2,1,0:T(8,128)(2,1)} %all-gather.2.cloned.1.call-done), calls=%async_computation.1 | async-start | bytes 3276800 | tf_op jit(solution)/shard_map/all_to_all | solution.py:150
  262.6 0.8 copy-start.10
Sparse Core Ops, SparseCore 0:
  179.1 44.7 all-gather.1
where the time goes:
time: 273 us; the launch traced here: 272 us
  blocking collectives  142 us (52%)
  waiting for transfers between devices  44.9 us (16%)
  local copies, waits for them, and re-layouts  42.1 us (15%)
  matrix products  15 us (5%)
  between operations  14.4 us (5%)
  other arithmetic  7.22 us (3%)
  starting transfers between devices  6.92 us (3%)
    all_gather x1, waiting for transfers between devices, shards(): right_rows = lax.all_gather(right_edge, 'row', axis=0, tiled=True)  44.9 us
    all_gather x1, blocking collectives, shards(): lax.all_gather(left_wide, 'row', axis=0, tiled=True)  32.9 us
    all_gather x1, blocking collectives, shards(): bias_all = lax.all_gather(bias_local, 'row', axis=1, tiled=True)  32.7 us
    all_gather x1, blocking collectives, shards(): lax.all_gather(right_side, 'row', axis=0, tiled=True)  27.1 us
    all_gather x1, blocking collectives, shards(): arrived = lax.all_gather(left_edge, 'col', axis=1, tiled=True)  26 us
    convert_element_type x1, local copies, waits for them, and re-layouts, shards(): averaged = (products * (1.0 / seq_total)).astype(jnp.bfloat16)  11.2 us
    dot_general x1, local copies, waits for them, and re-layouts, shards(): jnp.dot(averaged.reshape(-1, outer_width * outer_width), outer_output_wei...  9.08 us
    all_gather x1, blocking collectives, shards(): lax.all_gather(stack_lookup_vectors, 'col', axis=1, tiled=True)  8.43 us
  transfers between devices with their start and end apart: 3, of which 1 were waited for; matrix products, arithmetic and copies ran while one was open for 2% of the time, Pallas kernels for 0%

commit v1 on v0

--- a/solution.py
+++ b/solution.py
@@ -1,19 +1,415 @@
+import functools
+
 import jax
 import jax.numpy as jnp
+import numpy as np
 from jax import lax
+from jax.experimental import pallas as pl
+from jax.experimental.pallas import tpu as pltpu
 from jax.sharding import PartitionSpec as P
 
 epsilon = 1e-05
-
-
-def standardize_features(inputs):
+LANES = 128
+SUBLANES = 8
+F32 = jnp.float32
+BF16 = jnp.bfloat16
+ALL = ("row", "col")
+NT = (((1,), (1,)), ((), ()))
+VMEM = pl.BlockSpec(memory_space=pltpu.VMEM)
+SMEM = pl.BlockSpec(memory_space=pltpu.SMEM)
+
+
+def standardize_features(inputs, axis=-1):
     inputs = inputs.astype(jnp.float32)
-    center = inputs - jnp.mean(inputs, axis=-1, keepdims=True)
-    spread = jnp.mean(center * center, axis=-1, keepdims=True)
+    center = inputs - jnp.mean(inputs, axis=axis, keepdims=True)
+    spread = jnp.mean(center * center, axis=axis, keepdims=True)
     return center * lax.rsqrt(spread + epsilon)
 
 
-def shards(
+def dot(a, b):
+    return jnp.dot(a, b, preferred_element_type=F32)
+
+
+def dot_nt(a, b):
+    return lax.dot_general(a, b, NT, preferred_element_type=F32)
+
+
+def lane_iota(rows):
+    return lax.broadcasted_iota(jnp.int32, (rows, LANES), 1)
+
+
+def call(body, out_shape, scratch, in_specs, name):
+    return pl.pallas_call(
+        body,
+        out_shape=out_shape,
+        in_specs=in_specs,
+        out_specs=jax.tree.map(lambda _: VMEM, out_shape),
+        scratch_shapes=scratch,
+        name=name,
+        compiler_params=pltpu.CompilerParams(vmem_limit_bytes=40 * 1024 * 1024),
+    )
+
+
+class Plan:
+    def __init__(self, n_row, n_col, x, pair, heads, outer, channels_out):
+        self.n_row, self.n_col, self.n = n_row, n_col, n_row * n_col
+        self.seqs, self.res, self.feat = x
+        self.rows, self.cols, self.width = pair
+        self.heads, self.outer = heads, outer
+        self.hd = self.feat // heads
+        self.total = self.res * n_col
+        self.ok = False
+        if self.seqs % n_col or self.width != LANES or heads != SUBLANES or self.cols != self.res:
+            return
+        if self.rows * n_row != self.total or self.feat % LANES:
+            return
+        self.own = self.seqs // n_col
+        self.seq_total = self.own * self.n
+        self.i_main = LANES // heads
+        self.i_rem = self.rows - self.i_main
+        if not 0 < self.i_rem or LANES % (self.i_rem * heads) or self.cols % SUBLANES:
+            return
+        self.rem = self.i_rem * heads
+        self.fold = LANES // self.rem
+        if n_row % self.fold:
+            return
+        self.groups = self.cols // SUBLANES
+        self.rem_rows = -(-self.groups // self.fold)
+        self.bias_rows = self.cols + SUBLANES * self.rem_rows
+        if LANES % outer:
+            return
+        self.pack = LANES // outer
+        if self.rows % self.pack or self.cols % self.pack:
+            return
+        self.lk, self.rk = self.rows // self.pack, self.cols // self.pack
+        used = (self.lk + self.rk) * self.own
+        self.side_rows = -(-used // 16) * 16
+        self.cpad = -(-self.cols // 16) * 16
+        if self.width % self.n:
+            return
+        self.ch = self.width // self.n
+        if 2 * self.ch != SUBLANES or n_row % n_col:
+            return
+        self.q = LANES // self.cols
+        self.ig = -(-self.rows // self.q)
+        self.ipad = self.ig * self.q
+        self.per = n_row // n_col
+        self.jslot = self.per * self.ipad
+        if self.per * self.rows != self.cols or self.q * self.jslot > LANES:
+            return
+        self.m = n_row * self.ig
+        self.edge_rows = self.ig * SUBLANES
+        self.back_rows = -(-self.ig * self.ch // 16) * 16
+        self.ok = True
+
+    def j_base(self, c):
+        return (c // self.q) * LANES + (c % self.q) * self.jslot
+
+
+def bias_kernel(p, pair_ref, w_ref, out_ref):
+    normed = standardize_features(pair_ref[...])
+    heads = p.heads
+    spread = (lax.broadcasted_iota(jnp.int32, (heads, LANES), 1) % heads
+              == lax.broadcasted_iota(jnp.int32, (heads, LANES), 0))
+    tiled = dot(w_ref[...], jnp.where(spread, 1.0, 0.0).astype(BF16))
+    slot = lane_iota(p.width) // heads
+    main = jnp.zeros((p.cols, LANES), F32)
+    rem = jnp.zeros((p.cols, LANES), F32)
+    for i in range(p.rows):
+        block = normed[i * p.cols:(i + 1) * p.cols].astype(BF16)
+        if i < p.i_main:
+            main += dot(block, jnp.where(slot == i, tiled, 0.0).astype(BF16))
+        else:
+            rem += dot(block, jnp.where(slot % p.i_rem == i - p.i_main, tiled, 0.0).astype(BF16))
+    piece = [main]
+    at = lane_iota(SUBLANES) // p.rem
+    for k in range(p.rem_rows):
+        folded = jnp.zeros((SUBLANES, LANES), F32)
+        for f in range(p.fold):
+            g = k * p.fold + f
+            if g < p.groups:
+                folded = jnp.where(at == f, rem[g * SUBLANES:(g + 1) * SUBLANES], folded)
+        piece.append(folded)
+    piece = jnp.concatenate(piece, axis=0).astype(BF16)
+    for d in range(p.n):
+        out_ref[d] = piece
+
+
+def project_kernel(p, col_ref, *refs):
+    x_refs = refs[:p.n_col]
+    w_ref, q_ref, k_ref, v_ref, gate_ref, x_out, hold = refs[p.n_col:]
+    me = col_ref[0]
+    for shift in range(p.n_col):
+        hold[lax.rem(me + (p.n_col - shift), p.n_col)] = x_refs[shift][...].astype(F32)
+    f = p.feat
+    for s in range(p.own):
+        x = jnp.concatenate([hold[c, s] for c in range(p.n_col)], axis=0)
+        x_out[s] = x
+        lines = dot(standardize_features(x).astype(BF16), w_ref[...])
+        q_ref[s] = (lines[:, :f] * p.hd ** (-0.5)).astype(BF16)
+        k_ref[s] = lines[:, f:2 * f].astype(BF16)
+        v_ref[s] = lines[:, 2 * f:3 * f].astype(BF16)
+        gate_ref[s] = jax.nn.sigmoid(lines[:, 3 * f:])
+
+
+def attend_kernel(p, q_ref, k_ref, v_ref, gate_ref, x_ref, bias_ref, sel_ref, wf_ref, wl_ref, wr_ref,
+                  emb_ref, side_ref, bias, l4, r4, lint, rint, send):
+    h, t, f = p.heads, p.total, p.feat
+    main = p.n_row * LANES
+    for r in range(p.n_row):
+        for c in range(p.n_col):
+            bias[c * p.cols:(c + 1) * p.cols, r * LANES:(r + 1) * LANES] = (
+                bias_ref[r * p.n_col + c, 0:p.cols].astype(F32))
+    at = lane_iota(SUBLANES) // p.rem
+    for c in range(p.n_col):
+        for b in range(p.n_row // p.fold):
+            tails = [bias_ref[(b * p.fold + u) * p.n_col + c, p.cols:p.bias_rows].astype(F32)
+                     for u in range(p.fold)]
+            for g in range(p.groups):
+                k, part = g // p.fold, g % p.fold
+                block = jnp.zeros((SUBLANES, LANES), F32)
+                for u in range(p.fold):
+                    piece = tails[u][k * SUBLANES:(k + 1) * SUBLANES]
+                    turn = ((u - part) * p.rem) % LANES
+                    if turn:
+                        piece = pltpu.roll(piece, turn, axis=1)
+                    block = jnp.where(at == u, piece, block)
+                bias[c * p.cols + g * SUBLANES:c * p.cols + (g + 1) * SUBLANES,
+                     main + b * LANES:main + (b + 1) * LANES] = block
+    head_of = (lax.broadcasted_iota(jnp.int32, (h, f), 1) // p.hd
+               == lax.broadcasted_iota(jnp.int32, (h, f), 0))
+    head_mask = jnp.where(head_of, 1.0, 0.0)
+    wide = t * h
+    own_head = (lax.broadcasted_iota(jnp.int32, (f, wide), 0) // p.hd
+                == lax.broadcasted_iota(jnp.int32, (f, wide), 1) % h)
+    lane = lane_iota(t // p.pack) // p.outer
+    for s in range(p.own):
+        q = q_ref[s].astype(F32)
+        spread = jnp.broadcast_to(q[:, None, :], (t, h, f)) * head_mask[None]
+        parts = [spread[r * p.rows:r * p.rows + p.i_main] for r in range(p.n_row)]
+        parts += [spread[r * p.rows + p.i_main:(r + 1) * p.rows] for r in range(p.n_row)]
+        spread = jnp.concatenate(parts, axis=0).reshape(wide, f).astype(BF16)
+        scores = dot_nt(k_ref[s], spread) + bias[...]
+        peak = jnp.max(scores, axis=0, keepdims=True)
+        weights = jnp.exp(scores - peak)
+        total = jnp.sum(weights, axis=0, keepdims=True)
+        v_t = jnp.transpose(v_ref[s].astype(F32)).astype(BF16)
+        mixed = dot(v_t, weights.astype(BF16)) * (1.0 / total)
+        mixed = jnp.where(own_head, mixed, 0.0).astype(BF16)
+        attended = dot_nt(sel_ref[...], mixed)
+        gated = (gate_ref[s] * attended).astype(BF16)
+        new = (x_ref[s] + dot(gated, wf_ref[...])).astype(BF16).astype(F32)
+        for c in range(p.n_col):
+            emb_ref[c, s] = new[c * p.res:(c + 1) * p.res].astype(BF16)
+        normed = standardize_features(new).astype(BF16)
+        for w_ref, four, woven in ((wl_ref, l4, lint), (wr_ref, r4, rint)):
+            four[...] = dot(normed, w_ref[...])
+            packed = four[pl.ds(0, t // p.pack, stride=p.pack), :]
+            for a in range(1, p.pack):
+                packed = jnp.where(lane == a, four[pl.ds(a, t // p.pack, stride=p.pack), :], packed)
+            woven[pl.ds(s, t // p.pack, stride=p.own), :] = packed
+    nr, nl = p.rk * p.own, p.lk * p.own
+    for r in range(p.n_row):
+        for c in range(p.n_col):
+            d = r * p.n_col + c
+            send[d, 0:nr] = rint[c * nr:(c + 1) * nr]
+            send[d, nr:nr + nl] = lint[r * nl:(r + 1) * nl]
+            if nr + nl < p.side_rows:
+                send[d, nr + nl:p.side_rows] = jnp.zeros((p.side_rows - nr - nl, LANES), F32)
+    side_ref[...] = send[...].astype(BF16)
+
+
+def outer_kernel(p, recv_ref, pair_ref, wbd_ref, wv_ref, wg_ref, mid_ref, edge_ref,
+                 flat, rt, lhs, mid):
+    flat[...] = recv_ref[...].reshape(p.n * p.side_rows, LANES).astype(F32)
+
+    def chunk(k):
+        return jnp.concatenate(
+            [flat[pl.ds(k * p.own + s, p.n, stride=p.side_rows), :] for s in range(p.own)], axis=0)
+
+    left = jnp.concatenate([chunk(p.rk + k) for k in range(p.lk)], axis=1).astype(BF16)
+    for k in range(p.rk):
+        rt[k * LANES:(k + 1) * LANES, :] = jnp.transpose(chunk(k))
+    right = jnp.concatenate(
+        [rt[pl.ds(d, p.cols, stride=p.outer), :] for d in range(p.outer)], axis=0).astype(BF16)
+    products = dot(right, left) * (1.0 / p.seq_total)
+    for d in range(p.outer):
+        for g in range(p.lk):
+            lhs[g * p.cpad:g * p.cpad + p.cols, d * LANES:(d + 1) * LANES] = products[
+                d * p.cols:(d + 1) * p.cols, g * LANES:(g + 1) * LANES].astype(BF16)
+            if p.cpad > p.cols:
+                lhs[g * p.cpad + p.cols:(g + 1) * p.cpad, d * LANES:(d + 1) * LANES] = jnp.zeros(
+                    (p.cpad - p.cols, LANES), BF16)
+    update = dot(lhs[...], wbd_ref[...])
+    for i in range(p.rows):
+        g, a = i // p.pack, i % p.pack
+        fresh = (pair_ref[i].astype(F32)
+                 + update[g * p.cpad:g * p.cpad + p.cols, a * p.width:(a + 1) * p.width]).astype(BF16)
+        mid_ref[i] = fresh
+        mid[i * p.cols:(i + 1) * p.cols, :] = fresh.astype(F32)
+    tail = mid.shape[0] - p.rows * p.cols
+    mid[p.rows * p.cols:, :] = jnp.zeros((tail, LANES), F32)
+    step = p.q * p.cols
+    for k in range(p.ig):
+        normed = standardize_features(mid[k * step:k * step + LANES, :]).astype(BF16)
+        value = dot_nt(wv_ref[...], normed)
+        gate = jax.nn.sigmoid(dot_nt(wg_ref[...], normed))
+        edge_ref[:, k * SUBLANES:(k + 1) * SUBLANES, :] = (gate * value).reshape(
+            p.n, SUBLANES, LANES).astype(BF16)
+
+
+def gate_kernel(p, mid_ref, w_ref, out_ref):
+    normed = standardize_features(mid_ref[...]).reshape(p.rows * p.cols, p.width).astype(BF16)
+    out_ref[...] = jax.nn.sigmoid(dot(normed, w_ref[...]))
+
+
+def triangle_kernel(p, recv_ref, out_ref, flat, ls, rs, os, sb):
+    for r in range(p.n_row):
+        for c in range(p.n_col):
+            flat[c, r * p.edge_rows:(r + 1) * p.edge_rows, :] = recv_ref[r * p.n_col + c].astype(F32)
+    lane = lane_iota(p.m)
+    blocks = p.per * p.ig
+    rs[...] = jnp.zeros_like(rs)
+    for ch in range(p.ch):
+        for c in range(p.n_col):
+            left = flat[c, pl.ds(ch, p.m, stride=SUBLANES), :]
+            right = flat[c, pl.ds(p.ch + ch, p.m, stride=SUBLANES), :]
+            for a in range(p.q):
+                turn = (-a * p.cols) % LANES
+                lt = pltpu.roll(left, turn, axis=1) if turn else left
+                rt = pltpu.roll(right, turn, axis=1) if turn else right
+                ls[ch, c, pl.ds(a, p.m, stride=p.q), :] = jnp.where(lane < p.cols, lt, 0.0)
+                for first in range(0, p.n_col, p.q):
+                    many = min(p.q, p.n_col - first) * blocks
+                    rs[ch, c, pl.ds(p.j_base(first) + a, many, stride=p.q), :] = rt[
+                        first * blocks:first * blocks + many]
+    for ch in range(p.ch):
+        lfull = jnp.concatenate([ls[ch, c] for c in range(p.n_col)], axis=1).astype(BF16)
+        rfull = jnp.concatenate([rs[ch, c] for c in range(p.n_col)], axis=1).astype(BF16)
+        summed = dot_nt(lfull, rfull)
+        for b in range(summed.shape[1] // LANES):
+            os[ch, b] = summed[:, b * LANES:(b + 1) * LANES]
+        rows = [[os[ch, b, pl.ds(a, p.m, stride=p.q), :] for a in range(p.q)]
+                for b in range(summed.shape[1] // LANES)]
+        for c in range(p.n_col):
+            b, part = c // p.q, c % p.q
+            packed = None
+            for a in range(p.q):
+                turn = ((a - part) * p.jslot) % LANES
+                piece = pltpu.roll(rows[b][a], turn, axis=1) if turn else rows[b][a]
+                packed = piece if packed is None else jnp.where(lane // p.jslot == a, piece, packed)
+            sb[c, pl.ds(ch, p.m, stride=p.ch), :] = packed
+    used = p.ig * p.ch
+    for r in range(p.n_row):
+        for c in range(p.n_col):
+            d = r * p.n_col + c
+            out_ref[d, 0:used] = sb[c, r * used:(r + 1) * used, :].astype(BF16)
+            if used < p.back_rows:
+                out_ref[d, used:p.back_rows] = jnp.zeros((p.back_rows - used, LANES), BF16)
+
+
+def final_kernel(p, recv_ref, mid_ref, gate_ref, w_ref, out_ref, flat, hold, update):
+    flat[...] = recv_ref[...].reshape(p.n * p.back_rows, LANES).astype(F32)
+    for k in range(p.ig):
+        summed = jnp.concatenate(
+            [flat[pl.ds(k * p.ch + ch, p.n, stride=p.back_rows), :] for ch in range(p.ch)], axis=0)
+        normed = jnp.transpose(standardize_features(summed, axis=0)).astype(BF16)
+        hold[...] = dot(normed, w_ref[...])
+        for a in range(p.q):
+            i = k * p.q + a
+            if i < p.rows:
+                for u in range(p.per):
+                    update[i * p.cols + u * p.rows:i * p.cols + (u + 1) * p.rows, :] = hold[
+                        a * p.jslot + u * p.ipad:a * p.jslot + u * p.ipad + p.rows, :]
+    fresh = mid_ref[...].astype(F32).reshape(p.rows * p.cols, p.width) + gate_ref[...] * update[...]
+    out_ref[...] = fresh.reshape(p.rows, p.cols, p.width).astype(BF16)
+
+
+def fast(p, x, pair, w_in, w_out, w_bias, w_side, w_outer, w_tri, w_last):
+    col = lax.axis_index("col")
+    n, ch, width = p.n, p.ch, p.width
+    sds = jax.ShapeDtypeStruct
+
+    left_w, right_w = w_side[:, :p.outer], w_side[:, p.outer:]
+    left_w, right_w = jnp.tile(left_w, (1, p.pack)), jnp.tile(right_w, (1, p.pack))
+    by_d = jnp.transpose(w_outer.reshape(p.outer, p.outer, width), (1, 0, 2))
+    eye = jnp.eye(p.pack, dtype=bool)
+    w_bd = jnp.where(eye[None, :, None, :, None], by_d[:, None, :, None, :], jnp.zeros((), BF16)).reshape(
+        p.outer * LANES, p.pack * width)
+    blocks = jnp.transpose(w_tri.reshape(width, 5, width), (1, 2, 0)).reshape(5, n, ch, width)
+    value_w = jnp.concatenate([blocks[0], blocks[2]], axis=1).reshape(n * 2 * ch, width)
+    gate_w = jnp.concatenate([blocks[1], blocks[3]], axis=1).reshape(n * 2 * ch, width)
+    own_gate_w = w_tri[:, 4 * width:]
+    last_w = jnp.transpose(w_last.reshape(n, ch, width), (1, 0, 2)).reshape(width, width)
+    spot = np.arange(p.total).reshape(p.n_row, p.rows)
+    order = np.concatenate([spot[:, :p.i_main].reshape(-1), spot[:, p.i_main:].reshape(-1)])
+    sel = jnp.asarray((np.arange(p.total)[:, None] == np.repeat(order, p.heads)[None]), BF16)
+
+    piece = call(functools.partial(bias_kernel, p), sds((n, p.bias_rows, LANES), BF16), [], [VMEM] * 2, "bias")(
+        pair.reshape(p.rows * p.cols, width), w_bias)
+    bias = lax.all_to_all(piece, ALL, 0, 0, tiled=True)
+    chunks = x.reshape(p.n_col, p.own, p.res, p.feat)
+    parts = []
+    for shift in range(p.n_col):
+        part = lax.dynamic_index_in_dim(chunks, lax.rem(col + shift, p.n_col), 0, keepdims=False)
+        if shift:
+            part = lax.ppermute(part, "col", [(c, (c + shift) % p.n_col) for c in range(p.n_col)])
+        parts.append(part)
+    seq = (p.own, p.total, p.feat)
+    q, k, v, gate, whole = call(
+        functools.partial(project_kernel, p),
+        (sds(seq, BF16), sds(seq, BF16), sds(seq, BF16), sds(seq, F32), sds(seq, F32)),
+        [pltpu.VMEM((p.n_col, p.own, p.res, p.feat), F32)],
+        [SMEM] + [VMEM] * (p.n_col + 1), "project")(col.reshape(1), *parts, w_in)
+    emb, sides = call(
+        functools.partial(attend_kernel, p),
+        (sds((p.n_col, p.own, p.res, p.feat), BF16), sds((n, p.side_rows, LANES), BF16)),
+        [pltpu.VMEM((p.total, p.total * p.heads), F32)]
+        + [pltpu.VMEM((p.total, LANES), F32)] * 2
+        + [pltpu.VMEM((p.total // p.pack * p.own, LANES), F32)] * 2
+        + [pltpu.VMEM((n, p.side_rows, LANES), F32)],
+        [VMEM] * 10, "attend")(q, k, v, gate, whole, bias, sel, w_out, left_w, right_w)
+
+    sides = lax.all_to_all(sides, ALL, 0, 0, tiled=True)
+    mid, edges = call(
+        functools.partial(outer_kernel, p),
+        (sds((p.rows, p.cols, width), BF16), sds((n, p.edge_rows, LANES), BF16)),
+        [pltpu.VMEM((n * p.side_rows, LANES), F32),
+         pltpu.VMEM((p.rk * LANES, p.seq_total), F32),
+         pltpu.VMEM((p.lk * p.cpad, p.outer * LANES), BF16),
+         pltpu.VMEM(((p.ig - 1) * p.q * p.cols + LANES, LANES), F32)],
+        [VMEM] * 5, "outer")(sides, pair, w_bd, value_w, gate_w)
+
+    edges = lax.all_to_all(edges, ALL, 0, 0, tiled=True)
+    out_gate = call(functools.partial(gate_kernel, p), sds((p.rows * p.cols, width), F32), [], [VMEM] * 2, "gate")(
+        mid, own_gate_w)
+    n_lane = p.j_base(p.n_col - 1) // LANES + 1
+    back = call(
+        functools.partial(triangle_kernel, p), sds((n, p.back_rows, LANES), BF16),
+        [pltpu.VMEM((p.n_col, p.n_row * p.edge_rows, LANES), F32),
+         pltpu.VMEM((ch, p.n_col, p.m * p.q, LANES), F32),
+         pltpu.VMEM((ch, p.n_col, n_lane * LANES, LANES), F32),
+         pltpu.VMEM((ch, n_lane, p.m * p.q, LANES), F32),
+         pltpu.VMEM((p.n_col, p.m * ch, LANES), F32)],
+        [VMEM], "triangle")(edges)
+
+    home = jnp.zeros((p.n_col, p.own, p.res, p.feat), BF16)
+    for shift in range(p.n_col):
+        part = lax.dynamic_index_in_dim(emb, lax.rem(col + shift, p.n_col), 0, keepdims=False)
+        if shift:
+            part = lax.ppermute(part, "col", [(c, (c + shift) % p.n_col) for c in range(p.n_col)])
+        home = lax.dynamic_update_index_in_dim(home, part, lax.rem(col + p.n_col - shift, p.n_col), 0)
+
+    back = lax.all_to_all(back, ALL, 0, 0, tiled=True)
+    state = call(
+        functools.partial(final_kernel, p), sds((p.rows, p.cols, width), BF16),
+        [pltpu.VMEM((n * p.back_rows, LANES), F32), pltpu.VMEM((LANES, LANES), F32),
+         pltpu.VMEM((p.rows * p.cols, LANES), F32)],
+        [VMEM] * 4, "final")(back, mid, out_gate, last_w)
+    return home.reshape(x.shape), state
+
+
+def general(
     stack_embedding,
     pair_representation,
     mixing_entry_coefficients,
@@ -158,6 +554,13 @@
     return (stack_embedding_updated, pair_state_next)
 
 
+def shards(x, pair, w_in, w_out, w_bias, w_side, w_outer, w_tri, w_last):
+    p = Plan(lax.axis_size("row"), lax.axis_size("col"), x.shape, pair.shape, w_bias.shape[1],
+             w_side.shape[1] // 2, w_last.shape[1])
+    path = functools.partial(fast, p) if p.ok else general
+    return path(x, pair, w_in, w_out, w_bias, w_side, w_outer, w_tri, w_last)
+
+
 def solution(mesh):
     return jax.shard_map(
         shards,

time: 273 us -> 84.4 us (0.31)
  blocking collectives: 142 us -> 0 us
  local copies, waits for them, and re-layouts: 42.1 us -> 12.7 us
  matrix products: 15 us -> 0 us
  starting transfers between devices: 6.92 us -> 21.8 us
  between operations: 14.4 us -> 0.87 us
  Pallas kernels: 0 us -> 12.8 us
  waiting for transfers between devices: 44.9 us -> 33.8 us
  other arithmetic: 7.22 us -> 1.69 us
    all_gather x7 -> x0, blocking collectives: 142 us -> none  [the longest x1 32.9 us: shards(): lax.all_gather(left_wide, 'row', axis=0, tiled=True)]
    all_gather x1 -> x0, waiting for transfers between devices: 44.9 us -> none  [shards(): right_rows = lax.all_gather(right_edge, 'row', axis=0, tiled=True)]
    all_to_all x2 -> x4, waiting for transfers between devices: 0.01 us -> 33.1 us  [the longest x1 11.1 us: fast(): edges = lax.all_to_all(edges, ALL, 0, 0, tiled=True)]
    dot_general x11 -> x0, matrix products: 15 us -> none  [the longest x1 3.88 us: shards(): jnp.einsum('sic,sjd->ijcd', left_all, right_all, preferred_element_type=j...]
    convert_element_type x4 -> x0, local copies, waits for them, and re-layouts: 14 us -> none  [the longest x1 11.2 us: shards(): averaged = (products * (1.0 / seq_total)).astype(jnp.bfloat16)]
    pallas_call x0 -> x7, Pallas kernels: none -> 12.8 us  [the longest x1 3.82 us: fast(): call(functools.partial(outer_kernel, p), (sds((p.rows, p.cols, width), BF...]
    dot_general x1 -> x0, local copies, waits for them, and re-layouts: 9.08 us -> none  [shards(): jnp.dot(averaged.reshape(-1, outer_width * outer_width), outer_output_wei...]
    all_to_all x2 -> x4, starting transfers between devices: 6.87 us -> 15.3 us  [the longest x1 7.32 us: fast(): bias = lax.all_to_all(piece, ALL, 0, 0, tiled=True)]
  transfers between devices with their start and end apart: 3 -> 10, of which waited for: 1 -> 6; matrix products, arithmetic and copies ran while one was open for 2% -> 9% of each run, Pallas kernels for 0% -> 3%
where the time goes in v1:
time: 84.4 us; the launch traced here: 83.7 us
  waiting for transfers between devices  33.8 us (40%)
  starting transfers between devices  21.8 us (26%)
  Pallas kernels  12.8 us (15%)
  local copies, waits for them, and re-layouts  12.7 us (15%)
  other arithmetic  1.69 us (2%)
  between operations  0.87 us (1%)
    all_to_all x1, waiting for transfers between devices, fast(): edges = lax.all_to_all(edges, ALL, 0, 0, tiled=True)  11.1 us
    all_to_all x1, waiting for transfers between devices, fast(): back = lax.all_to_all(back, ALL, 0, 0, tiled=True)  10 us
    unnamed x21, local copies, waits for them, and re-layouts  9.73 us
    all_to_all x1, starting transfers between devices, fast(): bias = lax.all_to_all(piece, ALL, 0, 0, tiled=True)  7.32 us
    ppermute x6, starting transfers between devices, fast(): lax.ppermute(part, 'col', [(c, (c + shift) % p.n_col) for c in range(p.n_...  6.5 us
    all_to_all x1, waiting for transfers between devices, fast(): sides = lax.all_to_all(sides, ALL, 0, 0, tiled=True)  5.98 us
    all_to_all x1, waiting for transfers between devices, fast(): bias = lax.all_to_all(piece, ALL, 0, 0, tiled=True)  5.9 us
    pallas_call x1, Pallas kernels, fast(): call(functools.partial(outer_kernel, p), (sds((p.rows, p.cols, width), BF...  3.82 us
  transfers between devices with their start and end apart: 10, of which 6 were waited for; matrix products, arithmetic and copies ran while one was open for 9% of the time, Pallas kernels for 3%

profile of v1, /device:TPU:0, one launch (start us, length us, event | category | flops | bytes accessed | tf_op | source)
XLA Modules:
  0.0 83.7 jit_solution(15971845294724706926)
XLA Ops:
  1.4 0.9 %copy-done.1 = bf16[20,40,128]{2,1,0:T(8,128)(2,1)S(1)} copy-done((bf16[20,40,128]{2,1,0:T(8,128)(2,1)S(1)}, bf16[20,40,128]{2,1,0:T(8,128)(2,1)}, u32[]{:S(2)}) %copy-start.1) | copy-done | bytes 204824
  2.4 1.3 %bias.1 = bf16[32,56,128]{2,1,0:T(8,128)(2,1)} custom-call(bf16[800,128]{1,0:T(8,128)(2,1)S(1)} %bitcast.50, bf16[128,8]{1,0:T(8,128)(2,1)S(1)} %copy.21.w_ref), custom_call_target="tpu_custom_call" | custom-call | tf_op jit(solution)/shard_map/bias/pallas_call | solution.py:348
  3.7 7.3 %all-to-all-start = ((bf16[32,56,128]{2,1,0:T(8,128)(2,1)}), bf16[32,56,128]{2,1,0:T(8,128)(2,1)S(1)}, u32[]{:S(2)}, u32[]{:S(2)}) async-start(bf16[32,56,128]{2,1,0:T(8,128)(2,1)} %bias.1), calls=%async_computation | async-start | bytes 917504 | tf_op jit(solution)/shard_map/all_to_all | solution.py:350
  12.2 1.6 %collective-permute-start.1 = (bf16[2,40,256]{2,1,0:T(8,128)(2,1)S(1)}, bf16[2,40,256]{2,1,0:T(8,128)(2,1)S(1)}, u32[]{:S(2)}, u32[]{:S(2)}) collective-permute-start(bf16[2,40,256]{2,1,0:T(8,128)(2,1)S(1)} %get-tuple-element.29), channel_id=1, source_target_pairs={{0,2},{1,3},{2,0},{3,1},{4,6},{5,7},{6,4},{7,5},{8,10},{9,11},{10,... | collective-permute-start | bytes 122888 | tf_op jit(solution)/shard_map/ppermute | solution.py:356
  13.9 1.4 %collective-permute-start.2 = (bf16[2,40,256]{2,1,0:T(8,128)(2,1)S(1)}, bf16[2,40,256]{2,1,0:T(8,128)(2,1)S(1)}, u32[]{:S(2)}, u32[]{:S(2)}) collective-permute-start(bf16[2,40,256]{2,1,0:T(8,128)(2,1)S(1)} %get-tuple-element.28), channel_id=1, source_target_pairs={{0,3},{1,0},{2,1},{3,2},{4,7},{5,4},{6,5},{7,6},{8,11},{9,8},{10,9... | collective-permute-start | bytes 122888 | tf_op jit(solution)/shard_map/ppermute | solution.py:356
  16.2 1.1 %copy.24 = bf16[32,32,128]{2,1,0:T(8,128)(2,1)S(1)} copy(bf16[32,32,128]{2,0,1:T(8,128)(2,1)} %bitcast.56) | data formatting | bytes 524288 | tf_op jit(solution)/shard_map/transpose | solution.py:335
  18.0 1.0 %copy-done.3 = bf16[256,1024]{1,0:T(8,128)(2,1)S(1)} copy-done((bf16[256,1024]{1,0:T(8,128)(2,1)S(1)}, bf16[256,1024]{1,0:T(8,128)(2,1)}, u32[]{:S(2)}) %copy-start.3) | copy-done | bytes 524312
  19.6 5.9 %all-to-all-done.bias_ref = bf16[32,56,128]{2,1,0:T(8,128)(2,1)S(1)} async-done(((bf16[32,56,128]{2,1,0:T(8,128)(2,1)}), bf16[32,56,128]{2,1,0:T(8,128)(2,1)S(1)}, u32[]{:S(2)}, u32[]{:S(2)}) %all-to-all-start) | async-done | bytes 458784 | tf_op jit(solution)/shard_map/all_to_all | solution.py:350
  25.5 1.0 %copy-done.4 = bf16[160,1280]{1,0:T(8,128)(2,1)S(1)} copy-done((bf16[160,1280]{1,0:T(8,128)(2,1)S(1)}, bf16[160,1280]{1,0:T(8,128)(2,1)}, u32[]{:S(2)}) %copy-start.4) | copy-done | bytes 409624
  27.4 3.5 %attend.1 = (bf16[4,2,40,256]{3,2,1,0:T(8,128)(2,1)S(1)}, bf16[32,32,128]{2,1,0:T(8,128)(2,1)}) custom-call(bf16[2,160,256]{2,1,0:T(8,128)(2,1)S(1)} %get-tuple-element.11.q_ref, bf16[2,160,256]{2,1,0:T(8,128)(2,1)S(1)} %get-tuple-element.12.k_ref, bf16[2,160,256]{2,1,0:T(8,128)(2,1)S(1)} %get-tuple-element.13.v_ref, ...), custom_call_target="tpu_custom_call" | custom-call | tf_op jit(solution)/shard_map/attend/pallas_call | solution.py:364
  30.9 2.8 %all-to-all-start.1 = ((bf16[32,32,128]{2,1,0:T(8,128)(2,1)}), bf16[32,32,128]{2,1,0:T(8,128)(2,1)S(1)}, u32[]{:S(2)}, u32[]{:S(2)}) async-start(bf16[32,32,128]{2,1,0:T(8,128)(2,1)} %get-tuple-element.17), calls=%async_computation.1 | async-start | bytes 524288 | tf_op jit(solution)/shard_map/all_to_all | solution.py:373
  33.7 1.6 %broadcast_select_fusion = bf16[32,4,32,4,128]{4,3,2,1,0:T(4,128)(2,1)S(1)} fusion(pred[4,4]{1,0:T(4,128)(4,1)S(1)} %iota_compare_fusion, bf16[32,32,128]{2,1,0:T(8,128)(2,1)S(1)} %copy.24), kind=kLoop, calls=%fused_computation.1 | loop fusion | flops 2097152 | bytes 4456464 | tf_op jit(solution)/shard_map/jit(_where)/select_n | solution.py:337
  35.3 2.7 %copy.29 = bf16[512,8,4,128]{3,1,2,0:T(8,128)(2,1)} copy(bf16[512,8,4,128]{3,2,1,0:T(4,128)(2,1)S(1)} %bitcast.52) | data formatting | bytes 8388608
  38.3 6.0 %all-to-all-done.1.recv_ref = bf16[32,32,128]{2,1,0:T(8,128)(2,1)S(1)} async-done(((bf16[32,32,128]{2,1,0:T(8,128)(2,1)}), bf16[32,32,128]{2,1,0:T(8,128)(2,1)S(1)}, u32[]{:S(2)}, u32[]{:S(2)}) %all-to-all-start.1) | async-done | bytes 262176 | tf_op jit(solution)/shard_map/all_to_all | solution.py:373
  44.2 2.2 %copy-done = bf16[512,8,4,128]{3,1,2,0:T(8,128)(2,1)S(1)} copy-done((bf16[512,8,4,128]{3,1,2,0:T(8,128)(2,1)S(1)}, bf16[512,8,4,128]{3,1,2,0:T(8,128)(2,1)}, u32[]{:S(2)}) %copy-start) | copy-done | bytes 4194328
  46.4 3.8 %outer.1 = (bf16[20,40,128]{2,1,0:T(8,128)(2,1)S(1)}, bf16[32,56,128]{2,1,0:T(8,128)(2,1)}) custom-call(bf16[32,32,128]{2,1,0:T(8,128)(2,1)S(1)} %all-to-all-done.1.recv_ref, bf16[20,40,128]{2,1,0:T(8,128)(2,1)S(1)} %copy-done.2, bf16[4096,512]{1,0:T(8,128)(2,1)S(1)} %bitcast.49, bf16[256,128]{1,0:T(8,128)(2,1)S(1)} %get-tuple-element.34.wv_ref, ...), custom_call_target="tpu_custom_call" | custom-call | tf_op jit(solution)/shard_map/outer/pallas_call | solution.py:374
  50.3 2.6 %all-to-all-start.2 = ((bf16[32,56,128]{2,1,0:T(8,128)(2,1)}), bf16[32,56,128]{2,1,0:T(8,128)(2,1)S(1)}, u32[]{:S(2)}, u32[]{:S(2)}) async-start(bf16[32,56,128]{2,1,0:T(8,128)(2,1)} %get-tuple-element.18), calls=%async_computation.2 | async-start | bytes 917504 | tf_op jit(solution)/shard_map/all_to_all | solution.py:383
  53.1 1.7 %collective-permute-start.4 = (bf16[2,40,256]{2,1,0:T(8,128)(2,1)S(1)}, bf16[2,40,256]{2,1,0:T(8,128)(2,1)S(1)}, u32[]{:S(2)}, u32[]{:S(2)}) collective-permute-start(bf16[2,40,256]{2,1,0:T(8,128)(2,1)S(1)} %get-tuple-element.25), channel_id=1, source_target_pairs={{0,2},{1,3},{2,0},{3,1},{4,6},{5,7},{6,4},{7,5},{8,10},{9,11},{10,... | collective-permute-start | bytes 122888 | tf_op jit(solution)/shard_map/ppermute | solution.py:400
  54.8 1.3 %collective-permute-start.5 = (bf16[2,40,256]{2,1,0:T(8,128)(2,1)S(1)}, bf16[2,40,256]{2,1,0:T(8,128)(2,1)S(1)}, u32[]{:S(2)}, u32[]{:S(2)}) collective-permute-start(bf16[2,40,256]{2,1,0:T(8,128)(2,1)S(1)} %get-tuple-element.24), channel_id=1, source_target_pairs={{0,3},{1,0},{2,1},{3,2},{4,7},{5,4},{6,5},{7,6},{8,11},{9,8},{10,9... | collective-permute-start | bytes 122888 | tf_op jit(solution)/shard_map/ppermute | solution.py:400
  56.2 11.1 %all-to-all-done.2.recv_ref = bf16[32,56,128]{2,1,0:T(8,128)(2,1)S(1)} async-done(((bf16[32,56,128]{2,1,0:T(8,128)(2,1)}), bf16[32,56,128]{2,1,0:T(8,128)(2,1)S(1)}, u32[]{:S(2)}, u32[]{:S(2)}) %all-to-all-start.2) | async-done | bytes 458784 | tf_op jit(solution)/shard_map/all_to_all | solution.py:383
  67.3 1.8 %triangle.1 = bf16[32,32,128]{2,1,0:T(8,128)(2,1)} custom-call(bf16[32,56,128]{2,1,0:T(8,128)(2,1)S(1)} %all-to-all-done.2.recv_ref), custom_call_target="tpu_custom_call" | custom-call | tf_op jit(solution)/shard_map/triangle/pallas_call | solution.py:387
  69.1 2.7 %all-to-all-start.3 = ((bf16[32,32,128]{2,1,0:T(8,128)(2,1)}), bf16[32,32,128]{2,1,0:T(8,128)(2,1)S(1)}, u32[]{:S(2)}, u32[]{:S(2)}) async-start(bf16[32,32,128]{2,1,0:T(8,128)(2,1)} %triangle.1), calls=%async_computation.3 | async-start | bytes 524288 | tf_op jit(solution)/shard_map/all_to_all | solution.py:403
  72.3 10.0 %all-to-all-done.3.recv_ref = bf16[32,32,128]{2,1,0:T(8,128)(2,1)S(1)} async-done(((bf16[32,32,128]{2,1,0:T(8,128)(2,1)}), bf16[32,32,128]{2,1,0:T(8,128)(2,1)S(1)}, u32[]{:S(2)}, u32[]{:S(2)}) %all-to-all-start.3) | async-done | bytes 262176 | tf_op jit(solution)/shard_map/all_to_all | solution.py:403
  82.4 1.3 %final.1 = bf16[20,40,128]{2,1,0:T(8,128)(2,1)} custom-call(bf16[32,32,128]{2,1,0:T(8,128)(2,1)S(1)} %all-to-all-done.3.recv_ref, bf16[20,40,128]{2,1,0:T(8,128)(2,1)S(1)} %get-tuple-element.19.mid_ref, f32[800,128]{1,0:T(8,128)S(1)} %gate.1.gate_ref, bf16[128,128]{1,0:T(8,128)(2,1)S(1)} %bitcast.51), custom_call_target="tpu_custom_call" | custom-call | tf_op jit(solution)/shard_map/final/pallas_call | solution.py:404
  (42 shorter events, 6.0 us)
Async XLA Ops:
  1.4 0.9 %copy-start.1 = (bf16[20,40,128]{2,1,0:T(8,128)(2,1)S(1)}, bf16[20,40,128]{2,1,0:T(8,128)(2,1)}, u32[]{:S(2)}) copy-start(bf16[20,40,128]{2,1,0:T(8,128)(2,1)} %pair_ref.1) | copy-start | bytes 614404
  3.7 21.8 %all-to-all-start = ((bf16[32,56,128]{2,1,0:T(8,128)(2,1)}), bf16[32,56,128]{2,1,0:T(8,128)(2,1)S(1)}, u32[]{:S(2)}, u32[]{:S(2)}) async-start(bf16[32,56,128]{2,1,0:T(8,128)(2,1)} %bias.1), calls=%async_computation | async-start | bytes 917504 | tf_op jit(solution)/shard_map/all_to_all | solution.py:350
  11.9 5.4 %collective-permute-start = (bf16[2,40,256]{2,1,0:T(8,128)(2,1)S(1)}, bf16[2,40,256]{2,1,0:T(8,128)(2,1)S(1)}, u32[]{:S(2)}, u32[]{:S(2)}) collective-permute-start(bf16[2,40,256]{2,1,0:T(8,128)(2,1)S(1)} %get-tuple-element.30), channel_id=1, source_target_pairs={{0,1},{1,2},{2,3},{3,0},{4,5},{5,6},{6,7},{7,4},{8,9},{9,10},{10,1... | collective-permute-start | bytes 122888 | tf_op jit(solution)/shard_map/ppermute | solution.py:356
  12.2 5.2 %collective-permute-start.1 = (bf16[2,40,256]{2,1,0:T(8,128)(2,1)S(1)}, bf16[2,40,256]{2,1,0:T(8,128)(2,1)S(1)}, u32[]{:S(2)}, u32[]{:S(2)}) collective-permute-start(bf16[2,40,256]{2,1,0:T(8,128)(2,1)S(1)} %get-tuple-element.29), channel_id=1, source_target_pairs={{0,2},{1,3},{2,0},{3,1},{4,6},{5,7},{6,4},{7,5},{8,10},{9,11},{10,... | collective-permute-start | bytes 122888 | tf_op jit(solution)/shard_map/ppermute | solution.py:356
  13.9 4.1 %collective-permute-start.2 = (bf16[2,40,256]{2,1,0:T(8,128)(2,1)S(1)}, bf16[2,40,256]{2,1,0:T(8,128)(2,1)S(1)}, u32[]{:S(2)}, u32[]{:S(2)}) collective-permute-start(bf16[2,40,256]{2,1,0:T(8,128)(2,1)S(1)} %get-tuple-element.28), channel_id=1, source_target_pairs={{0,3},{1,0},{2,1},{3,2},{4,7},{5,4},{6,5},{7,6},{8,11},{9,8},{10,9... | collective-permute-start | bytes 122888 | tf_op jit(solution)/shard_map/ppermute | solution.py:356
  18.0 1.0 %copy-start.3 = (bf16[256,1024]{1,0:T(8,128)(2,1)S(1)}, bf16[256,1024]{1,0:T(8,128)(2,1)}, u32[]{:S(2)}) copy-start(bf16[256,1024]{1,0:T(8,128)(2,1)} %refs_4_.1) | copy-start | bytes 1572868
  25.5 1.0 %copy-start.4 = (bf16[160,1280]{1,0:T(8,128)(2,1)S(1)}, bf16[160,1280]{1,0:T(8,128)(2,1)}, u32[]{:S(2)}) copy-start(bf16[160,1280]{1,0:T(8,128)(2,1)} %constant.68.clone.sel_ref) | copy-start | bytes 1228804
  26.5 0.9 %copy-start.5 = (bf16[256,256]{1,0:T(8,128)(2,1)S(1)}, bf16[256,256]{1,0:T(8,128)(2,1)}, u32[]{:S(2)}) copy-start(bf16[256,256]{1,0:T(8,128)(2,1)} %wf_ref.1) | copy-start | bytes 393220
  30.9 13.3 %all-to-all-start.1 = ((bf16[32,32,128]{2,1,0:T(8,128)(2,1)}), bf16[32,32,128]{2,1,0:T(8,128)(2,1)S(1)}, u32[]{:S(2)}, u32[]{:S(2)}) async-start(bf16[32,32,128]{2,1,0:T(8,128)(2,1)} %get-tuple-element.17), calls=%async_computation.1 | async-start | bytes 524288 | tf_op jit(solution)/shard_map/all_to_all | solution.py:373
  35.3 2.7 %copy-start.6 = (bf16[128,640]{1,0:T(8,128)(2,1)S(1)}, bf16[128,640]{1,0:T(8,128)(2,1)}, u32[]{:S(2)}) copy-start(bf16[128,640]{1,0:T(8,128)(2,1)} %param.17) | copy-start | bytes 491524
  35.3 8.9 %copy-start.2 = (bf16[20,40,128]{2,1,0:T(8,128)(2,1)S(1)}, bf16[20,40,128]{2,1,0:T(8,128)(2,1)}, u32[]{:S(2)}) copy-start(bf16[20,40,128]{2,1,0:T(8,128)(2,1)} %pair_ref.1) | copy-start | bytes 614404
  38.0 15.1 %copy-start.8 = (bf16[128,128]{1,0:T(8,128)(2,1)S(1)}, bf16[128,128]{1,0:T(8,128)(2,1)}, u32[]{:S(2)}) copy-start(bf16[128,128]{1,0:T(8,128)(2,1)} %param.18) | copy-start | bytes 98308
  44.2 2.2 %copy-start = (bf16[512,8,4,128]{3,1,2,0:T(8,128)(2,1)S(1)}, bf16[512,8,4,128]{3,1,2,0:T(8,128)(2,1)}, u32[]{:S(2)}) copy-start(bf16[512,8,4,128]{3,1,2,0:T(8,128)(2,1)} %copy.29) | copy-start | bytes 12582916
  50.3 17.0 %all-to-all-start.2 = ((bf16[32,56,128]{2,1,0:T(8,128)(2,1)}), bf16[32,56,128]{2,1,0:T(8,128)(2,1)S(1)}, u32[]{:S(2)}, u32[]{:S(2)}) async-start(bf16[32,56,128]{2,1,0:T(8,128)(2,1)} %get-tuple-element.18), calls=%async_computation.2 | async-start | bytes 917504 | tf_op jit(solution)/shard_map/all_to_all | solution.py:383
  52.9 18.9 %collective-permute-start.3 = (bf16[2,40,256]{2,1,0:T(8,128)(2,1)S(1)}, bf16[2,40,256]{2,1,0:T(8,128)(2,1)S(1)}, u32[]{:S(2)}, u32[]{:S(2)}) collective-permute-start(bf16[2,40,256]{2,1,0:T(8,128)(2,1)S(1)} %get-tuple-element.26), channel_id=1, source_target_pairs={{0,1},{1,2},{2,3},{3,0},{4,5},{5,6},{6,7},{7,4},{8,9},{9,10},{10,1... | collective-permute-start | bytes 122888 | tf_op jit(solution)/shard_map/ppermute | solution.py:400
  53.1 18.7 %collective-permute-start.4 = (bf16[2,40,256]{2,1,0:T(8,128)(2,1)S(1)}, bf16[2,40,256]{2,1,0:T(8,128)(2,1)S(1)}, u32[]{:S(2)}, u32[]{:S(2)}) collective-permute-start(bf16[2,40,256]{2,1,0:T(8,128)(2,1)S(1)} %get-tuple-element.25), channel_id=1, source_target_pairs={{0,2},{1,3},{2,0},{3,1},{4,6},{5,7},{6,4},{7,5},{8,10},{9,11},{10,... | collective-permute-start | bytes 122888 | tf_op jit(solution)/shard_map/ppermute | solution.py:400
  54.8 17.0 %collective-permute-start.5 = (bf16[2,40,256]{2,1,0:T(8,128)(2,1)S(1)}, bf16[2,40,256]{2,1,0:T(8,128)(2,1)S(1)}, u32[]{:S(2)}, u32[]{:S(2)}) collective-permute-start(bf16[2,40,256]{2,1,0:T(8,128)(2,1)S(1)} %get-tuple-element.24), channel_id=1, source_target_pairs={{0,3},{1,0},{2,1},{3,2},{4,7},{5,4},{6,5},{7,6},{8,11},{9,8},{10,9... | collective-permute-start | bytes 122888 | tf_op jit(solution)/shard_map/ppermute | solution.py:400
  69.1 13.2 %all-to-all-start.3 = ((bf16[32,32,128]{2,1,0:T(8,128)(2,1)}), bf16[32,32,128]{2,1,0:T(8,128)(2,1)S(1)}, u32[]{:S(2)}, u32[]{:S(2)}) async-start(bf16[32,32,128]{2,1,0:T(8,128)(2,1)} %triangle.1), calls=%async_computation.3 | async-start | bytes 524288 | tf_op jit(solution)/shard_map/all_to_all | solution.py:403
  71.9 11.8 %copy-start.7 = (bf16[4,2,40,256]{3,2,1,0:T(8,128)(2,1)}, bf16[4,2,40,256]{3,2,1,0:T(8,128)(2,1)S(1)}, u32[]{:S(2)}) copy-start(bf16[4,2,40,256]{3,2,1,0:T(8,128)(2,1)S(1)} %bitcast_dynamic-update-slice_fusion) | copy-start | bytes 491524

commit v2 on v1

--- a/solution.py
+++ b/solution.py
@@ -46,7 +46,8 @@
         out_specs=jax.tree.map(lambda _: VMEM, out_shape),
         scratch_shapes=scratch,
         name=name,
-        compiler_params=pltpu.CompilerParams(vmem_limit_bytes=40 * 1024 * 1024),
+        cost_estimate=pl.CostEstimate(flops=400_000_000, bytes_accessed=4_000_000, transcendentals=0),
+        compiler_params=pltpu.CompilerParams(vmem_limit_bytes=24 * 1024 * 1024),
     )
 
 
@@ -76,7 +77,7 @@
         self.groups = self.cols // SUBLANES
         self.rem_rows = -(-self.groups // self.fold)
         self.bias_rows = self.cols + SUBLANES * self.rem_rows
-        if LANES % outer:
+        if LANES % outer or outer % (LANES // outer):
             return
         self.pack = LANES // outer
         if self.rows % self.pack or self.cols % self.pack:
@@ -111,7 +112,8 @@
     heads = p.heads
     spread = (lax.broadcasted_iota(jnp.int32, (heads, LANES), 1) % heads
               == lax.broadcasted_iota(jnp.int32, (heads, LANES), 0))
-    tiled = dot(w_ref[...], jnp.where(spread, 1.0, 0.0).astype(BF16))
+    tiled = lax.dot_general(w_ref[...], jnp.where(spread, 1.0, 0.0).astype(BF16), (((0,), (0,)), ((), ())),
+                            preferred_element_type=F32)
     slot = lane_iota(p.width) // heads
     main = jnp.zeros((p.cols, LANES), F32)
     rem = jnp.zeros((p.cols, LANES), F32)
@@ -219,7 +221,7 @@
     side_ref[...] = send[...].astype(BF16)
 
 
-def outer_kernel(p, recv_ref, pair_ref, wbd_ref, wv_ref, wg_ref, mid_ref, edge_ref,
+def outer_kernel(p, recv_ref, pair_ref, w_ref, wv_ref, wg_ref, mid_ref, edge_ref,
                  flat, rt, lhs, mid):
     flat[...] = recv_ref[...].reshape(p.n * p.side_rows, LANES).astype(F32)
 
@@ -227,24 +229,31 @@
         return jnp.concatenate(
             [flat[pl.ds(k * p.own + s, p.n, stride=p.side_rows), :] for s in range(p.own)], axis=0)
 
-    left = jnp.concatenate([chunk(p.rk + k) for k in range(p.lk)], axis=1).astype(BF16)
     for k in range(p.rk):
         rt[k * LANES:(k + 1) * LANES, :] = jnp.transpose(chunk(k))
-    right = jnp.concatenate(
-        [rt[pl.ds(d, p.cols, stride=p.outer), :] for d in range(p.outer)], axis=0).astype(BF16)
-    products = dot(right, left) * (1.0 / p.seq_total)
-    for d in range(p.outer):
-        for g in range(p.lk):
-            lhs[g * p.cpad:g * p.cpad + p.cols, d * LANES:(d + 1) * LANES] = products[
-                d * p.cols:(d + 1) * p.cols, g * LANES:(g + 1) * LANES].astype(BF16)
-            if p.cpad > p.cols:
-                lhs[g * p.cpad + p.cols:(g + 1) * p.cpad, d * LANES:(d + 1) * LANES] = jnp.zeros(
-                    (p.cpad - p.cols, LANES), BF16)
-    update = dot(lhs[...], wbd_ref[...])
+    right = []
+    for first in range(0, p.outer, p.pack):
+        right.append(jnp.concatenate(
+            [rt[pl.ds(first + d, p.cols, stride=p.outer), :] for d in range(p.pack)], axis=1))
+    right = jnp.concatenate(right, axis=0).astype(BF16)
+    at = lane_iota(p.seq_total) // p.outer
+    left = []
+    for g in range(p.lk):
+        base = chunk(p.rk + g)
+        turned = [base] + [pltpu.roll(base, t * p.outer, axis=1) for t in range(1, p.pack)]
+        for a in range(p.pack):
+            left.append(jnp.concatenate(
+                [jnp.where(at == d, turned[(d - a) % p.pack], 0.0) for d in range(p.pack)], axis=0).astype(BF16))
+    products = dot(right, jnp.concatenate(left, axis=1)) * (1.0 / p.seq_total)
     for i in range(p.rows):
-        g, a = i // p.pack, i % p.pack
-        fresh = (pair_ref[i].astype(F32)
-                 + update[g * p.cpad:g * p.cpad + p.cols, a * p.width:(a + 1) * p.width]).astype(BF16)
+        for g in range(p.outer // p.pack):
+            lhs[i * p.cpad:i * p.cpad + p.cols, g * LANES:(g + 1) * LANES] = products[
+                g * p.cols:(g + 1) * p.cols, i * LANES:(i + 1) * LANES].astype(BF16)
+        if p.cpad > p.cols:
+            lhs[i * p.cpad + p.cols:(i + 1) * p.cpad, :] = jnp.zeros((p.cpad - p.cols, lhs.shape[1]), BF16)
+    update = dot(lhs[...], w_ref[...])
+    for i in range(p.rows):
+        fresh = (pair_ref[i].astype(F32) + update[i * p.cpad:i * p.cpad + p.cols]).astype(BF16)
         mid_ref[i] = fresh
         mid[i * p.cols:(i + 1) * p.cols, :] = fresh.astype(F32)
     tail = mid.shape[0] - p.rows * p.cols
@@ -332,10 +341,7 @@
 
     left_w, right_w = w_side[:, :p.outer], w_side[:, p.outer:]
     left_w, right_w = jnp.tile(left_w, (1, p.pack)), jnp.tile(right_w, (1, p.pack))
-    by_d = jnp.transpose(w_outer.reshape(p.outer, p.outer, width), (1, 0, 2))
-    eye = jnp.eye(p.pack, dtype=bool)
-    w_bd = jnp.where(eye[None, :, None, :, None], by_d[:, None, :, None, :], jnp.zeros((), BF16)).reshape(
-        p.outer * LANES, p.pack * width)
+    by_d = jnp.transpose(w_outer.reshape(p.outer, p.outer, width), (1, 0, 2)).reshape(w_outer.shape)
     blocks = jnp.transpose(w_tri.reshape(width, 5, width), (1, 2, 0)).reshape(5, n, ch, width)
     value_w = jnp.concatenate([blocks[0], blocks[2]], axis=1).reshape(n * 2 * ch, width)
     gate_w = jnp.concatenate([blocks[1], blocks[3]], axis=1).reshape(n * 2 * ch, width)
@@ -346,7 +352,7 @@
     sel = jnp.asarray((np.arange(p.total)[:, None] == np.repeat(order, p.heads)[None]), BF16)
 
     piece = call(functools.partial(bias_kernel, p), sds((n, p.bias_rows, LANES), BF16), [], [VMEM] * 2, "bias")(
-        pair.reshape(p.rows * p.cols, width), w_bias)
+        pair.reshape(p.rows * p.cols, width), w_bias.T)
     bias = lax.all_to_all(piece, ALL, 0, 0, tiled=True)
     chunks = x.reshape(p.n_col, p.own, p.res, p.feat)
     parts = []
@@ -376,9 +382,9 @@
         (sds((p.rows, p.cols, width), BF16), sds((n, p.edge_rows, LANES), BF16)),
         [pltpu.VMEM((n * p.side_rows, LANES), F32),
          pltpu.VMEM((p.rk * LANES, p.seq_total), F32),
-         pltpu.VMEM((p.lk * p.cpad, p.outer * LANES), BF16),
+         pltpu.VMEM((p.rows * p.cpad, p.outer * p.outer), BF16),
          pltpu.VMEM(((p.ig - 1) * p.q * p.cols + LANES, LANES), F32)],
-        [VMEM] * 5, "outer")(sides, pair, w_bd, value_w, gate_w)
+        [VMEM] * 5, "outer")(sides, pair, by_d, value_w, gate_w)
 
     edges = lax.all_to_all(edges, ALL, 0, 0, tiled=True)
     out_gate = call(functools.partial(gate_kernel, p), sds((p.rows * p.cols, width), F32), [], [VMEM] * 2, "gate")(

time: 84.4 us -> 79.3 us (0.940)
  local copies, waits for them, and re-layouts: 12.7 us -> 3.89 us
  waiting for transfers between devices: 33.8 us -> 40.5 us
  other arithmetic: 1.69 us -> 0.07 us
    unnamed x21 -> x25, local copies, waits for them, and re-layouts: 9.73 us -> 3.43 us
    ppermute x6, waiting for transfers between devices: 0.7 us -> 4.18 us  [fast(): lax.ppermute(part, 'col', [(c, (c + shift) % p.n_col) for c in range(p.n_...]
    all_to_all x1, waiting for transfers between devices: 5.98 us -> 9.36 us  [fast(): sides = lax.all_to_all(sides, ALL, 0, 0, tiled=True)]
    select_n x1 -> x0, other arithmetic: 1.61 us -> none  [fast(): jnp.where(eye[None, :, None, :, None], by_d[:, None, :, None, :], jnp.zer...]
    transpose x1 -> x0, local copies, waits for them, and re-layouts: 1.06 us -> none  [fast(): by_d = jnp.transpose(w_outer.reshape(p.outer, p.outer, width), (1, 0, 2))]
  transfers between devices with their start and end apart: 10 -> 10, of which waited for: 6 -> 6; matrix products, arithmetic and copies ran while one was open for 9% -> 1% of each run, Pallas kernels for 3% -> 4%
where the time goes in v2:
time: 79.3 us; the launch traced here: 78.8 us
  waiting for transfers between devices  40.5 us (51%)
  starting transfers between devices  21.3 us (27%)
  Pallas kernels  12.1 us (15%)
  local copies, waits for them, and re-layouts  3.89 us (5%)
  between operations  0.92 us (1%)
    all_to_all x1, waiting for transfers between devices, fast(): edges = lax.all_to_all(edges, ALL, 0, 0, tiled=True)  11.1 us
    all_to_all x1, waiting for transfers between devices, fast(): back = lax.all_to_all(back, ALL, 0, 0, tiled=True)  9.82 us
    all_to_all x1, waiting for transfers between devices, fast(): sides = lax.all_to_all(sides, ALL, 0, 0, tiled=True)  9.36 us
    all_to_all x1, starting transfers between devices, fast(): bias = lax.all_to_all(piece, ALL, 0, 0, tiled=True)  7.32 us
    all_to_all x1, waiting for transfers between devices, fast(): bias = lax.all_to_all(piece, ALL, 0, 0, tiled=True)  6.05 us
    ppermute x6, starting transfers between devices, fast(): lax.ppermute(part, 'col', [(c, (c + shift) % p.n_col) for c in range(p.n_...  5.93 us
    ppermute x6, waiting for transfers between devices, fast(): lax.ppermute(part, 'col', [(c, (c + shift) % p.n_col) for c in range(p.n_...  4.18 us
    pallas_call x1, Pallas kernels, fast(): call(functools.partial(attend_kernel, p), (sds((p.n_col, p.own, p.res, p....  3.5 us
  transfers between devices with their start and end apart: 10, of which 6 were waited for; matrix products, arithmetic and copies ran while one was open for 1% of the time, Pallas kernels for 4%

profile of v2, /device:TPU:0, one launch (start us, length us, event | category | flops | bytes accessed | tf_op | source)
XLA Modules:
  0.0 78.8 jit_solution(2064935607054436014)
XLA Ops:
  0.6 0.7 copy-done.5
  1.3 0.9 %copy-done.3 = bf16[20,40,128]{2,1,0:T(8,128)(2,1)S(1)} copy-done((bf16[20,40,128]{2,1,0:T(8,128)(2,1)S(1)}, bf16[20,40,128]{2,1,0:T(8,128)(2,1)}, u32[]{:S(2)}) %copy-start.3) | copy-done | bytes 204824
  2.2 1.4 %bias.1 = bf16[32,56,128]{2,1,0:T(8,128)(2,1)} custom-call(bf16[800,128]{1,0:T(8,128)(2,1)S(1)} %bitcast.48, bf16[8,128]{1,0:T(8,128)(2,1)S(1)} %bitcast.49), custom_call_target="tpu_custom_call" | custom-call | flops 400000000 | bytes 4000000 | tf_op jit(solution)/shard_map/bias/pallas_call | solution.py:354
  3.6 7.3 %all-to-all-start = ((bf16[32,56,128]{2,1,0:T(8,128)(2,1)}), bf16[32,56,128]{2,1,0:T(8,128)(2,1)S(1)}, u32[]{:S(2)}, u32[]{:S(2)}) async-start(bf16[32,56,128]{2,1,0:T(8,128)(2,1)} %bias.1), calls=%async_computation | async-start | bytes 917504 | tf_op jit(solution)/shard_map/all_to_all | solution.py:356
  11.3 1.6 %collective-permute-start.1 = (bf16[2,40,256]{2,1,0:T(8,128)(2,1)S(1)}, bf16[2,40,256]{2,1,0:T(8,128)(2,1)S(1)}, u32[]{:S(2)}, u32[]{:S(2)}) collective-permute-start(bf16[2,40,256]{2,1,0:T(8,128)(2,1)S(1)} %get-tuple-element.29), channel_id=1, source_target_pairs={{0,2},{1,3},{2,0},{3,1},{4,6},{5,7},{6,4},{7,5},{8,10},{9,11},{10,... | collective-permute-start | bytes 122888 | tf_op jit(solution)/shard_map/ppermute | solution.py:362
  13.0 1.4 %collective-permute-start.2 = (bf16[2,40,256]{2,1,0:T(8,128)(2,1)S(1)}, bf16[2,40,256]{2,1,0:T(8,128)(2,1)S(1)}, u32[]{:S(2)}, u32[]{:S(2)}) collective-permute-start(bf16[2,40,256]{2,1,0:T(8,128)(2,1)S(1)} %get-tuple-element.28), channel_id=1, source_target_pairs={{0,3},{1,0},{2,1},{3,2},{4,7},{5,4},{6,5},{7,6},{8,11},{9,8},{10,9... | collective-permute-start | bytes 122888 | tf_op jit(solution)/shard_map/ppermute | solution.py:362
  14.6 1.0 %collective-permute-done.refs_1_ = bf16[2,40,256]{2,1,0:T(8,128)(2,1)S(1)} collective-permute-done((bf16[2,40,256]{2,1,0:T(8,128)(2,1)S(1)}, bf16[2,40,256]{2,1,0:T(8,128)(2,1)S(1)}, u32[]{:S(2)}, u32[]{:S(2)}) %collective-permute-start) | collective-permute-done | bytes 40992 | tf_op jit(solution)/shard_map/ppermute | solution.py:362
  15.6 3.1 %collective-permute-done.1.refs_2_ = bf16[2,40,256]{2,1,0:T(8,128)(2,1)S(1)} collective-permute-done((bf16[2,40,256]{2,1,0:T(8,128)(2,1)S(1)}, bf16[2,40,256]{2,1,0:T(8,128)(2,1)S(1)}, u32[]{:S(2)}, u32[]{:S(2)}) %collective-permute-start.1) | collective-permute-done | bytes 40992 | tf_op jit(solution)/shard_map/ppermute | solution.py:362
  18.8 0.5 project.1
  19.3 6.1 %all-to-all-done.bias_ref = bf16[32,56,128]{2,1,0:T(8,128)(2,1)S(1)} async-done(((bf16[32,56,128]{2,1,0:T(8,128)(2,1)}), bf16[32,56,128]{2,1,0:T(8,128)(2,1)S(1)}, u32[]{:S(2)}, u32[]{:S(2)}) %all-to-all-start) | async-done | bytes 458784 | tf_op jit(solution)/shard_map/all_to_all | solution.py:356
  25.4 3.5 %attend.1 = (bf16[4,2,40,256]{3,2,1,0:T(8,128)(2,1)S(1)}, bf16[32,32,128]{2,1,0:T(8,128)(2,1)}) custom-call(bf16[2,160,256]{2,1,0:T(8,128)(2,1)S(1)} %get-tuple-element.11.q_ref, bf16[2,160,256]{2,1,0:T(8,128)(2,1)S(1)} %get-tuple-element.12.k_ref, bf16[2,160,256]{2,1,0:T(8,128)(2,1)S(1)} %get-tuple-element.13.v_ref, ...), custom_call_target="tpu_custom_call" | custom-call | flops 400000000 | bytes 4000000 | tf_op jit(solution)/shard_map/attend/pallas_call | solution.py:370
  28.9 2.8 %all-to-all-start.1 = ((bf16[32,32,128]{2,1,0:T(8,128)(2,1)}), bf16[32,32,128]{2,1,0:T(8,128)(2,1)S(1)}, u32[]{:S(2)}, u32[]{:S(2)}) async-start(bf16[32,32,128]{2,1,0:T(8,128)(2,1)} %get-tuple-element.17), calls=%async_computation.1 | async-start | bytes 524288 | tf_op jit(solution)/shard_map/all_to_all | solution.py:379
  31.8 0.8 %copy-done.7 = bf16[128,640]{1,0:T(8,128)(2,1)S(1)} copy-done((bf16[128,640]{1,0:T(8,128)(2,1)S(1)}, bf16[128,640]{1,0:T(8,128)(2,1)}, u32[]{:S(2)}) %copy-start.7) | copy-done | bytes 163864
  32.9 9.4 %all-to-all-done.1.recv_ref = bf16[32,32,128]{2,1,0:T(8,128)(2,1)S(1)} async-done(((bf16[32,32,128]{2,1,0:T(8,128)(2,1)}), bf16[32,32,128]{2,1,0:T(8,128)(2,1)S(1)}, u32[]{:S(2)}, u32[]{:S(2)}) %all-to-all-start.1) | async-done | bytes 262176 | tf_op jit(solution)/shard_map/all_to_all | solution.py:379
  42.2 3.2 %outer.1 = (bf16[20,40,128]{2,1,0:T(8,128)(2,1)S(1)}, bf16[32,56,128]{2,1,0:T(8,128)(2,1)}) custom-call(bf16[32,32,128]{2,1,0:T(8,128)(2,1)S(1)} %all-to-all-done.1.recv_ref, bf16[20,40,128]{2,1,0:T(8,128)(2,1)S(1)} %copy-done.4, bf16[1024,128]{1,0:T(8,128)(2,1)S(1)} %bitcast.46, bf16[256,128]{1,0:T(8,128)(2,1)S(1)} %get-tuple-element.34.wv_ref, ...), custom_call_target="tpu_custom_call" | custom-call | flops 400000000 | bytes 4000000 | tf_op jit(solution)/shard_map/outer/pallas_call | solution.py:380
  45.4 2.6 %all-to-all-start.2 = ((bf16[32,56,128]{2,1,0:T(8,128)(2,1)}), bf16[32,56,128]{2,1,0:T(8,128)(2,1)S(1)}, u32[]{:S(2)}, u32[]{:S(2)}) async-start(bf16[32,56,128]{2,1,0:T(8,128)(2,1)} %get-tuple-element.18), calls=%async_computation.2 | async-start | bytes 917504 | tf_op jit(solution)/shard_map/all_to_all | solution.py:389
  48.3 0.6 copy-done.11
  48.8 1.6 %collective-permute-start.4 = (bf16[2,40,256]{2,1,0:T(8,128)(2,1)S(1)}, bf16[2,40,256]{2,1,0:T(8,128)(2,1)S(1)}, u32[]{:S(2)}, u32[]{:S(2)}) collective-permute-start(bf16[2,40,256]{2,1,0:T(8,128)(2,1)S(1)} %get-tuple-element.25), channel_id=1, source_target_pairs={{0,2},{1,3},{2,0},{3,1},{4,6},{5,7},{6,4},{7,5},{8,10},{9,11},{10,... | collective-permute-start | bytes 122888 | tf_op jit(solution)/shard_map/ppermute | solution.py:406
  50.5 0.8 %collective-permute-start.5 = (bf16[2,40,256]{2,1,0:T(8,128)(2,1)S(1)}, bf16[2,40,256]{2,1,0:T(8,128)(2,1)S(1)}, u32[]{:S(2)}, u32[]{:S(2)}) collective-permute-start(bf16[2,40,256]{2,1,0:T(8,128)(2,1)S(1)} %get-tuple-element.24), channel_id=1, source_target_pairs={{0,3},{1,0},{2,1},{3,2},{4,7},{5,4},{6,5},{7,6},{8,11},{9,8},{10,9... | collective-permute-start | bytes 122888 | tf_op jit(solution)/shard_map/ppermute | solution.py:406
  51.3 11.1 %all-to-all-done.2.recv_ref = bf16[32,56,128]{2,1,0:T(8,128)(2,1)S(1)} async-done(((bf16[32,56,128]{2,1,0:T(8,128)(2,1)}), bf16[32,56,128]{2,1,0:T(8,128)(2,1)S(1)}, u32[]{:S(2)}, u32[]{:S(2)}) %all-to-all-start.2) | async-done | bytes 458784 | tf_op jit(solution)/shard_map/all_to_all | solution.py:389
  62.4 1.8 %triangle.1 = bf16[32,32,128]{2,1,0:T(8,128)(2,1)} custom-call(bf16[32,56,128]{2,1,0:T(8,128)(2,1)S(1)} %all-to-all-done.2.recv_ref), custom_call_target="tpu_custom_call" | custom-call | flops 400000000 | bytes 4000000 | tf_op jit(solution)/shard_map/triangle/pallas_call | solution.py:393
  64.2 2.7 %all-to-all-start.3 = ((bf16[32,32,128]{2,1,0:T(8,128)(2,1)}), bf16[32,32,128]{2,1,0:T(8,128)(2,1)S(1)}, u32[]{:S(2)}, u32[]{:S(2)}) async-start(bf16[32,32,128]{2,1,0:T(8,128)(2,1)} %triangle.1), calls=%async_computation.3 | async-start | bytes 524288 | tf_op jit(solution)/shard_map/all_to_all | solution.py:409
  67.7 9.8 %all-to-all-done.3.recv_ref = bf16[32,32,128]{2,1,0:T(8,128)(2,1)S(1)} async-done(((bf16[32,32,128]{2,1,0:T(8,128)(2,1)}), bf16[32,32,128]{2,1,0:T(8,128)(2,1)S(1)}, u32[]{:S(2)}, u32[]{:S(2)}) %all-to-all-start.3) | async-done | bytes 262176 | tf_op jit(solution)/shard_map/all_to_all | solution.py:409
  77.5 1.3 %final.1 = bf16[20,40,128]{2,1,0:T(8,128)(2,1)} custom-call(bf16[32,32,128]{2,1,0:T(8,128)(2,1)S(1)} %all-to-all-done.3.recv_ref, bf16[20,40,128]{2,1,0:T(8,128)(2,1)S(1)} %get-tuple-element.19.mid_ref, f32[800,128]{1,0:T(8,128)S(1)} %gate.1.gate_ref, bf16[128,128]{1,0:T(8,128)(2,1)S(1)} %bitcast.47), custom_call_target="tpu_custom_call" | custom-call | flops 400000000 | bytes 4000000 | tf_op jit(solution)/shard_map/final/pallas_call | solution.py:410
  (44 shorter events, 1.9 us)
Async XLA Ops:
  0.6 0.7 copy-start.5
  1.3 0.9 %copy-start.3 = (bf16[20,40,128]{2,1,0:T(8,128)(2,1)S(1)}, bf16[20,40,128]{2,1,0:T(8,128)(2,1)}, u32[]{:S(2)}) copy-start(bf16[20,40,128]{2,1,0:T(8,128)(2,1)} %pair_ref.1) | copy-start | bytes 614404
  3.6 7.4 %copy-start.8 = (bf16[8,40,256]{2,1,0:T(8,128)(2,1)S(1)}, bf16[8,40,256]{2,1,0:T(8,128)(2,1)}, u32[]{:S(2)}) copy-start(bf16[8,40,256]{2,1,0:T(8,128)(2,1)} %param.10) | copy-start | bytes 491524
  3.6 10.7 %copy-start.10 = (bf16[256,64]{0,1:T(8,128)(2,1)S(1)}, bf16[256,64]{0,1:T(8,128)(2,1)}, u32[]{:S(2)}) copy-start(bf16[256,64]{0,1:T(8,128)(2,1)} %param.15) | copy-start | bytes 98308
  3.6 21.8 %all-to-all-start = ((bf16[32,56,128]{2,1,0:T(8,128)(2,1)}), bf16[32,56,128]{2,1,0:T(8,128)(2,1)S(1)}, u32[]{:S(2)}, u32[]{:S(2)}) async-start(bf16[32,56,128]{2,1,0:T(8,128)(2,1)} %bias.1), calls=%async_computation | async-start | bytes 917504 | tf_op jit(solution)/shard_map/all_to_all | solution.py:356
  11.0 7.8 %copy-start.2 = (bf16[256,1024]{1,0:T(8,128)(2,1)S(1)}, bf16[256,1024]{1,0:T(8,128)(2,1)}, u32[]{:S(2)}) copy-start(bf16[256,1024]{1,0:T(8,128)(2,1)} %refs_4_.1) | copy-start | bytes 1572868
  11.0 4.6 %collective-permute-start = (bf16[2,40,256]{2,1,0:T(8,128)(2,1)S(1)}, bf16[2,40,256]{2,1,0:T(8,128)(2,1)S(1)}, u32[]{:S(2)}, u32[]{:S(2)}) collective-permute-start(bf16[2,40,256]{2,1,0:T(8,128)(2,1)S(1)} %get-tuple-element.30), channel_id=1, source_target_pairs={{0,1},{1,2},{2,3},{3,0},{4,5},{5,6},{6,7},{7,4},{8,9},{9,10},{10,1... | collective-permute-start | bytes 122888 | tf_op jit(solution)/shard_map/ppermute | solution.py:362
  11.3 7.4 %collective-permute-start.1 = (bf16[2,40,256]{2,1,0:T(8,128)(2,1)S(1)}, bf16[2,40,256]{2,1,0:T(8,128)(2,1)S(1)}, u32[]{:S(2)}, u32[]{:S(2)}) collective-permute-start(bf16[2,40,256]{2,1,0:T(8,128)(2,1)S(1)} %get-tuple-element.29), channel_id=1, source_target_pairs={{0,2},{1,3},{2,0},{3,1},{4,6},{5,7},{6,4},{7,5},{8,10},{9,11},{10,... | collective-permute-start | bytes 122888 | tf_op jit(solution)/shard_map/ppermute | solution.py:362
  13.0 5.8 %collective-permute-start.2 = (bf16[2,40,256]{2,1,0:T(8,128)(2,1)S(1)}, bf16[2,40,256]{2,1,0:T(8,128)(2,1)S(1)}, u32[]{:S(2)}, u32[]{:S(2)}) collective-permute-start(bf16[2,40,256]{2,1,0:T(8,128)(2,1)S(1)} %get-tuple-element.28), channel_id=1, source_target_pairs={{0,3},{1,0},{2,1},{3,2},{4,7},{5,4},{6,5},{7,6},{8,11},{9,8},{10,9... | collective-permute-start | bytes 122888 | tf_op jit(solution)/shard_map/ppermute | solution.py:362
  18.8 6.6 %copy-start = (bf16[160,1280]{1,0:T(8,128)(2,1)S(1)}, bf16[160,1280]{1,0:T(8,128)(2,1)}, u32[]{:S(2)}) copy-start(bf16[160,1280]{1,0:T(8,128)(2,1)} %constant.67.clone.sel_ref) | copy-start | bytes 1228804
  18.8 6.6 %copy-start.1 = (bf16[256,256]{1,0:T(8,128)(2,1)S(1)}, bf16[256,256]{1,0:T(8,128)(2,1)}, u32[]{:S(2)}) copy-start(bf16[256,256]{1,0:T(8,128)(2,1)} %wf_ref.1) | copy-start | bytes 393220
  28.9 2.8 %copy-start.6 = (bf16[1024,128]{1,0:T(8,128)(2,1)S(1)}, bf16[1024,128]{1,0:T(8,128)(2,1)}, u32[]{:S(2)}) copy-start(bf16[1024,128]{1,0:T(8,128)(2,1)} %param.16) | copy-start | bytes 786436
  28.9 13.3 %all-to-all-start.1 = ((bf16[32,32,128]{2,1,0:T(8,128)(2,1)}), bf16[32,32,128]{2,1,0:T(8,128)(2,1)S(1)}, u32[]{:S(2)}, u32[]{:S(2)}) async-start(bf16[32,32,128]{2,1,0:T(8,128)(2,1)} %get-tuple-element.17), calls=%async_computation.1 | async-start | bytes 524288 | tf_op jit(solution)/shard_map/all_to_all | solution.py:379
  31.7 0.9 %copy-start.7 = (bf16[128,640]{1,0:T(8,128)(2,1)S(1)}, bf16[128,640]{1,0:T(8,128)(2,1)}, u32[]{:S(2)}) copy-start(bf16[128,640]{1,0:T(8,128)(2,1)} %param.17) | copy-start | bytes 491524
  32.8 9.5 %copy-start.4 = (bf16[20,40,128]{2,1,0:T(8,128)(2,1)S(1)}, bf16[20,40,128]{2,1,0:T(8,128)(2,1)}, u32[]{:S(2)}) copy-start(bf16[20,40,128]{2,1,0:T(8,128)(2,1)} %pair_ref.1) | copy-start | bytes 614404
  45.4 17.0 %all-to-all-start.2 = ((bf16[32,56,128]{2,1,0:T(8,128)(2,1)}), bf16[32,56,128]{2,1,0:T(8,128)(2,1)S(1)}, u32[]{:S(2)}, u32[]{:S(2)}) async-start(bf16[32,56,128]{2,1,0:T(8,128)(2,1)} %get-tuple-element.18), calls=%async_computation.2 | async-start | bytes 917504 | tf_op jit(solution)/shard_map/all_to_all | solution.py:389
  48.1 0.8 copy-start.11
  48.1 18.8 %collective-permute-start.3 = (bf16[2,40,256]{2,1,0:T(8,128)(2,1)S(1)}, bf16[2,40,256]{2,1,0:T(8,128)(2,1)S(1)}, u32[]{:S(2)}, u32[]{:S(2)}) collective-permute-start(bf16[2,40,256]{2,1,0:T(8,128)(2,1)S(1)} %get-tuple-element.26), channel_id=1, source_target_pairs={{0,1},{1,2},{2,3},{3,0},{4,5},{5,6},{6,7},{7,4},{8,9},{9,10},{10,1... | collective-permute-start | bytes 122888 | tf_op jit(solution)/shard_map/ppermute | solution.py:406
  48.8 18.1 %collective-permute-start.4 = (bf16[2,40,256]{2,1,0:T(8,128)(2,1)S(1)}, bf16[2,40,256]{2,1,0:T(8,128)(2,1)S(1)}, u32[]{:S(2)}, u32[]{:S(2)}) collective-permute-start(bf16[2,40,256]{2,1,0:T(8,128)(2,1)S(1)} %get-tuple-element.25), channel_id=1, source_target_pairs={{0,2},{1,3},{2,0},{3,1},{4,6},{5,7},{6,4},{7,5},{8,10},{9,11},{10,... | collective-permute-start | bytes 122888 | tf_op jit(solution)/shard_map/ppermute | solution.py:406
  50.5 16.5 %collective-permute-start.5 = (bf16[2,40,256]{2,1,0:T(8,128)(2,1)S(1)}, bf16[2,40,256]{2,1,0:T(8,128)(2,1)S(1)}, u32[]{:S(2)}, u32[]{:S(2)}) collective-permute-start(bf16[2,40,256]{2,1,0:T(8,128)(2,1)S(1)} %get-tuple-element.24), channel_id=1, source_target_pairs={{0,3},{1,0},{2,1},{3,2},{4,7},{5,4},{6,5},{7,6},{8,11},{9,8},{10,9... | collective-permute-start | bytes 122888 | tf_op jit(solution)/shard_map/ppermute | solution.py:406
  64.2 13.2 %all-to-all-start.3 = ((bf16[32,32,128]{2,1,0:T(8,128)(2,1)}), bf16[32,32,128]{2,1,0:T(8,128)(2,1)S(1)}, u32[]{:S(2)}, u32[]{:S(2)}) async-start(bf16[32,32,128]{2,1,0:T(8,128)(2,1)} %triangle.1), calls=%async_computation.3 | async-start | bytes 524288 | tf_op jit(solution)/shard_map/all_to_all | solution.py:409
  67.0 0.7 copy-start.9

commit v3 on v2

--- a/solution.py
+++ b/solution.py
@@ -2,7 +2,6 @@
 
 import jax
 import jax.numpy as jnp
-import numpy as np
 from jax import lax
 from jax.experimental import pallas as pl
 from jax.experimental.pallas import tpu as pltpu
@@ -34,8 +33,20 @@
     return lax.dot_general(a, b, NT, preferred_element_type=F32)
 
 
-def lane_iota(rows):
-    return lax.broadcasted_iota(jnp.int32, (rows, LANES), 1)
+def lane_iota(rows, width=LANES):
+    return lax.broadcasted_iota(jnp.int32, (rows, width), 1)
+
+
+def row_iota(rows, width=LANES):
+    return lax.broadcasted_iota(jnp.int32, (rows, width), 0)
+
+
+def over(index, size):
+    return lax.shift_right_logical(index, jnp.int32(size.bit_length() - 1))
+
+
+def modulo(index, size):
+    return lax.bitwise_and(index, jnp.int32(size - 1))
 
 
 def call(body, out_shape, scratch, in_specs, name):
@@ -60,43 +71,64 @@
         self.hd = self.feat // heads
         self.total = self.res * n_col
         self.ok = False
+        if any(size & (size - 1) for size in (heads, outer, self.hd, n_row, n_col)):
+            return
         if self.seqs % n_col or self.width != LANES or heads != SUBLANES or self.cols != self.res:
             return
         if self.rows * n_row != self.total or self.feat % LANES:
             return
-        self.own = self.seqs // n_col
-        self.seq_total = self.own * self.n
-        self.i_main = LANES // heads
-        self.i_rem = self.rows - self.i_main
-        if not 0 < self.i_rem or LANES % (self.i_rem * heads) or self.cols % SUBLANES:
-            return
-        self.rem = self.i_rem * heads
-        self.fold = LANES // self.rem
-        if n_row % self.fold:
-            return
-        self.groups = self.cols // SUBLANES
-        self.rem_rows = -(-self.groups // self.fold)
-        self.bias_rows = self.cols + SUBLANES * self.rem_rows
+        self.split = 2
+        if n_col % self.split:
+            return
+        self.n_group = n_col // self.split
+        self.own = self.seqs // self.n_group
+        self.seq_total = self.own * self.n_group * n_row
         if LANES % outer or outer % (LANES // outer):
             return
         self.pack = LANES // outer
         if self.rows % self.pack or self.cols % self.pack:
             return
+        self.half = -(-self.rows // (self.split * self.pack)) * self.pack
+        self.late = self.rows - self.half
+        self.queries = n_row * self.half
+        self.i_main = LANES // heads // 2
+        self.i_rem = self.half - self.i_main
+        if not 0 < self.i_rem or self.i_main % self.pack or self.i_rem % self.pack or LANES % (self.i_rem * heads) or self.cols % SUBLANES:
+            return
+        self.km = self.i_main // self.pack
+        self.main, self.rem = self.i_main * heads, self.i_rem * heads
+        self.groups = self.cols // SUBLANES
+        self.tall = -(-self.groups // 2)
+        self.fold = LANES // self.rem
+        if n_row % 2 or n_row % self.fold:
+            return
+        self.main_at = [(g % self.tall, g // self.tall * self.main) for g in range(self.groups)]
+        spare = [(self.tall, f * self.rem) for f in range(self.fold)]
+        if self.groups % 2:
+            spare += [(self.tall - 1, self.main + f * self.rem) for f in range(self.main // self.rem)]
+        if len(spare) < self.groups:
+            return
+        self.rem_at = spare[:self.groups]
+        self.bias_rows = (self.tall + 1) * SUBLANES
+        self.per = n_row // n_col
+        if n_row % n_col or self.per * self.rows != self.cols:
+            return
         self.lk, self.rk = self.rows // self.pack, self.cols // self.pack
-        used = (self.lk + self.rk) * self.own
-        self.side_rows = -(-used // 16) * 16
+        self.hk = self.half // self.pack
+        self.ek = self.lk - self.hk
+        chunks = max(self.ek + self.per * self.hk, self.hk + self.per * self.ek)
+        self.side_rows = -(-chunks * self.own // 16) * 16
         self.cpad = -(-self.cols // 16) * 16
         if self.width % self.n:
             return
         self.ch = self.width // self.n
-        if 2 * self.ch != SUBLANES or n_row % n_col:
+        if 2 * self.ch != SUBLANES:
             return
         self.q = LANES // self.cols
         self.ig = -(-self.rows // self.q)
         self.ipad = self.ig * self.q
-        self.per = n_row // n_col
         self.jslot = self.per * self.ipad
-        if self.per * self.rows != self.cols or self.q * self.jslot > LANES:
+        if self.q * self.jslot > LANES:
             return
         self.m = n_row * self.ig
         self.edge_rows = self.ig * SUBLANES
@@ -110,87 +142,89 @@
 def bias_kernel(p, pair_ref, w_ref, out_ref):
     normed = standardize_features(pair_ref[...])
     heads = p.heads
-    spread = (lax.broadcasted_iota(jnp.int32, (heads, LANES), 1) % heads
-              == lax.broadcasted_iota(jnp.int32, (heads, LANES), 0))
+    spread = modulo(lane_iota(heads), heads) == row_iota(heads)
     tiled = lax.dot_general(w_ref[...], jnp.where(spread, 1.0, 0.0).astype(BF16), (((0,), (0,)), ((), ())),
                             preferred_element_type=F32)
-    slot = lane_iota(p.width) // heads
-    main = jnp.zeros((p.cols, LANES), F32)
-    rem = jnp.zeros((p.cols, LANES), F32)
-    for i in range(p.rows):
-        block = normed[i * p.cols:(i + 1) * p.cols].astype(BF16)
-        if i < p.i_main:
-            main += dot(block, jnp.where(slot == i, tiled, 0.0).astype(BF16))
-        else:
-            rem += dot(block, jnp.where(slot % p.i_rem == i - p.i_main, tiled, 0.0).astype(BF16))
-    piece = [main]
-    at = lane_iota(SUBLANES) // p.rem
-    for k in range(p.rem_rows):
-        folded = jnp.zeros((SUBLANES, LANES), F32)
-        for f in range(p.fold):
-            g = k * p.fold + f
-            if g < p.groups:
-                folded = jnp.where(at == f, rem[g * SUBLANES:(g + 1) * SUBLANES], folded)
-        piece.append(folded)
-    piece = jnp.concatenate(piece, axis=0).astype(BF16)
+    slot = over(lane_iota(p.width), heads)
+    main_slot, rem_slot = modulo(slot, p.i_main), modulo(slot, p.i_rem)
+    at = lane_iota(SUBLANES)
+    pieces = []
+    for h in range(p.split):
+        main = jnp.zeros((p.cols, LANES), F32)
+        rem = jnp.zeros((p.cols, LANES), F32)
+        for m in range(p.half):
+            i = h * p.late + m
+            block = normed[i * p.cols:(i + 1) * p.cols].astype(BF16)
+            if m < p.i_main:
+                main += dot(block, jnp.where(main_slot == m, tiled, 0.0).astype(BF16))
+            else:
+                rem += dot(block, jnp.where(rem_slot == m - p.i_main, tiled, 0.0).astype(BF16))
+        blocks = [jnp.zeros((SUBLANES, LANES), F32) for _ in range(p.tall + 1)]
+        for value, places, wide in ((main, p.main_at, p.main), (rem, p.rem_at, p.rem)):
+            for g, (b, lane) in enumerate(places):
+                here = (at >= lane) & (at < lane + wide)
+                blocks[b] = jnp.where(here, value[g * SUBLANES:(g + 1) * SUBLANES], blocks[b])
+        pieces.append(jnp.concatenate(blocks, axis=0).astype(BF16))
     for d in range(p.n):
-        out_ref[d] = piece
+        out_ref[d] = pieces[d % p.n_col % p.split]
+
+
+def pick_half(p, second, rows):
+    main, rest = [], []
+    for r in range(p.n_row):
+        a, b = r * p.rows, r * p.rows + p.late
+        main.append(jnp.where(second, rows[b:b + p.i_main], rows[a:a + p.i_main]))
+        rest.append(jnp.where(second, rows[b + p.i_main:b + p.half], rows[a + p.i_main:a + p.half]))
+    return jnp.concatenate(main + rest, axis=0)
 
 
 def project_kernel(p, col_ref, *refs):
     x_refs = refs[:p.n_col]
     w_ref, q_ref, k_ref, v_ref, gate_ref, x_out, hold = refs[p.n_col:]
     me = col_ref[0]
+    second = lax.rem(me, p.split) == 1
     for shift in range(p.n_col):
         hold[lax.rem(me + (p.n_col - shift), p.n_col)] = x_refs[shift][...].astype(F32)
     f = p.feat
     for s in range(p.own):
         x = jnp.concatenate([hold[c, s] for c in range(p.n_col)], axis=0)
-        x_out[s] = x
-        lines = dot(standardize_features(x).astype(BF16), w_ref[...])
-        q_ref[s] = (lines[:, :f] * p.hd ** (-0.5)).astype(BF16)
-        k_ref[s] = lines[:, f:2 * f].astype(BF16)
-        v_ref[s] = lines[:, 2 * f:3 * f].astype(BF16)
-        gate_ref[s] = jax.nn.sigmoid(lines[:, 3 * f:])
-
-
-def attend_kernel(p, q_ref, k_ref, v_ref, gate_ref, x_ref, bias_ref, sel_ref, wf_ref, wl_ref, wr_ref,
-                  emb_ref, side_ref, bias, l4, r4, lint, rint, send):
-    h, t, f = p.heads, p.total, p.feat
-    main = p.n_row * LANES
-    for r in range(p.n_row):
+        normed = standardize_features(x)
+        x_out[s] = pick_half(p, second, x).astype(BF16)
+        lines = dot(normed.astype(BF16), w_ref[:, f:3 * f])
+        k_ref[s] = lines[:, :f].astype(BF16)
+        v_ref[s] = lines[:, f:].astype(BF16)
+        normed = pick_half(p, second, normed).astype(BF16)
+        gate_ref[s] = jax.nn.sigmoid(dot(normed, w_ref[:, 3 * f:]))
+        q_ref[s] = (dot(normed, w_ref[:, :f]) * p.hd ** (-0.5)).astype(BF16)
+
+
+def attend_kernel(p, col_ref, q_ref, k_ref, v_ref, gate_ref, x_ref, bias_ref, wf_ref, ws_ref,
+                  emb_ref, side_ref, bias, four, lint, rint, send):
+    h, t, f, m = p.heads, p.queries, p.feat, p.half
+    at = lane_iota(SUBLANES)
+    for first, places, wide in ((0, p.main_at, p.main), (p.n_row * p.main, p.rem_at, p.rem)):
+        fold = LANES // wide
+        slot = over(at, wide)
         for c in range(p.n_col):
-            bias[c * p.cols:(c + 1) * p.cols, r * LANES:(r + 1) * LANES] = (
-                bias_ref[r * p.n_col + c, 0:p.cols].astype(F32))
-    at = lane_iota(SUBLANES) // p.rem
-    for c in range(p.n_col):
-        for b in range(p.n_row // p.fold):
-            tails = [bias_ref[(b * p.fold + u) * p.n_col + c, p.cols:p.bias_rows].astype(F32)
-                     for u in range(p.fold)]
-            for g in range(p.groups):
-                k, part = g // p.fold, g % p.fold
-                block = jnp.zeros((SUBLANES, LANES), F32)
-                for u in range(p.fold):
-                    piece = tails[u][k * SUBLANES:(k + 1) * SUBLANES]
-                    turn = ((u - part) * p.rem) % LANES
-                    if turn:
-                        piece = pltpu.roll(piece, turn, axis=1)
-                    block = jnp.where(at == u, piece, block)
-                bias[c * p.cols + g * SUBLANES:c * p.cols + (g + 1) * SUBLANES,
-                     main + b * LANES:main + (b + 1) * LANES] = block
-    head_of = (lax.broadcasted_iota(jnp.int32, (h, f), 1) // p.hd
-               == lax.broadcasted_iota(jnp.int32, (h, f), 0))
-    head_mask = jnp.where(head_of, 1.0, 0.0)
+            for b in range(p.n_row // fold):
+                for g, (block, lane) in enumerate(places):
+                    built = None
+                    for u in range(fold):
+                        piece = bias_ref[(b * fold + u) * p.n_col + c,
+                                         block * SUBLANES:(block + 1) * SUBLANES].astype(F32)
+                        turn = (u * wide - lane) % LANES
+                        piece = pltpu.roll(piece, turn, axis=1) if turn else piece
+                        built = piece if u == 0 else jnp.where(slot == u, piece, built)
+                    row = c * p.cols + g * SUBLANES
+                    bias[row:row + SUBLANES, first + b * LANES:first + (b + 1) * LANES] = built
     wide = t * h
-    own_head = (lax.broadcasted_iota(jnp.int32, (f, wide), 0) // p.hd
-                == lax.broadcasted_iota(jnp.int32, (f, wide), 1) % h)
-    lane = lane_iota(t // p.pack) // p.outer
+    own_head = over(row_iota(f, wide), p.hd) == modulo(lane_iota(f, wide), h)
+    pick = jnp.where(over(lane_iota(t, wide), h) == row_iota(t, wide), 1.0, 0.0).astype(BF16)
+    head_mask = jnp.where(over(lane_iota(h, f), p.hd) == row_iota(h, f), 1.0, 0.0)
+    new = []
     for s in range(p.own):
         q = q_ref[s].astype(F32)
-        spread = jnp.broadcast_to(q[:, None, :], (t, h, f)) * head_mask[None]
-        parts = [spread[r * p.rows:r * p.rows + p.i_main] for r in range(p.n_row)]
-        parts += [spread[r * p.rows + p.i_main:(r + 1) * p.rows] for r in range(p.n_row)]
-        spread = jnp.concatenate(parts, axis=0).reshape(wide, f).astype(BF16)
+        spread = (jnp.broadcast_to(q[:, None, :], (t, h, f)) * head_mask[None]).reshape(wide, f).astype(BF16)
         scores = dot_nt(k_ref[s], spread) + bias[...]
         peak = jnp.max(scores, axis=0, keepdims=True)
         weights = jnp.exp(scores - peak)
@@ -198,48 +232,98 @@
         v_t = jnp.transpose(v_ref[s].astype(F32)).astype(BF16)
         mixed = dot(v_t, weights.astype(BF16)) * (1.0 / total)
         mixed = jnp.where(own_head, mixed, 0.0).astype(BF16)
-        attended = dot_nt(sel_ref[...], mixed)
-        gated = (gate_ref[s] * attended).astype(BF16)
-        new = (x_ref[s] + dot(gated, wf_ref[...])).astype(BF16).astype(F32)
+        new.append((gate_ref[s] * dot_nt(pick, mixed)).astype(BF16))
+    new = dot(jnp.concatenate(new, axis=0), wf_ref[...])
+    new = (x_ref[...].astype(F32).reshape(p.own * t, f) + new).astype(BF16).astype(F32)
+    a, b = p.per * p.i_main, p.per * p.i_rem
+    for s in range(p.own):
         for c in range(p.n_col):
-            emb_ref[c, s] = new[c * p.res:(c + 1) * p.res].astype(BF16)
-        normed = standardize_features(new).astype(BF16)
-        for w_ref, four, woven in ((wl_ref, l4, lint), (wr_ref, r4, rint)):
-            four[...] = dot(normed, w_ref[...])
-            packed = four[pl.ds(0, t // p.pack, stride=p.pack), :]
+            row, tail = s * t + c * a, s * t + p.n_row * p.i_main + c * b
+            emb_ref[c, s] = jnp.concatenate([new[row:row + a], new[tail:tail + b]], axis=0).astype(BF16)
+    sides = dot(standardize_features(new).astype(BF16), ws_ref[...])
+    four[0] = sides[:, :LANES]
+    four[1] = sides[:, LANES:]
+    n4 = t // p.pack
+    lane = over(lane_iota(n4), p.outer)
+    for s in range(p.own):
+        for side, woven in enumerate((lint, rint)):
+            packed = four[side, pl.ds(s * t, n4, stride=p.pack), :]
             for a in range(1, p.pack):
-                packed = jnp.where(lane == a, four[pl.ds(a, t // p.pack, stride=p.pack), :], packed)
-            woven[pl.ds(s, t // p.pack, stride=p.own), :] = packed
-    nr, nl = p.rk * p.own, p.lk * p.own
-    for r in range(p.n_row):
-        for c in range(p.n_col):
-            d = r * p.n_col + c
-            send[d, 0:nr] = rint[c * nr:(c + 1) * nr]
-            send[d, nr:nr + nl] = lint[r * nl:(r + 1) * nl]
-            if nr + nl < p.side_rows:
-                send[d, nr + nl:p.side_rows] = jnp.zeros((p.side_rows - nr - nl, LANES), F32)
+                packed = jnp.where(lane == a, four[side, pl.ds(s * t + a, n4, stride=p.pack), :], packed)
+            woven[pl.ds(s, n4, stride=p.own), :] = packed
+    o = p.own
+
+    def place(r, k):
+        return (r * p.km + k if k < p.km else p.n_row * p.km + r * (p.hk - p.km) + k - p.km) * o
+
+    def fill(left, right):
+        for r in range(p.n_row):
+            for c in range(p.n_col):
+                d, row = r * p.n_col + c, 0
+                spans = [(lint, place(r, k)) for k in left]
+                spans += [(rint, place(c * p.per + u, k)) for u in range(p.per) for k in right]
+                for source, start in spans:
+                    send[d, row:row + o] = source[start:start + o]
+                    row += o
+                if row < p.side_rows:
+                    send[d, row:p.side_rows] = jnp.zeros((p.side_rows - row, LANES), F32)
+
+    second = lax.rem(col_ref[0], p.split) == 1
+
+    @pl.when(jnp.logical_not(second))
+    def _():
+        fill(range(p.ek), range(p.hk))
+
+    @pl.when(second)
+    def _():
+        fill(range(p.hk), range(p.hk - p.ek, p.hk))
+
     side_ref[...] = send[...].astype(BF16)
+
+
+def home_kernel(p, col_ref, *refs):
+    part_refs = refs[:p.n_col]
+    out_ref, hold = refs[p.n_col:]
+    me = col_ref[0]
+    for shift in range(p.n_col):
+        hold[lax.rem(me + (p.n_col - shift), p.n_col)] = part_refs[shift][...].astype(F32)
+    both = 2 * p.half - p.rows
+    tail = p.per * p.i_main
+    for g in range(p.n_group):
+        for s in range(p.own):
+            rows = []
+            for u in range(p.per):
+                for skip, half in ((0, hold[g * p.split, s]), (both, hold[g * p.split + 1, s])):
+                    rows.append(half[u * p.i_main + min(skip, p.i_main):(u + 1) * p.i_main])
+                    rows.append(half[tail + u * p.i_rem + max(skip - p.i_main, 0):tail + (u + 1) * p.i_rem])
+            rows = [value for value in rows if value.shape[0]]
+            out_ref[g * p.own + s] = jnp.concatenate(rows, axis=0).astype(BF16)
 
 
 def outer_kernel(p, recv_ref, pair_ref, w_ref, wv_ref, wg_ref, mid_ref, edge_ref,
                  flat, rt, lhs, mid):
     flat[...] = recv_ref[...].reshape(p.n * p.side_rows, LANES).astype(F32)
 
-    def chunk(k):
+    def chunk(h, k):
         return jnp.concatenate(
-            [flat[pl.ds(k * p.own + s, p.n, stride=p.side_rows), :] for s in range(p.own)], axis=0)
-
-    for k in range(p.rk):
-        rt[k * LANES:(k + 1) * LANES, :] = jnp.transpose(chunk(k))
+            [flat[pl.ds(h * p.side_rows + k * p.own + s, p.n // p.split, stride=p.split * p.side_rows), :]
+             for s in range(p.own)], axis=0)
+
+    hk, ek = p.hk, p.ek
+    for u in range(p.per):
+        for k in range(p.lk):
+            value = chunk(0, ek + u * hk + k) if k < hk else chunk(1, hk + u * ek + k - hk)
+            row = (u * p.lk + k) * LANES
+            rt[row:row + LANES, :] = jnp.transpose(value)
     right = []
     for first in range(0, p.outer, p.pack):
         right.append(jnp.concatenate(
             [rt[pl.ds(first + d, p.cols, stride=p.outer), :] for d in range(p.pack)], axis=1))
     right = jnp.concatenate(right, axis=0).astype(BF16)
-    at = lane_iota(p.seq_total) // p.outer
+    at = over(lane_iota(p.seq_total), p.outer)
     left = []
     for g in range(p.lk):
-        base = chunk(p.rk + g)
+        base = chunk(0, g) if g < ek else chunk(1, g - ek)
         turned = [base] + [pltpu.roll(base, t * p.outer, axis=1) for t in range(1, p.pack)]
         for a in range(p.pack):
             left.append(jnp.concatenate(
@@ -277,6 +361,7 @@
         for c in range(p.n_col):
             flat[c, r * p.edge_rows:(r + 1) * p.edge_rows, :] = recv_ref[r * p.n_col + c].astype(F32)
     lane = lane_iota(p.m)
+    part_of = jnp.broadcast_to(lane_iota(1) // p.jslot, (p.m, LANES))
     blocks = p.per * p.ig
     rs[...] = jnp.zeros_like(rs)
     for ch in range(p.ch):
@@ -306,7 +391,7 @@
             for a in range(p.q):
                 turn = ((a - part) * p.jslot) % LANES
                 piece = pltpu.roll(rows[b][a], turn, axis=1) if turn else rows[b][a]
-                packed = piece if packed is None else jnp.where(lane // p.jslot == a, piece, packed)
+                packed = piece if packed is None else jnp.where(part_of == a, piece, packed)
             sb[c, pl.ds(ch, p.m, stride=p.ch), :] = packed
     used = p.ig * p.ch
     for r in range(p.n_row):
@@ -339,42 +424,42 @@
     n, ch, width = p.n, p.ch, p.width
     sds = jax.ShapeDtypeStruct
 
-    left_w, right_w = w_side[:, :p.outer], w_side[:, p.outer:]
-    left_w, right_w = jnp.tile(left_w, (1, p.pack)), jnp.tile(right_w, (1, p.pack))
+    side_w = jnp.concatenate([w_side[:, :p.outer]] * p.pack + [w_side[:, p.outer:]] * p.pack, axis=1)
     by_d = jnp.transpose(w_outer.reshape(p.outer, p.outer, width), (1, 0, 2)).reshape(w_outer.shape)
     blocks = jnp.transpose(w_tri.reshape(width, 5, width), (1, 2, 0)).reshape(5, n, ch, width)
     value_w = jnp.concatenate([blocks[0], blocks[2]], axis=1).reshape(n * 2 * ch, width)
     gate_w = jnp.concatenate([blocks[1], blocks[3]], axis=1).reshape(n * 2 * ch, width)
     own_gate_w = w_tri[:, 4 * width:]
     last_w = jnp.transpose(w_last.reshape(n, ch, width), (1, 0, 2)).reshape(width, width)
-    spot = np.arange(p.total).reshape(p.n_row, p.rows)
-    order = np.concatenate([spot[:, :p.i_main].reshape(-1), spot[:, p.i_main:].reshape(-1)])
-    sel = jnp.asarray((np.arange(p.total)[:, None] == np.repeat(order, p.heads)[None]), BF16)
 
     piece = call(functools.partial(bias_kernel, p), sds((n, p.bias_rows, LANES), BF16), [], [VMEM] * 2, "bias")(
         pair.reshape(p.rows * p.cols, width), w_bias.T)
     bias = lax.all_to_all(piece, ALL, 0, 0, tiled=True)
-    chunks = x.reshape(p.n_col, p.own, p.res, p.feat)
-    parts = []
-    for shift in range(p.n_col):
-        part = lax.dynamic_index_in_dim(chunks, lax.rem(col + shift, p.n_col), 0, keepdims=False)
-        if shift:
-            part = lax.ppermute(part, "col", [(c, (c + shift) % p.n_col) for c in range(p.n_col)])
-        parts.append(part)
-    seq = (p.own, p.total, p.feat)
-    q, k, v, gate, whole = call(
+    def ring(send):
+        parts = []
+        for shift in range(p.n_col):
+            part = send(lax.rem(col + shift, p.n_col))
+            if shift:
+                part = lax.ppermute(part, "col", [(c, (c + shift) % p.n_col) for c in range(p.n_col)])
+            parts.append(part)
+        return parts
+
+    at = col.reshape(1)
+    chunks = x.reshape(p.n_group, p.own, p.res, p.feat)
+    parts = ring(lambda to: lax.dynamic_index_in_dim(chunks, to // p.split, 0, keepdims=False))
+    mine, every = (p.own, p.queries, p.feat), (p.own, p.total, p.feat)
+    q, k, v, gate, rest = call(
         functools.partial(project_kernel, p),
-        (sds(seq, BF16), sds(seq, BF16), sds(seq, BF16), sds(seq, F32), sds(seq, F32)),
+        (sds(mine, BF16), sds(every, BF16), sds(every, BF16), sds(mine, F32), sds(mine, BF16)),
         [pltpu.VMEM((p.n_col, p.own, p.res, p.feat), F32)],
-        [SMEM] + [VMEM] * (p.n_col + 1), "project")(col.reshape(1), *parts, w_in)
+        [SMEM] + [VMEM] * (p.n_col + 1), "project")(at, *parts, w_in)
     emb, sides = call(
         functools.partial(attend_kernel, p),
-        (sds((p.n_col, p.own, p.res, p.feat), BF16), sds((n, p.side_rows, LANES), BF16)),
-        [pltpu.VMEM((p.total, p.total * p.heads), F32)]
-        + [pltpu.VMEM((p.total, LANES), F32)] * 2
-        + [pltpu.VMEM((p.total // p.pack * p.own, LANES), F32)] * 2
+        (sds((p.n_col, p.own, p.per * p.half, p.feat), BF16), sds((n, p.side_rows, LANES), BF16)),
+        [pltpu.VMEM((p.total, p.queries * p.heads), F32), pltpu.VMEM((2, p.own * p.queries, LANES), F32)]
+        + [pltpu.VMEM((p.queries // p.pack * p.own, LANES), F32)] * 2
         + [pltpu.VMEM((n, p.side_rows, LANES), F32)],
-        [VMEM] * 10, "attend")(q, k, v, gate, whole, bias, sel, w_out, left_w, right_w)
+        [SMEM] + [VMEM] * 8, "attend")(at, q, k, v, gate, rest, bias, w_out, side_w)
 
     sides = lax.all_to_all(sides, ALL, 0, 0, tiled=True)
     mid, edges = call(
@@ -399,12 +484,10 @@
          pltpu.VMEM((p.n_col, p.m * ch, LANES), F32)],
         [VMEM], "triangle")(edges)
 
-    home = jnp.zeros((p.n_col, p.own, p.res, p.feat), BF16)
-    for shift in range(p.n_col):
-        part = lax.dynamic_index_in_dim(emb, lax.rem(col + shift, p.n_col), 0, keepdims=False)
-        if shift:
-            part = lax.ppermute(part, "col", [(c, (c + shift) % p.n_col) for c in range(p.n_col)])
-        home = lax.dynamic_update_index_in_dim(home, part, lax.rem(col + p.n_col - shift, p.n_col), 0)
+    parts = ring(lambda to: lax.dynamic_index_in_dim(emb, to, 0, keepdims=False))
+    home = call(functools.partial(home_kernel, p), sds(x.shape, BF16),
+                [pltpu.VMEM((p.n_col, p.own, p.per * p.half, p.feat), F32)],
+                [SMEM] + [VMEM] * p.n_col, "home")(at, *parts)
 
     back = lax.all_to_all(back, ALL, 0, 0, tiled=True)
     state = call(
@@ -412,7 +495,7 @@
         [pltpu.VMEM((n * p.back_rows, LANES), F32), pltpu.VMEM((LANES, LANES), F32),
          pltpu.VMEM((p.rows * p.cols, LANES), F32)],
         [VMEM] * 4, "final")(back, mid, out_gate, last_w)
-    return home.reshape(x.shape), state
+    return home, state
 
 
 def general(

time: 79.3 us -> 75.1 us (0.947)
  waiting for transfers between devices: 40.5 us -> 20.5 us
  blocking collectives: 0 us -> 16.6 us
  starting transfers between devices: 21.3 us -> 20.5 us
    all_to_all x0 -> x1, blocking collectives: none -> 16.6 us  [fast(): edges = lax.all_to_all(edges, ALL, 0, 0, tiled=True)]
    all_to_all x1 -> x0, waiting for transfers between devices: 11.1 us -> none  [fast(): edges = lax.all_to_all(edges, ALL, 0, 0, tiled=True)]
    all_to_all x1, waiting for transfers between devices: 9.82 us -> 3.47 us  [fast(): back = lax.all_to_all(back, ALL, 0, 0, tiled=True)]
    all_to_all x1, waiting for transfers between devices: 6.05 us -> 1.54 us  [fast(): bias = lax.all_to_all(piece, ALL, 0, 0, tiled=True)]
    all_to_all x1 -> x0, starting transfers between devices: 2.6 us -> none  [fast(): edges = lax.all_to_all(edges, ALL, 0, 0, tiled=True)]
    ppermute x6, waiting for transfers between devices: 4.18 us -> 6.15 us  [ring(): lax.ppermute(part, 'col', [(c, (c + shift) % p.n_col) for c in range(p.n_...]
    all_to_all x1, starting transfers between devices: 2.76 us -> 3.82 us  [fast(): sides = lax.all_to_all(sides, ALL, 0, 0, tiled=True)]
    pallas_call x2 -> x3, Pallas kernels: 4.04 us -> 4.73 us  [the longest x1 3.23 us: fast(): call(functools.partial(attend_kernel, p), (sds((p.n_col, p.own, p.per * p...]
  transfers between devices with their start and end apart: 10 -> 9, of which waited for: 6 -> 8; matrix products, arithmetic and copies ran while one was open for 1% -> 1% of each run, Pallas kernels for 4% -> 3%
where the time goes in v3:
time: 75.1 us; the launch traced here: 74.7 us
  starting transfers between devices  20.5 us (27%)
  waiting for transfers between devices  20.5 us (27%)
  blocking collectives  16.6 us (22%)
  Pallas kernels  12.1 us (16%)
  local copies, waits for them, and re-layouts  3.95 us (5%)
  between operations  0.94 us (1%)
    all_to_all x1, blocking collectives, fast(): edges = lax.all_to_all(edges, ALL, 0, 0, tiled=True)  16.6 us
    all_to_all x1, waiting for transfers between devices, fast(): sides = lax.all_to_all(sides, ALL, 0, 0, tiled=True)  9.39 us
    all_to_all x1, starting transfers between devices, fast(): bias = lax.all_to_all(piece, ALL, 0, 0, tiled=True)  7.32 us
    ppermute x6, starting transfers between devices, ring(): lax.ppermute(part, 'col', [(c, (c + shift) % p.n_col) for c in range(p.n_...  6.57 us
    ppermute x6, waiting for transfers between devices, ring(): lax.ppermute(part, 'col', [(c, (c + shift) % p.n_col) for c in range(p.n_...  6.15 us
    all_to_all x1, starting transfers between devices, fast(): sides = lax.all_to_all(sides, ALL, 0, 0, tiled=True)  3.82 us
    unnamed x22, local copies, waits for them, and re-layouts  3.49 us
    all_to_all x1, waiting for transfers between devices, fast(): back = lax.all_to_all(back, ALL, 0, 0, tiled=True)  3.47 us
  transfers between devices with their start and end apart: 9, of which 8 were waited for; matrix products, arithmetic and copies ran while one was open for 1% of the time, Pallas kernels for 3%

profile of v3, /device:TPU:0, one launch (start us, length us, event | category | flops | bytes accessed | tf_op | source)
XLA Modules:
  0.0 74.7 jit_solution(17747337909268919015)
XLA Ops:
  1.3 0.9 %copy-done.2 = bf16[20,40,128]{2,1,0:T(8,128)(2,1)S(1)} copy-done((bf16[20,40,128]{2,1,0:T(8,128)(2,1)S(1)}, bf16[20,40,128]{2,1,0:T(8,128)(2,1)}, u32[]{:S(2)}) %copy-start.2) | copy-done | bytes 204824
  2.2 1.4 %bias.1 = bf16[32,32,128]{2,1,0:T(8,128)(2,1)} custom-call(bf16[800,128]{1,0:T(8,128)(2,1)S(1)} %bitcast.41, bf16[8,128]{1,0:T(8,128)(2,1)S(1)} %bitcast.42), custom_call_target="tpu_custom_call" | custom-call | flops 400000000 | bytes 4000000 | tf_op jit(solution)/shard_map/bias/pallas_call | solution.py:435
  3.6 7.3 %all-to-all-start = ((bf16[32,32,128]{2,1,0:T(8,128)(2,1)}), bf16[32,32,128]{2,1,0:T(8,128)(2,1)S(1)}, u32[]{:S(2)}, u32[]{:S(2)}) async-start(bf16[32,32,128]{2,1,0:T(8,128)(2,1)} %bias.1), calls=%async_computation | async-start | bytes 524288 | tf_op jit(solution)/shard_map/all_to_all | solution.py:437
  11.1 0.8 %copy-done.5 = bf16[8,40,256]{2,1,0:T(8,128)(2,1)S(1)} copy-done((bf16[8,40,256]{2,1,0:T(8,128)(2,1)S(1)}, bf16[8,40,256]{2,1,0:T(8,128)(2,1)}, u32[]{:S(2)}) %copy-start.5) | copy-done | bytes 163864
  12.2 1.6 %collective-permute-start.1 = (bf16[4,40,256]{2,1,0:T(8,128)(2,1)S(1)}, bf16[4,40,256]{2,1,0:T(8,128)(2,1)S(1)}, u32[]{:S(2)}, u32[]{:S(2)}) collective-permute-start(bf16[4,40,256]{2,1,0:T(8,128)(2,1)S(1)} %get-tuple-element.29), channel_id=1, source_target_pairs={{0,2},{1,3},{2,0},{3,1},{4,6},{5,7},{6,4},{7,5},{8,10},{9,11},{10,... | collective-permute-start | bytes 245768 | tf_op jit(solution)/shard_map/ppermute | solution.py:443
  13.9 1.4 %collective-permute-start.2 = (bf16[4,40,256]{2,1,0:T(8,128)(2,1)S(1)}, bf16[4,40,256]{2,1,0:T(8,128)(2,1)S(1)}, u32[]{:S(2)}, u32[]{:S(2)}) collective-permute-start(bf16[4,40,256]{2,1,0:T(8,128)(2,1)S(1)} %get-tuple-element.28), channel_id=1, source_target_pairs={{0,3},{1,0},{2,1},{3,2},{4,7},{5,4},{6,5},{7,6},{8,11},{9,8},{10,9... | collective-permute-start | bytes 245768 | tf_op jit(solution)/shard_map/ppermute | solution.py:443
  15.6 1.9 %collective-permute-done.refs_1_ = bf16[4,40,256]{2,1,0:T(8,128)(2,1)S(1)} collective-permute-done((bf16[4,40,256]{2,1,0:T(8,128)(2,1)S(1)}, bf16[4,40,256]{2,1,0:T(8,128)(2,1)S(1)}, u32[]{:S(2)}, u32[]{:S(2)}) %collective-permute-start) | collective-permute-done | bytes 81952 | tf_op jit(solution)/shard_map/ppermute | solution.py:443
  17.6 1.0 %collective-permute-done.1.refs_2_ = bf16[4,40,256]{2,1,0:T(8,128)(2,1)S(1)} collective-permute-done((bf16[4,40,256]{2,1,0:T(8,128)(2,1)S(1)}, bf16[4,40,256]{2,1,0:T(8,128)(2,1)S(1)}, u32[]{:S(2)}, u32[]{:S(2)}) %collective-permute-start.1) | collective-permute-done | bytes 81952 | tf_op jit(solution)/shard_map/ppermute | solution.py:443
  19.2 0.8 %project.1 = (bf16[4,96,256]{2,1,0:T(8,128)(2,1)S(1)}, bf16[4,160,256]{2,1,0:T(8,128)(2,1)S(1)}, bf16[4,160,256]{2,1,0:T(8,128)(2,1)S(1)}, f32[4,96,256]{2,1,0:T(8,128)S(1)}, bf16[4,96,256]{2,1,0:T(8,128)(2,1)S(1)}) custom-call(s32[1]{0:T(128)} %bitcast.col_ref, bf16[4,40,256]{2,1,0:T(8,128)(2,1)S(1)} %get-tuple-element.31.refs_0_, ...), custom_call_target="tpu_custom_call" | custom-call | flops 400000000 | bytes 4000000 | tf_op jit(solution)/shard_map/project/pallas_call | solution.py:451
  20.0 1.5 %all-to-all-done.bias_ref = bf16[32,32,128]{2,1,0:T(8,128)(2,1)S(1)} async-done(((bf16[32,32,128]{2,1,0:T(8,128)(2,1)}), bf16[32,32,128]{2,1,0:T(8,128)(2,1)S(1)}, u32[]{:S(2)}, u32[]{:S(2)}) %all-to-all-start) | async-done | bytes 262176 | tf_op jit(solution)/shard_map/all_to_all | solution.py:437
  21.6 3.2 %attend.1 = (bf16[4,4,24,256]{3,2,1,0:T(8,128)(2,1)S(1)}, bf16[32,32,128]{2,1,0:T(8,128)(2,1)}) custom-call(s32[1]{0:T(128)} %bitcast.col_ref, bf16[4,96,256]{2,1,0:T(8,128)(2,1)S(1)} %get-tuple-element.11.q_ref, bf16[4,160,256]{2,1,0:T(8,128)(2,1)S(1)} %get-tuple-element.12.k_ref, bf16[4,160,256]{2,1,0:T(8,128)(2,1)S(1)} %get-tuple-element.13.v_ref, ...), custom_call_target="tpu_custom_call" | custom-call | flops 400000000 | bytes 4000000 | tf_op jit(solution)/shard_map/attend/pallas_call | solution.py:456
  24.8 3.8 %all-to-all-start.1 = ((bf16[32,32,128]{2,1,0:T(8,128)(2,1)}), bf16[32,32,128]{2,1,0:T(8,128)(2,1)S(1)}, u32[]{:S(2)}, u32[]{:S(2)}) async-start(bf16[32,32,128]{2,1,0:T(8,128)(2,1)} %get-tuple-element.17), calls=%async_computation.1 | async-start | bytes 524288 | tf_op jit(solution)/shard_map/all_to_all | solution.py:464
  28.8 0.8 %copy-done.6 = bf16[1024,128]{1,0:T(8,128)(2,1)S(1)} copy-done((bf16[1024,128]{1,0:T(8,128)(2,1)S(1)}, bf16[1024,128]{1,0:T(8,128)(2,1)}, u32[]{:S(2)}) %copy-start.6) | copy-done | bytes 262168
  29.8 9.4 %all-to-all-done.1.recv_ref = bf16[32,32,128]{2,1,0:T(8,128)(2,1)S(1)} async-done(((bf16[32,32,128]{2,1,0:T(8,128)(2,1)}), bf16[32,32,128]{2,1,0:T(8,128)(2,1)S(1)}, u32[]{:S(2)}, u32[]{:S(2)}) %all-to-all-start.1) | async-done | bytes 262176 | tf_op jit(solution)/shard_map/all_to_all | solution.py:464
  39.2 2.4 %outer.1 = (bf16[20,40,128]{2,1,0:T(8,128)(2,1)S(1)}, bf16[32,56,128]{2,1,0:T(8,128)(2,1)S(1)}) custom-call(bf16[32,32,128]{2,1,0:T(8,128)(2,1)S(1)} %all-to-all-done.1.recv_ref, bf16[20,40,128]{2,1,0:T(8,128)(2,1)S(1)} %copy-done.3, bf16[1024,128]{1,0:T(8,128)(2,1)S(1)} %bitcast.39, bf16[256,128]{1,0:T(8,128)(2,1)S(1)} %get-tuple-element.34.wv_ref, ...), custom_call_target="tpu_custom_call" | custom-call | flops 400000000 | bytes 4000000 | tf_op jit(solution)/shard_map/outer/pallas_call | solution.py:465
  41.6 16.6 %all_to_all.20.recv_ref = bf16[32,56,128]{2,1,0:T(8,128)(2,1)S(1)} all-to-all(bf16[32,56,128]{2,1,0:T(8,128)(2,1)S(1)} %get-tuple-element.18), channel_id=1, replica_groups=mesh['row'=8,'col'=4] {'row','col'}, dimensions={0} | all-to-all | bytes 917504 | tf_op jit(solution)/shard_map/all_to_all | solution.py:474
  58.2 1.8 %triangle.1 = bf16[32,32,128]{2,1,0:T(8,128)(2,1)} custom-call(bf16[32,56,128]{2,1,0:T(8,128)(2,1)S(1)} %all_to_all.20.recv_ref), custom_call_target="tpu_custom_call" | custom-call | flops 400000000 | bytes 4000000 | tf_op jit(solution)/shard_map/triangle/pallas_call | solution.py:478
  60.0 2.8 %all-to-all-start.3 = ((bf16[32,32,128]{2,1,0:T(8,128)(2,1)}), bf16[32,32,128]{2,1,0:T(8,128)(2,1)S(1)}, u32[]{:S(2)}, u32[]{:S(2)}) async-start(bf16[32,32,128]{2,1,0:T(8,128)(2,1)} %triangle.1), calls=%async_computation.3 | async-start | bytes 524288 | tf_op jit(solution)/shard_map/all_to_all | solution.py:492
  63.1 1.6 %collective-permute-start.4 = (bf16[4,24,256]{2,1,0:T(8,128)(2,1)S(1)}, bf16[4,24,256]{2,1,0:T(8,128)(2,1)S(1)}, u32[]{:S(2)}, u32[]{:S(2)}) collective-permute-start(bf16[4,24,256]{2,1,0:T(8,128)(2,1)S(1)} %get-tuple-element.21), channel_id=1, source_target_pairs={{0,2},{1,3},{2,0},{3,1},{4,6},{5,7},{6,4},{7,5},{8,10},{9,11},{10,... | collective-permute-start | bytes 147464 | tf_op jit(solution)/shard_map/ppermute | solution.py:443
  64.8 1.4 %collective-permute-start.5 = (bf16[4,24,256]{2,1,0:T(8,128)(2,1)S(1)}, bf16[4,24,256]{2,1,0:T(8,128)(2,1)S(1)}, u32[]{:S(2)}, u32[]{:S(2)}) collective-permute-start(bf16[4,24,256]{2,1,0:T(8,128)(2,1)S(1)} %get-tuple-element.20), channel_id=1, source_target_pairs={{0,3},{1,0},{2,1},{3,2},{4,7},{5,4},{6,5},{7,6},{8,11},{9,8},{10,9... | collective-permute-start | bytes 147464 | tf_op jit(solution)/shard_map/ppermute | solution.py:443
  66.8 1.9 %collective-permute-done.4.refs_2_ = bf16[4,24,256]{2,1,0:T(8,128)(2,1)S(1)} collective-permute-done((bf16[4,24,256]{2,1,0:T(8,128)(2,1)S(1)}, bf16[4,24,256]{2,1,0:T(8,128)(2,1)S(1)}, u32[]{:S(2)}, u32[]{:S(2)}) %collective-permute-start.4) | collective-permute-done | bytes 49184 | tf_op jit(solution)/shard_map/ppermute | solution.py:443
  68.7 0.7 home.1
  69.9 3.5 %all-to-all-done.3.recv_ref = bf16[32,32,128]{2,1,0:T(8,128)(2,1)S(1)} async-done(((bf16[32,32,128]{2,1,0:T(8,128)(2,1)}), bf16[32,32,128]{2,1,0:T(8,128)(2,1)S(1)}, u32[]{:S(2)}, u32[]{:S(2)}) %all-to-all-start.3) | async-done | bytes 262176 | tf_op jit(solution)/shard_map/all_to_all | solution.py:492
  73.3 1.3 %final.1 = bf16[20,40,128]{2,1,0:T(8,128)(2,1)} custom-call(bf16[32,32,128]{2,1,0:T(8,128)(2,1)S(1)} %all-to-all-done.3.recv_ref, bf16[20,40,128]{2,1,0:T(8,128)(2,1)S(1)} %get-tuple-element.19.mid_ref, f32[800,128]{1,0:T(8,128)S(1)} %gate.1.gate_ref, bf16[128,128]{1,0:T(8,128)(2,1)S(1)} %bitcast.40), custom_call_target="tpu_custom_call" | custom-call | flops 400000000 | bytes 4000000 | tf_op jit(solution)/shard_map/final/pallas_call | solution.py:493
  (34 shorter events, 3.8 us)
Async XLA Ops:
  0.6 0.7 copy-start.4
  1.3 0.9 %copy-start.2 = (bf16[20,40,128]{2,1,0:T(8,128)(2,1)S(1)}, bf16[20,40,128]{2,1,0:T(8,128)(2,1)}, u32[]{:S(2)}) copy-start(bf16[20,40,128]{2,1,0:T(8,128)(2,1)} %pair_ref.1) | copy-start | bytes 614404
  3.6 17.9 %all-to-all-start = ((bf16[32,32,128]{2,1,0:T(8,128)(2,1)}), bf16[32,32,128]{2,1,0:T(8,128)(2,1)S(1)}, u32[]{:S(2)}, u32[]{:S(2)}) async-start(bf16[32,32,128]{2,1,0:T(8,128)(2,1)} %bias.1), calls=%async_computation | async-start | bytes 524288 | tf_op jit(solution)/shard_map/all_to_all | solution.py:437
  11.0 0.9 %copy-start.5 = (bf16[8,40,256]{2,1,0:T(8,128)(2,1)S(1)}, bf16[8,40,256]{2,1,0:T(8,128)(2,1)}, u32[]{:S(2)}) copy-start(bf16[8,40,256]{2,1,0:T(8,128)(2,1)} %param.9) | copy-start | bytes 491524
  11.9 3.3 %copy-start.8 = (bf16[256,64]{0,1:T(8,128)(2,1)S(1)}, bf16[256,64]{0,1:T(8,128)(2,1)}, u32[]{:S(2)}) copy-start(bf16[256,64]{0,1:T(8,128)(2,1)} %param.14) | copy-start | bytes 98308
  11.9 7.3 %copy-start.1 = (bf16[256,1024]{1,0:T(8,128)(2,1)S(1)}, bf16[256,1024]{1,0:T(8,128)(2,1)}, u32[]{:S(2)}) copy-start(bf16[256,1024]{1,0:T(8,128)(2,1)} %refs_4_.1) | copy-start | bytes 1572868
  11.9 5.6 %collective-permute-start = (bf16[4,40,256]{2,1,0:T(8,128)(2,1)S(1)}, bf16[4,40,256]{2,1,0:T(8,128)(2,1)S(1)}, u32[]{:S(2)}, u32[]{:S(2)}) collective-permute-start(bf16[4,40,256]{2,1,0:T(8,128)(2,1)S(1)} %get-tuple-element.30), channel_id=1, source_target_pairs={{0,1},{1,2},{2,3},{3,0},{4,5},{5,6},{6,7},{7,4},{8,9},{9,10},{10,1... | collective-permute-start | bytes 245768 | tf_op jit(solution)/shard_map/ppermute | solution.py:443
  12.2 6.3 %collective-permute-start.1 = (bf16[4,40,256]{2,1,0:T(8,128)(2,1)S(1)}, bf16[4,40,256]{2,1,0:T(8,128)(2,1)S(1)}, u32[]{:S(2)}, u32[]{:S(2)}) collective-permute-start(bf16[4,40,256]{2,1,0:T(8,128)(2,1)S(1)} %get-tuple-element.29), channel_id=1, source_target_pairs={{0,2},{1,3},{2,0},{3,1},{4,6},{5,7},{6,4},{7,5},{8,10},{9,11},{10,... | collective-permute-start | bytes 245768 | tf_op jit(solution)/shard_map/ppermute | solution.py:443
  13.9 5.3 %collective-permute-start.2 = (bf16[4,40,256]{2,1,0:T(8,128)(2,1)S(1)}, bf16[4,40,256]{2,1,0:T(8,128)(2,1)S(1)}, u32[]{:S(2)}, u32[]{:S(2)}) collective-permute-start(bf16[4,40,256]{2,1,0:T(8,128)(2,1)S(1)} %get-tuple-element.28), channel_id=1, source_target_pairs={{0,3},{1,0},{2,1},{3,2},{4,7},{5,4},{6,5},{7,6},{8,11},{9,8},{10,9... | collective-permute-start | bytes 245768 | tf_op jit(solution)/shard_map/ppermute | solution.py:443
  19.2 2.3 %copy-start = (bf16[256,256]{1,0:T(8,128)(2,1)S(1)}, bf16[256,256]{1,0:T(8,128)(2,1)}, u32[]{:S(2)}) copy-start(bf16[256,256]{1,0:T(8,128)(2,1)} %wf_ref.1) | copy-start | bytes 393220
  24.8 3.8 %copy-start.7 = (bf16[128,640]{1,0:T(8,128)(2,1)S(1)}, bf16[128,640]{1,0:T(8,128)(2,1)}, u32[]{:S(2)}) copy-start(bf16[128,640]{1,0:T(8,128)(2,1)} %param.16) | copy-start | bytes 491524
  24.8 14.4 %all-to-all-start.1 = ((bf16[32,32,128]{2,1,0:T(8,128)(2,1)}), bf16[32,32,128]{2,1,0:T(8,128)(2,1)S(1)}, u32[]{:S(2)}, u32[]{:S(2)}) async-start(bf16[32,32,128]{2,1,0:T(8,128)(2,1)} %get-tuple-element.17), calls=%async_computation.1 | async-start | bytes 524288 | tf_op jit(solution)/shard_map/all_to_all | solution.py:464
  28.6 1.0 %copy-start.6 = (bf16[1024,128]{1,0:T(8,128)(2,1)S(1)}, bf16[1024,128]{1,0:T(8,128)(2,1)}, u32[]{:S(2)}) copy-start(bf16[1024,128]{1,0:T(8,128)(2,1)} %param.15) | copy-start | bytes 786436
  29.7 9.5 %copy-start.3 = (bf16[20,40,128]{2,1,0:T(8,128)(2,1)S(1)}, bf16[20,40,128]{2,1,0:T(8,128)(2,1)}, u32[]{:S(2)}) copy-start(bf16[20,40,128]{2,1,0:T(8,128)(2,1)} %pair_ref.1) | copy-start | bytes 614404
  60.0 13.3 %all-to-all-start.3 = ((bf16[32,32,128]{2,1,0:T(8,128)(2,1)}), bf16[32,32,128]{2,1,0:T(8,128)(2,1)S(1)}, u32[]{:S(2)}, u32[]{:S(2)}) async-start(bf16[32,32,128]{2,1,0:T(8,128)(2,1)} %triangle.1), calls=%async_computation.3 | async-start | bytes 524288 | tf_op jit(solution)/shard_map/all_to_all | solution.py:492
  62.8 3.9 %collective-permute-start.3 = (bf16[4,24,256]{2,1,0:T(8,128)(2,1)S(1)}, bf16[4,24,256]{2,1,0:T(8,128)(2,1)S(1)}, u32[]{:S(2)}, u32[]{:S(2)}) collective-permute-start(bf16[4,24,256]{2,1,0:T(8,128)(2,1)S(1)} %get-tuple-element.22), channel_id=1, source_target_pairs={{0,1},{1,2},{2,3},{3,0},{4,5},{5,6},{6,7},{7,4},{8,9},{9,10},{10,1... | collective-permute-start | bytes 147464 | tf_op jit(solution)/shard_map/ppermute | solution.py:443
  63.1 5.6 %collective-permute-start.4 = (bf16[4,24,256]{2,1,0:T(8,128)(2,1)S(1)}, bf16[4,24,256]{2,1,0:T(8,128)(2,1)S(1)}, u32[]{:S(2)}, u32[]{:S(2)}) collective-permute-start(bf16[4,24,256]{2,1,0:T(8,128)(2,1)S(1)} %get-tuple-element.21), channel_id=1, source_target_pairs={{0,2},{1,3},{2,0},{3,1},{4,6},{5,7},{6,4},{7,5},{8,10},{9,11},{10,... | collective-permute-start | bytes 147464 | tf_op jit(solution)/shard_map/ppermute | solution.py:443
  64.8 1.4 %copy-start.9 = (bf16[128,128]{1,0:T(8,128)(2,1)S(1)}, bf16[128,128]{1,0:T(8,128)(2,1)}, u32[]{:S(2)}) copy-start(bf16[128,128]{1,0:T(8,128)(2,1)} %param.17) | copy-start | bytes 98308
  64.8 4.0 %collective-permute-start.5 = (bf16[4,24,256]{2,1,0:T(8,128)(2,1)S(1)}, bf16[4,24,256]{2,1,0:T(8,128)(2,1)S(1)}, u32[]{:S(2)}, u32[]{:S(2)}) collective-permute-start(bf16[4,24,256]{2,1,0:T(8,128)(2,1)S(1)} %get-tuple-element.20), channel_id=1, source_target_pairs={{0,3},{1,0},{2,1},{3,2},{4,7},{5,4},{6,5},{7,6},{8,11},{9,8},{10,9... | collective-permute-start | bytes 147464 | tf_op jit(solution)/shard_map/ppermute | solution.py:443

commit v4 on v3

--- a/solution.py
+++ b/solution.py
@@ -9,6 +9,7 @@
 
 epsilon = 1e-05
 LANES = 128
+MOST_VMEM = 67_043_328
 SUBLANES = 8
 F32 = jnp.float32
 BF16 = jnp.bfloat16
@@ -16,6 +17,7 @@
 NT = (((1,), (1,)), ((), ()))
 VMEM = pl.BlockSpec(memory_space=pltpu.VMEM)
 SMEM = pl.BlockSpec(memory_space=pltpu.SMEM)
+HBM = pl.BlockSpec(memory_space=pltpu.HBM)
 
 
 def standardize_features(inputs, axis=-1):
@@ -49,16 +51,16 @@
     return lax.bitwise_and(index, jnp.int32(size - 1))
 
 
-def call(body, out_shape, scratch, in_specs, name):
+def call(body, out_shape, scratch, in_specs, name, limit=24, out_spec=VMEM):
     return pl.pallas_call(
         body,
         out_shape=out_shape,
         in_specs=in_specs,
-        out_specs=jax.tree.map(lambda _: VMEM, out_shape),
+        out_specs=out_spec if isinstance(out_spec, tuple) else jax.tree.map(lambda _: out_spec, out_shape),
         scratch_shapes=scratch,
         name=name,
         cost_estimate=pl.CostEstimate(flops=400_000_000, bytes_accessed=4_000_000, transcendentals=0),
-        compiler_params=pltpu.CompilerParams(vmem_limit_bytes=24 * 1024 * 1024),
+        compiler_params=pltpu.CompilerParams(vmem_limit_bytes=min(limit * 1024 * 1024, MOST_VMEM)),
     )
 
 
@@ -132,15 +134,19 @@
             return
         self.m = n_row * self.ig
         self.edge_rows = self.ig * SUBLANES
-        self.back_rows = -(-self.ig * self.ch // 16) * 16
         self.ok = True
 
     def j_base(self, c):
         return (c // self.q) * LANES + (c % self.q) * self.jslot
 
 
-def bias_kernel(p, pair_ref, w_ref, out_ref):
-    normed = standardize_features(pair_ref[...])
+def bias_kernel(p, pair_hbm, w_hbm, out_hbm, pair_ref, w_ref, piece_ref, sems, out_sems):
+    copies = [pltpu.make_async_copy(pair_hbm, pair_ref, sems.at[0]), pltpu.make_async_copy(w_hbm, w_ref, sems.at[1])]
+    for copy in copies:
+        copy.start()
+    for copy in copies:
+        copy.wait()
+    normed = standardize_features(pair_ref[...]).reshape(p.rows * p.cols, p.width)
     heads = p.heads
     spread = modulo(lane_iota(heads), heads) == row_iota(heads)
     tiled = lax.dot_general(w_ref[...], jnp.where(spread, 1.0, 0.0).astype(BF16), (((0,), (0,)), ((), ())),
@@ -164,9 +170,13 @@
             for g, (b, lane) in enumerate(places):
                 here = (at >= lane) & (at < lane + wide)
                 blocks[b] = jnp.where(here, value[g * SUBLANES:(g + 1) * SUBLANES], blocks[b])
-        pieces.append(jnp.concatenate(blocks, axis=0).astype(BF16))
-    for d in range(p.n):
-        out_ref[d] = pieces[d % p.n_col % p.split]
+        piece_ref[h] = jnp.concatenate(blocks, axis=0).astype(BF16)
+        for d in range(p.n):
+            if d % p.n_col % p.split == h:
+                pieces.append(pltpu.make_async_copy(piece_ref.at[h], out_hbm.at[d], out_sems.at[d]))
+                pieces[-1].start()
+    for copy in pieces:
+        copy.wait()
 
 
 def pick_half(p, second, rows):
@@ -199,7 +209,7 @@
 
 
 def attend_kernel(p, col_ref, q_ref, k_ref, v_ref, gate_ref, x_ref, bias_ref, wf_ref, ws_ref,
-                  emb_ref, side_ref, bias, four, lint, rint, send):
+                  emb_ref, side_hbm, bias, four, lint, rint, send, side_ref, sems):
     h, t, f, m = p.heads, p.queries, p.feat, p.half
     at = lane_iota(SUBLANES)
     for first, places, wide in ((0, p.main_at, p.main), (p.n_row * p.main, p.rem_at, p.rem)):
@@ -267,6 +277,13 @@
                     row += o
                 if row < p.side_rows:
                     send[d, row:p.side_rows] = jnp.zeros((p.side_rows - row, LANES), F32)
+            block = slice(r * p.n_col, (r + 1) * p.n_col)
+            side_ref[block] = send[block].astype(BF16)
+            leave(r).start()
+
+    def leave(r):
+        block = pl.ds(r * p.n_col, p.n_col)
+        return pltpu.make_async_copy(side_ref.at[block], side_hbm.at[block], sems.at[r])
 
     second = lax.rem(col_ref[0], p.split) == 1
 
@@ -278,7 +295,8 @@
     def _():
         fill(range(p.hk), range(p.hk - p.ek, p.hk))
 
-    side_ref[...] = send[...].astype(BF16)
+    for r in range(p.n_row):
+        leave(r).wait()
 
 
 def home_kernel(p, col_ref, *refs):
@@ -300,7 +318,7 @@
             out_ref[g * p.own + s] = jnp.concatenate(rows, axis=0).astype(BF16)
 
 
-def outer_kernel(p, recv_ref, pair_ref, w_ref, wv_ref, wg_ref, mid_ref, edge_ref,
+def outer_kernel(p, recv_ref, pair_ref, w_ref, wv_ref, wg_ref, wo_ref, mid_ref, edge_ref, gate_ref,
                  flat, rt, lhs, mid):
     flat[...] = recv_ref[...].reshape(p.n * p.side_rows, LANES).astype(F32)
 
@@ -349,11 +367,8 @@
         gate = jax.nn.sigmoid(dot_nt(wg_ref[...], normed))
         edge_ref[:, k * SUBLANES:(k + 1) * SUBLANES, :] = (gate * value).reshape(
             p.n, SUBLANES, LANES).astype(BF16)
-
-
-def gate_kernel(p, mid_ref, w_ref, out_ref):
-    normed = standardize_features(mid_ref[...]).reshape(p.rows * p.cols, p.width).astype(BF16)
-    out_ref[...] = jax.nn.sigmoid(dot(normed, w_ref[...]))
+        many = min(step, p.rows * p.cols - k * step)
+        gate_ref[k * step:k * step + many, :] = jax.nn.sigmoid(dot(normed, wo_ref[...]))[:many]
 
 
 def triangle_kernel(p, recv_ref, out_ref, flat, ls, rs, os, sb):
@@ -393,30 +408,35 @@
                 piece = pltpu.roll(rows[b][a], turn, axis=1) if turn else rows[b][a]
                 packed = piece if packed is None else jnp.where(part_of == a, piece, packed)
             sb[c, pl.ds(ch, p.m, stride=p.ch), :] = packed
-    used = p.ig * p.ch
     for r in range(p.n_row):
         for c in range(p.n_col):
-            d = r * p.n_col + c
-            out_ref[d, 0:used] = sb[c, r * used:(r + 1) * used, :].astype(BF16)
-            if used < p.back_rows:
-                out_ref[d, used:p.back_rows] = jnp.zeros((p.back_rows - used, LANES), BF16)
-
-
-def final_kernel(p, recv_ref, mid_ref, gate_ref, w_ref, out_ref, flat, hold, update):
-    flat[...] = recv_ref[...].reshape(p.n * p.back_rows, LANES).astype(F32)
+            for k in range(p.ig):
+                row = (r * p.ig + k) * p.ch
+                out_ref[r * p.n_col + c, k] = sb[c, row:row + p.ch, :].astype(BF16)
+
+
+def final_kernel(p, recv_ref, mid_ref, gate_ref, w_ref, out_hbm, flat, hold, update, out_ref, sems):
+    copies = []
     for k in range(p.ig):
-        summed = jnp.concatenate(
-            [flat[pl.ds(k * p.ch + ch, p.n, stride=p.back_rows), :] for ch in range(p.ch)], axis=0)
-        normed = jnp.transpose(standardize_features(summed, axis=0)).astype(BF16)
-        hold[...] = dot(normed, w_ref[...])
-        for a in range(p.q):
-            i = k * p.q + a
-            if i < p.rows:
-                for u in range(p.per):
-                    update[i * p.cols + u * p.rows:i * p.cols + (u + 1) * p.rows, :] = hold[
-                        a * p.jslot + u * p.ipad:a * p.jslot + u * p.ipad + p.rows, :]
-    fresh = mid_ref[...].astype(F32).reshape(p.rows * p.cols, p.width) + gate_ref[...] * update[...]
-    out_ref[...] = fresh.reshape(p.rows, p.cols, p.width).astype(BF16)
+        for d in range(p.n):
+            flat[k, d * p.ch:(d + 1) * p.ch, :] = recv_ref[d, k].astype(F32)
+    for k in range(p.ig):
+        normed = jnp.transpose(standardize_features(flat[k], axis=0)).astype(BF16)
+        hold[k] = dot(normed, w_ref[...])
+        first, last = k * p.q, min((k + 1) * p.q, p.rows)
+        for i in range(first, last):
+            for u in range(p.per):
+                row = (i - first) * p.jslot + u * p.ipad
+                update[i * p.cols + u * p.rows:i * p.cols + (u + 1) * p.rows, :] = hold[k, row:row + p.rows, :]
+        span = slice(first * p.cols, last * p.cols)
+        fresh = mid_ref[first:last].astype(F32) + (gate_ref[span] * update[span]).reshape(
+            last - first, p.cols, p.width)
+        out_ref[first:last] = fresh.astype(BF16)
+        rows = pl.ds(first, last - first)
+        copies.append(pltpu.make_async_copy(out_ref.at[rows], out_hbm.at[rows], sems.at[k]))
+        copies[-1].start()
+    for copy in copies:
+        copy.wait()
 
 
 def fast(p, x, pair, w_in, w_out, w_bias, w_side, w_outer, w_tri, w_last):
@@ -430,10 +450,11 @@
     value_w = jnp.concatenate([blocks[0], blocks[2]], axis=1).reshape(n * 2 * ch, width)
     gate_w = jnp.concatenate([blocks[1], blocks[3]], axis=1).reshape(n * 2 * ch, width)
     own_gate_w = w_tri[:, 4 * width:]
-    last_w = jnp.transpose(w_last.reshape(n, ch, width), (1, 0, 2)).reshape(width, width)
-
-    piece = call(functools.partial(bias_kernel, p), sds((n, p.bias_rows, LANES), BF16), [], [VMEM] * 2, "bias")(
-        pair.reshape(p.rows * p.cols, width), w_bias.T)
+
+    piece = call(functools.partial(bias_kernel, p), sds((n, p.bias_rows, LANES), BF16),
+                 [pltpu.VMEM(pair.shape, BF16), pltpu.VMEM((p.heads, width), BF16),
+                  pltpu.VMEM((p.split, p.bias_rows, LANES), BF16), pltpu.SemaphoreType.DMA((2,)),
+                  pltpu.SemaphoreType.DMA((n,))], [HBM] * 2, "bias", limit=64, out_spec=HBM)(pair, w_bias.T)
     bias = lax.all_to_all(piece, ALL, 0, 0, tiled=True)
     def ring(send):
         parts = []
@@ -458,25 +479,32 @@
         (sds((p.n_col, p.own, p.per * p.half, p.feat), BF16), sds((n, p.side_rows, LANES), BF16)),
         [pltpu.VMEM((p.total, p.queries * p.heads), F32), pltpu.VMEM((2, p.own * p.queries, LANES), F32)]
         + [pltpu.VMEM((p.queries // p.pack * p.own, LANES), F32)] * 2
-        + [pltpu.VMEM((n, p.side_rows, LANES), F32)],
-        [SMEM] + [VMEM] * 8, "attend")(at, q, k, v, gate, rest, bias, w_out, side_w)
+        + [pltpu.VMEM((n, p.side_rows, LANES), F32), pltpu.VMEM((n, p.side_rows, LANES), BF16),
+           pltpu.SemaphoreType.DMA((p.n_row,))],
+        [SMEM] + [VMEM] * 8, "attend", out_spec=(VMEM, HBM))(at, q, k, v, gate, rest, bias, w_out, side_w)
 
     sides = lax.all_to_all(sides, ALL, 0, 0, tiled=True)
-    mid, edges = call(
+
+    parts = ring(lambda to: lax.dynamic_index_in_dim(emb, to, 0, keepdims=False))
+    home = call(functools.partial(home_kernel, p), sds(x.shape, BF16),
+                [pltpu.VMEM((p.n_col, p.own, p.per * p.half, p.feat), F32)],
+                [SMEM] + [VMEM] * p.n_col, "home")(at, *parts)
+
+    mid, edges, out_gate = call(
         functools.partial(outer_kernel, p),
-        (sds((p.rows, p.cols, width), BF16), sds((n, p.edge_rows, LANES), BF16)),
+        (sds((p.rows, p.cols, width), BF16), sds((n, p.edge_rows, LANES), BF16),
+         sds((p.rows * p.cols, width), F32)),
         [pltpu.VMEM((n * p.side_rows, LANES), F32),
          pltpu.VMEM((p.rk * LANES, p.seq_total), F32),
          pltpu.VMEM((p.rows * p.cpad, p.outer * p.outer), BF16),
          pltpu.VMEM(((p.ig - 1) * p.q * p.cols + LANES, LANES), F32)],
-        [VMEM] * 5, "outer")(sides, pair, by_d, value_w, gate_w)
-
+        [VMEM] * 6, "outer")(sides, pair, by_d, value_w, gate_w, own_gate_w)
+
+    edges, home = lax.optimization_barrier((edges, home))
     edges = lax.all_to_all(edges, ALL, 0, 0, tiled=True)
-    out_gate = call(functools.partial(gate_kernel, p), sds((p.rows * p.cols, width), F32), [], [VMEM] * 2, "gate")(
-        mid, own_gate_w)
     n_lane = p.j_base(p.n_col - 1) // LANES + 1
     back = call(
-        functools.partial(triangle_kernel, p), sds((n, p.back_rows, LANES), BF16),
+        functools.partial(triangle_kernel, p), sds((n, p.ig, ch, LANES), BF16),
         [pltpu.VMEM((p.n_col, p.n_row * p.edge_rows, LANES), F32),
          pltpu.VMEM((ch, p.n_col, p.m * p.q, LANES), F32),
          pltpu.VMEM((ch, p.n_col, n_lane * LANES, LANES), F32),
@@ -484,17 +512,13 @@
          pltpu.VMEM((p.n_col, p.m * ch, LANES), F32)],
         [VMEM], "triangle")(edges)
 
-    parts = ring(lambda to: lax.dynamic_index_in_dim(emb, to, 0, keepdims=False))
-    home = call(functools.partial(home_kernel, p), sds(x.shape, BF16),
-                [pltpu.VMEM((p.n_col, p.own, p.per * p.half, p.feat), F32)],
-                [SMEM] + [VMEM] * p.n_col, "home")(at, *parts)
-
     back = lax.all_to_all(back, ALL, 0, 0, tiled=True)
     state = call(
         functools.partial(final_kernel, p), sds((p.rows, p.cols, width), BF16),
-        [pltpu.VMEM((n * p.back_rows, LANES), F32), pltpu.VMEM((LANES, LANES), F32),
-         pltpu.VMEM((p.rows * p.cols, LANES), F32)],
-        [VMEM] * 4, "final")(back, mid, out_gate, last_w)
+        [pltpu.VMEM((p.ig, width, LANES), F32), pltpu.VMEM((p.ig, LANES, LANES), F32),
+         pltpu.VMEM((p.rows * p.cols, LANES), F32), pltpu.VMEM((p.rows, p.cols, width), BF16),
+         pltpu.SemaphoreType.DMA((p.ig,))],
+        [VMEM] * 4, "final", out_spec=HBM)(back, mid, out_gate, w_last)
     return home, state
 
 

time: 75.1 us -> 73.1 us (0.973)
  blocking collectives: 16.6 us -> 29.1 us
  waiting for transfers between devices: 20.5 us -> 11.2 us
  starting transfers between devices: 20.5 us -> 17.7 us
  local copies, waits for them, and re-layouts: 3.95 us -> 1.58 us
    all_to_all x0 -> x1, blocking collectives: none -> 12.4 us  [fast(): back = lax.all_to_all(back, ALL, 0, 0, tiled=True)]
    all_to_all x1, waiting for transfers between devices: 9.39 us -> 3.43 us  [fast(): sides = lax.all_to_all(sides, ALL, 0, 0, tiled=True)]
    all_to_all x1 -> x0, waiting for transfers between devices: 3.47 us -> none  [fast(): back = lax.all_to_all(back, ALL, 0, 0, tiled=True)]
    all_to_all x1 -> x0, starting transfers between devices: 2.75 us -> none  [fast(): back = lax.all_to_all(back, ALL, 0, 0, tiled=True)]
    unnamed x22 -> x18, local copies, waits for them, and re-layouts: 3.49 us -> 1.11 us
    pallas_call x1, Pallas kernels: 1.4 us -> 2.58 us  [fast(): call(functools.partial(bias_kernel, p), sds((n, p.bias_rows, LANES), BF16...]
    pallas_call x2 -> x1, Pallas kernels: 2.23 us -> 1.1 us  [fast(): call(functools.partial(triangle_kernel, p), sds((n, p.ig, ch, LANES), BF1...]
  transfers between devices with their start and end apart: 9 -> 8, of which waited for: 8 -> 7; matrix products, arithmetic and copies ran while one was open for 1% -> 1% of each run, Pallas kernels for 3% -> 2%
where the time goes in v4:
time: 73.1 us; the launch traced here: 72.7 us
  blocking collectives  29.1 us (40%)
  starting transfers between devices  17.7 us (24%)
  Pallas kernels  12.1 us (17%)
  waiting for transfers between devices  11.2 us (15%)
  local copies, waits for them, and re-layouts  1.58 us (2%)
  between operations  0.96 us (1%)
    all_to_all x1, blocking collectives, fast(): edges = lax.all_to_all(edges, ALL, 0, 0, tiled=True)  16.8 us
    all_to_all x1, blocking collectives, fast(): back = lax.all_to_all(back, ALL, 0, 0, tiled=True)  12.4 us
    all_to_all x1, starting transfers between devices, fast(): bias = lax.all_to_all(piece, ALL, 0, 0, tiled=True)  7.33 us
    ppermute x6, starting transfers between devices, ring(): lax.ppermute(part, 'col', [(c, (c + shift) % p.n_col) for c in range(p.n_...  6.57 us
    ppermute x6, waiting for transfers between devices, ring(): lax.ppermute(part, 'col', [(c, (c + shift) % p.n_col) for c in range(p.n_...  6.2 us
    all_to_all x1, starting transfers between devices, fast(): sides = lax.all_to_all(sides, ALL, 0, 0, tiled=True)  3.82 us
    all_to_all x1, waiting for transfers between devices, fast(): sides = lax.all_to_all(sides, ALL, 0, 0, tiled=True)  3.43 us
    pallas_call x1, Pallas kernels, fast(): call(functools.partial(attend_kernel, p), (sds((p.n_col, p.own, p.per * p...  3.24 us
  transfers between devices with their start and end apart: 8, of which 7 were waited for; matrix products, arithmetic and copies ran while one was open for 1% of the time, Pallas kernels for 2%

profile of v4, /device:TPU:0, one launch (start us, length us, event | category | flops | bytes accessed | tf_op | source)
XLA Modules:
  0.0 72.7 jit_solution(18176888263486007625)
XLA Ops:
  0.6 2.6 %bias.1 = bf16[32,32,128]{2,1,0:T(8,128)(2,1)} custom-call(bf16[20,40,128]{2,1,0:T(8,128)(2,1)} %pair_ref.1, bf16[8,128]{1,0:T(8,128)(2,1)} %bitcast.42), custom_call_target="tpu_custom_call" | custom-call | flops 400000000 | bytes 4000000 | tf_op jit(solution)/shard_map/bias/pallas_call | solution.py:454
  3.2 7.3 %all-to-all-start = ((bf16[32,32,128]{2,1,0:T(8,128)(2,1)}), bf16[32,32,128]{2,1,0:T(8,128)(2,1)S(1)}, u32[]{:S(2)}, u32[]{:S(2)}) async-start(bf16[32,32,128]{2,1,0:T(8,128)(2,1)} %bias.1), calls=%async_computation | async-start | bytes 524288 | tf_op jit(solution)/shard_map/all_to_all | solution.py:458
  10.7 0.8 %copy-done.4 = bf16[8,40,256]{2,1,0:T(8,128)(2,1)S(1)} copy-done((bf16[8,40,256]{2,1,0:T(8,128)(2,1)S(1)}, bf16[8,40,256]{2,1,0:T(8,128)(2,1)}, u32[]{:S(2)}) %copy-start.4) | copy-done | bytes 163864
  11.5 0.3 collective-permute-start
  11.8 1.6 %collective-permute-start.1 = (bf16[4,40,256]{2,1,0:T(8,128)(2,1)S(1)}, bf16[4,40,256]{2,1,0:T(8,128)(2,1)S(1)}, u32[]{:S(2)}, u32[]{:S(2)}) collective-permute-start(bf16[4,40,256]{2,1,0:T(8,128)(2,1)S(1)} %get-tuple-element.35), channel_id=1, source_target_pairs={{0,2},{1,3},{2,0},{3,1},{4,6},{5,7},{6,4},{7,5},{8,10},{9,11},{10,... | collective-permute-start | bytes 245768 | tf_op jit(solution)/shard_map/ppermute | solution.py:464
  13.5 1.4 %collective-permute-start.2 = (bf16[4,40,256]{2,1,0:T(8,128)(2,1)S(1)}, bf16[4,40,256]{2,1,0:T(8,128)(2,1)S(1)}, u32[]{:S(2)}, u32[]{:S(2)}) collective-permute-start(bf16[4,40,256]{2,1,0:T(8,128)(2,1)S(1)} %get-tuple-element.34), channel_id=1, source_target_pairs={{0,3},{1,0},{2,1},{3,2},{4,7},{5,4},{6,5},{7,6},{8,11},{9,8},{10,9... | collective-permute-start | bytes 245768 | tf_op jit(solution)/shard_map/ppermute | solution.py:464
  15.2 1.9 %collective-permute-done.refs_1_ = bf16[4,40,256]{2,1,0:T(8,128)(2,1)S(1)} collective-permute-done((bf16[4,40,256]{2,1,0:T(8,128)(2,1)S(1)}, bf16[4,40,256]{2,1,0:T(8,128)(2,1)S(1)}, u32[]{:S(2)}, u32[]{:S(2)}) %collective-permute-start) | collective-permute-done | bytes 81952 | tf_op jit(solution)/shard_map/ppermute | solution.py:464
  17.1 1.0 %collective-permute-done.1.refs_2_ = bf16[4,40,256]{2,1,0:T(8,128)(2,1)S(1)} collective-permute-done((bf16[4,40,256]{2,1,0:T(8,128)(2,1)S(1)}, bf16[4,40,256]{2,1,0:T(8,128)(2,1)S(1)}, u32[]{:S(2)}, u32[]{:S(2)}) %collective-permute-start.1) | collective-permute-done | bytes 81952 | tf_op jit(solution)/shard_map/ppermute | solution.py:464
  18.1 0.6 collective-permute-done.2.refs_3_
  18.8 0.8 %project.1 = (bf16[4,96,256]{2,1,0:T(8,128)(2,1)S(1)}, bf16[4,160,256]{2,1,0:T(8,128)(2,1)S(1)}, bf16[4,160,256]{2,1,0:T(8,128)(2,1)S(1)}, f32[4,96,256]{2,1,0:T(8,128)S(1)}, bf16[4,96,256]{2,1,0:T(8,128)(2,1)S(1)}) custom-call(s32[1]{0:T(128)} %bitcast.col_ref, bf16[4,40,256]{2,1,0:T(8,128)(2,1)S(1)} %get-tuple-element.37.refs_0_, ...), custom_call_target="tpu_custom_call" | custom-call | flops 400000000 | bytes 4000000 | tf_op jit(solution)/shard_map/project/pallas_call | solution.py:472
  19.6 1.5 %all-to-all-done.bias_ref = bf16[32,32,128]{2,1,0:T(8,128)(2,1)S(1)} async-done(((bf16[32,32,128]{2,1,0:T(8,128)(2,1)}), bf16[32,32,128]{2,1,0:T(8,128)(2,1)S(1)}, u32[]{:S(2)}, u32[]{:S(2)}) %all-to-all-start) | async-done | bytes 262176 | tf_op jit(solution)/shard_map/all_to_all | solution.py:458
  21.1 3.2 %attend.1 = (bf16[4,4,24,256]{3,2,1,0:T(8,128)(2,1)S(1)}, bf16[32,32,128]{2,1,0:T(8,128)(2,1)}) custom-call(s32[1]{0:T(128)} %bitcast.col_ref, bf16[4,96,256]{2,1,0:T(8,128)(2,1)S(1)} %get-tuple-element.14.q_ref, bf16[4,160,256]{2,1,0:T(8,128)(2,1)S(1)} %get-tuple-element.15.k_ref, bf16[4,160,256]{2,1,0:T(8,128)(2,1)S(1)} %get-tuple-element.16.v_ref, ...), custom_call_target="tpu_custom_call" | custom-call | flops 400000000 | bytes 4000000 | tf_op jit(solution)/shard_map/attend/pallas_call | solution.py:477
  24.4 3.8 %all-to-all-start.1 = ((bf16[32,32,128]{2,1,0:T(8,128)(2,1)}), bf16[32,32,128]{2,1,0:T(8,128)(2,1)S(1)}, u32[]{:S(2)}, u32[]{:S(2)}) async-start(bf16[32,32,128]{2,1,0:T(8,128)(2,1)} %get-tuple-element.19), calls=%async_computation.1 | async-start | bytes 524288 | tf_op jit(solution)/shard_map/all_to_all | solution.py:486
  28.8 1.6 %collective-permute-start.4 = (bf16[4,24,256]{2,1,0:T(8,128)(2,1)S(1)}, bf16[4,24,256]{2,1,0:T(8,128)(2,1)S(1)}, u32[]{:S(2)}, u32[]{:S(2)}) collective-permute-start(bf16[4,24,256]{2,1,0:T(8,128)(2,1)S(1)} %get-tuple-element.27), channel_id=1, source_target_pairs={{0,2},{1,3},{2,0},{3,1},{4,6},{5,7},{6,4},{7,5},{8,10},{9,11},{10,... | collective-permute-start | bytes 147464 | tf_op jit(solution)/shard_map/ppermute | solution.py:464
  30.4 1.4 %collective-permute-start.5 = (bf16[4,24,256]{2,1,0:T(8,128)(2,1)S(1)}, bf16[4,24,256]{2,1,0:T(8,128)(2,1)S(1)}, u32[]{:S(2)}, u32[]{:S(2)}) collective-permute-start(bf16[4,24,256]{2,1,0:T(8,128)(2,1)S(1)} %get-tuple-element.26), channel_id=1, source_target_pairs={{0,3},{1,0},{2,1},{3,2},{4,7},{5,4},{6,5},{7,6},{8,11},{9,8},{10,9... | collective-permute-start | bytes 147464 | tf_op jit(solution)/shard_map/ppermute | solution.py:464
  32.0 1.0 %collective-permute-done.3.refs_1_ = bf16[4,24,256]{2,1,0:T(8,128)(2,1)S(1)} collective-permute-done((bf16[4,24,256]{2,1,0:T(8,128)(2,1)S(1)}, bf16[4,24,256]{2,1,0:T(8,128)(2,1)S(1)}, u32[]{:S(2)}, u32[]{:S(2)}) %collective-permute-start.3) | collective-permute-done | bytes 49184 | tf_op jit(solution)/shard_map/ppermute | solution.py:464
  33.0 1.6 %collective-permute-done.4.refs_2_ = bf16[4,24,256]{2,1,0:T(8,128)(2,1)S(1)} collective-permute-done((bf16[4,24,256]{2,1,0:T(8,128)(2,1)S(1)}, bf16[4,24,256]{2,1,0:T(8,128)(2,1)S(1)}, u32[]{:S(2)}, u32[]{:S(2)}) %collective-permute-start.4) | collective-permute-done | bytes 49184 | tf_op jit(solution)/shard_map/ppermute | solution.py:464
  34.6 0.7 home.1
  35.4 3.4 %all-to-all-done.1.recv_ref = bf16[32,32,128]{2,1,0:T(8,128)(2,1)S(1)} async-done(((bf16[32,32,128]{2,1,0:T(8,128)(2,1)}), bf16[32,32,128]{2,1,0:T(8,128)(2,1)S(1)}, u32[]{:S(2)}, u32[]{:S(2)}) %all-to-all-start.1) | async-done | bytes 262176 | tf_op jit(solution)/shard_map/all_to_all | solution.py:486
  38.8 2.5 %outer.1 = (bf16[20,40,128]{2,1,0:T(8,128)(2,1)S(1)}, bf16[32,56,128]{2,1,0:T(8,128)(2,1)S(1)}, f32[800,128]{1,0:T(8,128)S(1)}) custom-call(bf16[32,32,128]{2,1,0:T(8,128)(2,1)S(1)} %all-to-all-done.1.recv_ref, bf16[20,40,128]{2,1,0:T(8,128)(2,1)S(1)} %copy-done.2, bf16[1024,128]{1,0:T(8,128)(2,1)S(1)} %bitcast.34, ...), custom_call_target="tpu_custom_call" | custom-call | flops 400000000 | bytes 4000000 | tf_op jit(solution)/shard_map/outer/pallas_call | solution.py:493
  41.3 16.8 %all_to_all.20.recv_ref = bf16[32,56,128]{2,1,0:T(8,128)(2,1)S(1)} all-to-all(bf16[32,56,128]{2,1,0:T(8,128)(2,1)S(1)} %get-tuple-element.23), channel_id=1, replica_groups=mesh['row'=8,'col'=4] {'row','col'}, dimensions={0} | all-to-all | bytes 917504 | tf_op jit(solution)/shard_map/all_to_all | solution.py:504
  58.1 1.1 %triangle.1 = bf16[32,7,4,128]{3,2,1,0:T(4,128)(2,1)S(1)} custom-call(bf16[32,56,128]{2,1,0:T(8,128)(2,1)S(1)} %all_to_all.20.recv_ref), custom_call_target="tpu_custom_call" | custom-call | flops 400000000 | bytes 4000000 | tf_op jit(solution)/shard_map/triangle/pallas_call | solution.py:506
  59.2 12.4 %all_to_all.21.recv_ref = bf16[32,7,4,128]{3,2,1,0:T(4,128)(2,1)S(1)} all-to-all(bf16[32,7,4,128]{3,2,1,0:T(4,128)(2,1)S(1)} %triangle.1), channel_id=1, replica_groups=mesh['row'=8,'col'=4] {'row','col'}, dimensions={0} | all-to-all | bytes 458752 | tf_op jit(solution)/shard_map/all_to_all | solution.py:515
  71.6 1.1 %final.1 = bf16[20,40,128]{2,1,0:T(8,128)(2,1)} custom-call(bf16[32,7,4,128]{3,2,1,0:T(4,128)(2,1)S(1)} %all_to_all.21.recv_ref, bf16[20,40,128]{2,1,0:T(8,128)(2,1)S(1)} %get-tuple-element.24.mid_ref, f32[800,128]{1,0:T(8,128)S(1)} %get-tuple-element.25.gate_ref, bf16[128,128]{1,0:T(8,128)(2,1)S(1)} %copy-done.3), custom_call_target="tpu_custom_call" | custom-call | flops 400000000 | bytes 4000000 | tf_op jit(solution)/shard_map/final/pallas_call | solution.py:516
  (27 shorter events, 1.2 us)
Async XLA Ops:
  3.2 17.9 %all-to-all-start = ((bf16[32,32,128]{2,1,0:T(8,128)(2,1)}), bf16[32,32,128]{2,1,0:T(8,128)(2,1)S(1)}, u32[]{:S(2)}, u32[]{:S(2)}) async-start(bf16[32,32,128]{2,1,0:T(8,128)(2,1)} %bias.1), calls=%async_computation | async-start | bytes 524288 | tf_op jit(solution)/shard_map/all_to_all | solution.py:458
  10.6 0.9 %copy-start.4 = (bf16[8,40,256]{2,1,0:T(8,128)(2,1)S(1)}, bf16[8,40,256]{2,1,0:T(8,128)(2,1)}, u32[]{:S(2)}) copy-start(bf16[8,40,256]{2,1,0:T(8,128)(2,1)} %param.9) | copy-start | bytes 491524
  11.5 3.3 %copy-start.7 = (bf16[256,64]{0,1:T(8,128)(2,1)S(1)}, bf16[256,64]{0,1:T(8,128)(2,1)}, u32[]{:S(2)}) copy-start(bf16[256,64]{0,1:T(8,128)(2,1)} %param.14) | copy-start | bytes 98308
  11.5 7.3 %copy-start.1 = (bf16[256,1024]{1,0:T(8,128)(2,1)S(1)}, bf16[256,1024]{1,0:T(8,128)(2,1)}, u32[]{:S(2)}) copy-start(bf16[256,1024]{1,0:T(8,128)(2,1)} %refs_4_.1) | copy-start | bytes 1572868
  11.5 5.6 %collective-permute-start = (bf16[4,40,256]{2,1,0:T(8,128)(2,1)S(1)}, bf16[4,40,256]{2,1,0:T(8,128)(2,1)S(1)}, u32[]{:S(2)}, u32[]{:S(2)}) collective-permute-start(bf16[4,40,256]{2,1,0:T(8,128)(2,1)S(1)} %get-tuple-element.36), channel_id=1, source_target_pairs={{0,1},{1,2},{2,3},{3,0},{4,5},{5,6},{6,7},{7,4},{8,9},{9,10},{10,1... | collective-permute-start | bytes 245768 | tf_op jit(solution)/shard_map/ppermute | solution.py:464
  11.8 6.3 %collective-permute-start.1 = (bf16[4,40,256]{2,1,0:T(8,128)(2,1)S(1)}, bf16[4,40,256]{2,1,0:T(8,128)(2,1)S(1)}, u32[]{:S(2)}, u32[]{:S(2)}) collective-permute-start(bf16[4,40,256]{2,1,0:T(8,128)(2,1)S(1)} %get-tuple-element.35), channel_id=1, source_target_pairs={{0,2},{1,3},{2,0},{3,1},{4,6},{5,7},{6,4},{7,5},{8,10},{9,11},{10,... | collective-permute-start | bytes 245768 | tf_op jit(solution)/shard_map/ppermute | solution.py:464
  13.5 5.3 %collective-permute-start.2 = (bf16[4,40,256]{2,1,0:T(8,128)(2,1)S(1)}, bf16[4,40,256]{2,1,0:T(8,128)(2,1)S(1)}, u32[]{:S(2)}, u32[]{:S(2)}) collective-permute-start(bf16[4,40,256]{2,1,0:T(8,128)(2,1)S(1)} %get-tuple-element.34), channel_id=1, source_target_pairs={{0,3},{1,0},{2,1},{3,2},{4,7},{5,4},{6,5},{7,6},{8,11},{9,8},{10,9... | collective-permute-start | bytes 245768 | tf_op jit(solution)/shard_map/ppermute | solution.py:464
  18.8 2.3 %copy-start = (bf16[256,256]{1,0:T(8,128)(2,1)S(1)}, bf16[256,256]{1,0:T(8,128)(2,1)}, u32[]{:S(2)}) copy-start(bf16[256,256]{1,0:T(8,128)(2,1)} %wf_ref.1) | copy-start | bytes 393220
  24.4 3.9 %copy-start.6 = (bf16[128,640]{1,0:T(8,128)(2,1)S(1)}, bf16[128,640]{1,0:T(8,128)(2,1)}, u32[]{:S(2)}) copy-start(bf16[128,640]{1,0:T(8,128)(2,1)} %param.16) | copy-start | bytes 491524
  24.4 14.4 %all-to-all-start.1 = ((bf16[32,32,128]{2,1,0:T(8,128)(2,1)}), bf16[32,32,128]{2,1,0:T(8,128)(2,1)S(1)}, u32[]{:S(2)}, u32[]{:S(2)}) async-start(bf16[32,32,128]{2,1,0:T(8,128)(2,1)} %get-tuple-element.19), calls=%async_computation.1 | async-start | bytes 524288 | tf_op jit(solution)/shard_map/all_to_all | solution.py:486
  28.5 3.4 %copy-start.5 = (bf16[1024,128]{1,0:T(8,128)(2,1)S(1)}, bf16[1024,128]{1,0:T(8,128)(2,1)}, u32[]{:S(2)}) copy-start(bf16[1024,128]{1,0:T(8,128)(2,1)} %param.15) | copy-start | bytes 786436
  28.5 4.5 %collective-permute-start.3 = (bf16[4,24,256]{2,1,0:T(8,128)(2,1)S(1)}, bf16[4,24,256]{2,1,0:T(8,128)(2,1)S(1)}, u32[]{:S(2)}, u32[]{:S(2)}) collective-permute-start(bf16[4,24,256]{2,1,0:T(8,128)(2,1)S(1)} %get-tuple-element.28), channel_id=1, source_target_pairs={{0,1},{1,2},{2,3},{3,0},{4,5},{5,6},{6,7},{7,4},{8,9},{9,10},{10,1... | collective-permute-start | bytes 147464 | tf_op jit(solution)/shard_map/ppermute | solution.py:464
  28.8 5.8 %collective-permute-start.4 = (bf16[4,24,256]{2,1,0:T(8,128)(2,1)S(1)}, bf16[4,24,256]{2,1,0:T(8,128)(2,1)S(1)}, u32[]{:S(2)}, u32[]{:S(2)}) collective-permute-start(bf16[4,24,256]{2,1,0:T(8,128)(2,1)S(1)} %get-tuple-element.27), channel_id=1, source_target_pairs={{0,2},{1,3},{2,0},{3,1},{4,6},{5,7},{6,4},{7,5},{8,10},{9,11},{10,... | collective-permute-start | bytes 147464 | tf_op jit(solution)/shard_map/ppermute | solution.py:464
  30.4 4.2 %collective-permute-start.5 = (bf16[4,24,256]{2,1,0:T(8,128)(2,1)S(1)}, bf16[4,24,256]{2,1,0:T(8,128)(2,1)S(1)}, u32[]{:S(2)}, u32[]{:S(2)}) collective-permute-start(bf16[4,24,256]{2,1,0:T(8,128)(2,1)S(1)} %get-tuple-element.26), channel_id=1, source_target_pairs={{0,3},{1,0},{2,1},{3,2},{4,7},{5,4},{6,5},{7,6},{8,11},{9,8},{10,9... | collective-permute-start | bytes 147464 | tf_op jit(solution)/shard_map/ppermute | solution.py:464
  34.6 4.2 %copy-start.2 = (bf16[20,40,128]{2,1,0:T(8,128)(2,1)S(1)}, bf16[20,40,128]{2,1,0:T(8,128)(2,1)}, u32[]{:S(2)}) copy-start(bf16[20,40,128]{2,1,0:T(8,128)(2,1)} %pair_ref.1) | copy-start | bytes 614404
  59.2 12.4 %copy-start.3 = (bf16[128,128]{1,0:T(8,128)(2,1)S(1)}, bf16[128,128]{1,0:T(8,128)(2,1)}, u32[]{:S(2)}) copy-start(bf16[128,128]{1,0:T(8,128)(2,1)} %w_ref.1) | copy-start | bytes 98308

commit v5 on v4

--- a/solution.py
+++ b/solution.py
@@ -95,14 +95,14 @@
         self.queries = n_row * self.half
         self.i_main = LANES // heads // 2
         self.i_rem = self.half - self.i_main
-        if not 0 < self.i_rem or self.i_main % self.pack or self.i_rem % self.pack or LANES % (self.i_rem * heads) or self.cols % SUBLANES:
+        if self.i_main != SUBLANES or 2 * self.i_rem != SUBLANES or self.i_main % self.pack or self.i_rem % self.pack or LANES % (self.i_rem * heads) or self.cols % SUBLANES:
             return
         self.km = self.i_main // self.pack
         self.main, self.rem = self.i_main * heads, self.i_rem * heads
         self.groups = self.cols // SUBLANES
         self.tall = -(-self.groups // 2)
         self.fold = LANES // self.rem
-        if n_row % 2 or n_row % self.fold:
+        if n_row % 2 or n_row % self.fold or n_row * self.main % (2 * LANES) or n_row * self.rem % (2 * LANES):
             return
         self.main_at = [(g % self.tall, g // self.tall * self.main) for g in range(self.groups)]
         spare = [(self.tall, f * self.rem) for f in range(self.fold)]
@@ -140,21 +140,31 @@
         return (c // self.q) * LANES + (c % self.q) * self.jslot
 
 
-def bias_kernel(p, pair_hbm, w_hbm, out_hbm, pair_ref, w_ref, piece_ref, sems, out_sems):
-    copies = [pltpu.make_async_copy(pair_hbm, pair_ref, sems.at[0]), pltpu.make_async_copy(w_hbm, w_ref, sems.at[1])]
+def bias_kernel(p, col_ref, pair_hbm, w_hbm, x_hbm, *refs):
+    out_hbm, *part_hbm = refs[:p.n_col + 1]
+    pair_ref, w_ref, x_ref, piece_ref, sems, out_sems, part_sems = refs[p.n_col + 1:]
+    copies = [pltpu.make_async_copy(pair_hbm, pair_ref, sems.at[0]), pltpu.make_async_copy(w_hbm, w_ref, sems.at[1]),
+              pltpu.make_async_copy(x_hbm, x_ref, sems.at[2])]
     for copy in copies:
         copy.start()
     for copy in copies:
         copy.wait()
+    parts = []
+    for shift in range(p.n_col):
+        group = over(lax.rem(col_ref[0] + shift, p.n_col), p.split)
+        parts.append(pltpu.make_async_copy(x_ref.at[group], part_hbm[shift], part_sems.at[shift]))
+        parts[-1].start()
     normed = standardize_features(pair_ref[...]).reshape(p.rows * p.cols, p.width)
     heads = p.heads
-    spread = modulo(lane_iota(heads), heads) == row_iota(heads)
-    tiled = lax.dot_general(w_ref[...], jnp.where(spread, 1.0, 0.0).astype(BF16), (((0,), (0,)), ((), ())),
-                            preferred_element_type=F32)
-    slot = over(lane_iota(p.width), heads)
-    main_slot, rem_slot = modulo(slot, p.i_main), modulo(slot, p.i_rem)
+
+    def tile(many):
+        spread = modulo(over(lane_iota(heads), many), heads) == row_iota(heads)
+        return lax.dot_general(w_ref[...], jnp.where(spread, 1.0, 0.0).astype(BF16), (((0,), (0,)), ((), ())),
+                               preferred_element_type=F32)
+
+    main_w, rem_w = tile(p.i_main), tile(p.i_rem)
+    main_slot, rem_slot = modulo(lane_iota(p.width), p.i_main), modulo(lane_iota(p.width), p.i_rem)
     at = lane_iota(SUBLANES)
-    pieces = []
     for h in range(p.split):
         main = jnp.zeros((p.cols, LANES), F32)
         rem = jnp.zeros((p.cols, LANES), F32)
@@ -162,20 +172,22 @@
             i = h * p.late + m
             block = normed[i * p.cols:(i + 1) * p.cols].astype(BF16)
             if m < p.i_main:
-                main += dot(block, jnp.where(main_slot == m, tiled, 0.0).astype(BF16))
+                main += dot(block, jnp.where(main_slot == m, main_w, 0.0).astype(BF16))
             else:
-                rem += dot(block, jnp.where(rem_slot == m - p.i_main, tiled, 0.0).astype(BF16))
+                rem += dot(block, jnp.where(rem_slot == m - p.i_main, rem_w, 0.0).astype(BF16))
         blocks = [jnp.zeros((SUBLANES, LANES), F32) for _ in range(p.tall + 1)]
         for value, places, wide in ((main, p.main_at, p.main), (rem, p.rem_at, p.rem)):
             for g, (b, lane) in enumerate(places):
                 here = (at >= lane) & (at < lane + wide)
                 blocks[b] = jnp.where(here, value[g * SUBLANES:(g + 1) * SUBLANES], blocks[b])
-        piece_ref[h] = jnp.concatenate(blocks, axis=0).astype(BF16)
-        for d in range(p.n):
-            if d % p.n_col % p.split == h:
-                pieces.append(pltpu.make_async_copy(piece_ref.at[h], out_hbm.at[d], out_sems.at[d]))
-                pieces[-1].start()
+        piece = jnp.concatenate(blocks, axis=0).astype(BF16)
+        for c in range(h, p.n_col, p.split):
+            piece_ref[c] = piece
+    pieces = [pltpu.make_async_copy(piece_ref, out_hbm.at[pl.ds(r * p.n_col, p.n_col)], out_sems.at[r])
+              for r in range(p.n_row)]
     for copy in pieces:
+        copy.start()
+    for copy in pieces + parts:
         copy.wait()
 
 
@@ -227,22 +239,44 @@
                         built = piece if u == 0 else jnp.where(slot == u, piece, built)
                     row = c * p.cols + g * SUBLANES
                     bias[row:row + SUBLANES, first + b * LANES:first + (b + 1) * LANES] = built
-    wide = t * h
-    own_head = over(row_iota(f, wide), p.hd) == modulo(lane_iota(f, wide), h)
-    pick = jnp.where(over(lane_iota(t, wide), h) == row_iota(t, wide), 1.0, 0.0).astype(BF16)
-    head_mask = jnp.where(over(lane_iota(h, f), p.hd) == row_iota(h, f), 1.0, 0.0)
-    new = []
-    for s in range(p.own):
-        q = q_ref[s].astype(F32)
-        spread = (jnp.broadcast_to(q[:, None, :], (t, h, f)) * head_mask[None]).reshape(wide, f).astype(BF16)
-        scores = dot_nt(k_ref[s], spread) + bias[...]
-        peak = jnp.max(scores, axis=0, keepdims=True)
-        weights = jnp.exp(scores - peak)
-        total = jnp.sum(weights, axis=0, keepdims=True)
-        v_t = jnp.transpose(v_ref[s].astype(F32)).astype(BF16)
-        mixed = dot(v_t, weights.astype(BF16)) * (1.0 / total)
-        mixed = jnp.where(own_head, mixed, 0.0).astype(BF16)
-        new.append((gate_ref[s] * dot_nt(pick, mixed)).astype(BF16))
+    step = 2 * LANES
+    lane, row = lane_iota(f, step), row_iota(f, step)
+    blocks = []
+    for many, wide, count in ((p.i_main, p.main, p.n_row * p.main // step), (p.i_rem, p.rem, p.n_row * p.rem // step)):
+        own_head = over(row, p.hd) == modulo(over(lane, many), h)
+        at = lane_iota(step // h, step)
+        pick = jnp.where(row_iota(step // h, step) == over(at, wide) * many + modulo(at, many), 1.0, 0.0).astype(BF16)
+        blocks += [(own_head, pick)] * count
+    head_lane, low = over(lane_iota(SUBLANES, f), p.hd), row_iota(SUBLANES, f) >= p.i_rem
+    own_lane = [jnp.where(head_lane == g, 1.0, 0.0) for g in range(h)]
+    own_pair = [jnp.where(low, own_lane[g + 1], own_lane[g]) for g in range(0, h, 2)]
+    new, tall, together = [], step // SUBLANES, 4
+    for first in range(0, p.own, together):
+        jobs = []
+        for s in range(first, min(first + together, p.own)):
+            q = q_ref[s].astype(F32)
+            spread = []
+            for r in range(p.n_row):
+                rows = q[r * p.i_main:(r + 1) * p.i_main]
+                spread += [rows * mask for mask in own_lane]
+            for r in range(p.n_row):
+                start = p.n_row * p.i_main + r * p.i_rem
+                rows = jnp.concatenate([q[start:start + p.i_rem]] * 2, axis=0)
+                spread += [rows * mask for mask in own_pair]
+            for n in range(len(blocks)):
+                jobs.append((s, n, jnp.concatenate(spread[n * tall:(n + 1) * tall], axis=0).astype(BF16)))
+        v_t = {s: jnp.transpose(v_ref[s].astype(F32)).astype(BF16) for s in range(first, first + together)
+               if s < p.own}
+        scores = [dot_nt(k_ref[s], rows) + bias[:, n * step:(n + 1) * step] for s, n, rows in jobs]
+        weights = [jnp.exp(score - jnp.max(score, axis=0, keepdims=True)) for score in scores]
+        share = [1.0 / jnp.sum(weight, axis=0, keepdims=True) for weight in weights]
+        mixed = [dot(v_t[s], weight.astype(BF16)) for (s, _, _), weight in zip(jobs, weights)]
+        mixed = [jnp.where(blocks[n][0], value * part, 0.0).astype(BF16)
+                 for (_, n, _), value, part in zip(jobs, mixed, share)]
+        attended = [dot_nt(blocks[n][1], value) for (_, n, _), value in zip(jobs, mixed)]
+        for i, at in enumerate(range(0, len(jobs), len(blocks))):
+            rows = jnp.concatenate(attended[at:at + len(blocks)], axis=0)
+            new.append((gate_ref[first + i] * rows).astype(BF16))
     new = dot(jnp.concatenate(new, axis=0), wf_ref[...])
     new = (x_ref[...].astype(F32).reshape(p.own * t, f) + new).astype(BF16).astype(F32)
     a, b = p.per * p.i_main, p.per * p.i_rem
@@ -451,23 +485,22 @@
     gate_w = jnp.concatenate([blocks[1], blocks[3]], axis=1).reshape(n * 2 * ch, width)
     own_gate_w = w_tri[:, 4 * width:]
 
-    piece = call(functools.partial(bias_kernel, p), sds((n, p.bias_rows, LANES), BF16),
-                 [pltpu.VMEM(pair.shape, BF16), pltpu.VMEM((p.heads, width), BF16),
-                  pltpu.VMEM((p.split, p.bias_rows, LANES), BF16), pltpu.SemaphoreType.DMA((2,)),
-                  pltpu.SemaphoreType.DMA((n,))], [HBM] * 2, "bias", limit=64, out_spec=HBM)(pair, w_bias.T)
+    at = col.reshape(1)
+    chunks = (p.own, p.res, p.feat)
+    piece, *parts = call(
+        functools.partial(bias_kernel, p), (sds((n, p.bias_rows, LANES), BF16),) + (sds(chunks, BF16),) * p.n_col,
+        [pltpu.VMEM(pair.shape, BF16), pltpu.VMEM((p.heads, width), BF16), pltpu.VMEM((p.n_group,) + chunks, BF16),
+         pltpu.VMEM((p.n_col, p.bias_rows, LANES), BF16), pltpu.SemaphoreType.DMA((3,)),
+         pltpu.SemaphoreType.DMA((p.n_row,)), pltpu.SemaphoreType.DMA((p.n_col,))],
+        [SMEM] + [HBM] * 3, "bias", limit=64, out_spec=HBM)(at, pair, w_bias.T, x.reshape((p.n_group,) + chunks))
     bias = lax.all_to_all(piece, ALL, 0, 0, tiled=True)
-    def ring(send):
-        parts = []
-        for shift in range(p.n_col):
-            part = send(lax.rem(col + shift, p.n_col))
-            if shift:
-                part = lax.ppermute(part, "col", [(c, (c + shift) % p.n_col) for c in range(p.n_col)])
-            parts.append(part)
-        return parts
-
-    at = col.reshape(1)
-    chunks = x.reshape(p.n_group, p.own, p.res, p.feat)
-    parts = ring(lambda to: lax.dynamic_index_in_dim(chunks, to // p.split, 0, keepdims=False))
+
+    def ring(parts):
+        return [parts[0]] + [
+            lax.ppermute(parts[shift], "col", [(c, (c + shift) % p.n_col) for c in range(p.n_col)])
+            for shift in range(1, p.n_col)]
+
+    parts = ring(parts)
     mine, every = (p.own, p.queries, p.feat), (p.own, p.total, p.feat)
     q, k, v, gate, rest = call(
         functools.partial(project_kernel, p),
@@ -485,7 +518,8 @@
 
     sides = lax.all_to_all(sides, ALL, 0, 0, tiled=True)
 
-    parts = ring(lambda to: lax.dynamic_index_in_dim(emb, to, 0, keepdims=False))
+    parts = ring([lax.dynamic_index_in_dim(emb, lax.rem(col + shift, p.n_col), 0, keepdims=False)
+                  for shift in range(p.n_col)])
     home = call(functools.partial(home_kernel, p), sds(x.shape, BF16),
                 [pltpu.VMEM((p.n_col, p.own, p.per * p.half, p.feat), F32)],
                 [SMEM] + [VMEM] * p.n_col, "home")(at, *parts)

time: 73.1 us -> 72.6 us (level)
  waiting for transfers between devices: 11.2 us -> 12.1 us
  local copies, waits for them, and re-layouts: 1.58 us -> 0.78 us
    unnamed x18 -> x24, local copies, waits for them, and re-layouts: 1.11 us -> 0.34 us
where the time goes in v5:
time: 72.6 us; the launch traced here: 72.3 us
  blocking collectives  29.1 us (40%)
  starting transfers between devices  17.5 us (24%)
  waiting for transfers between devices  12.1 us (17%)
  Pallas kernels  11.9 us (16%)
  between operations  0.89 us (1%)
  local copies, waits for them, and re-layouts  0.78 us (1%)
    all_to_all x1, blocking collectives, fast(): edges = lax.all_to_all(edges, ALL, 0, 0, tiled=True)  16.8 us
    all_to_all x1, blocking collectives, fast(): back = lax.all_to_all(back, ALL, 0, 0, tiled=True)  12.4 us
    all_to_all x1, starting transfers between devices, fast(): bias = lax.all_to_all(piece, ALL, 0, 0, tiled=True)  7.33 us
    ppermute x6, starting transfers between devices, ring(): lax.ppermute(parts[shift], 'col', [(c, (c + shift) % p.n_col) for c in ra...  6.57 us
    ppermute x6, waiting for transfers between devices, ring(): lax.ppermute(parts[shift], 'col', [(c, (c + shift) % p.n_col) for c in ra...  6.45 us
    all_to_all x1, starting transfers between devices, fast(): sides = lax.all_to_all(sides, ALL, 0, 0, tiled=True)  3.56 us
    all_to_all x1, waiting for transfers between devices, fast(): sides = lax.all_to_all(sides, ALL, 0, 0, tiled=True)  3.43 us
    pallas_call x1, Pallas kernels, fast(): call(functools.partial(attend_kernel, p), (sds((p.n_col, p.own, p.per * p...  3.07 us
  transfers between devices with their start and end apart: 8, of which 7 were waited for; matrix products, arithmetic and copies ran while one was open for 1% of the time, Pallas kernels for 2%

profile of v5, /device:TPU:0, one launch (start us, length us, event | category | flops | bytes accessed | tf_op | source)
XLA Modules:
  0.0 72.3 jit_solution(14478914134180144421)
XLA Ops:
  0.6 2.5 %bias.1 = (bf16[32,32,128]{2,1,0:T(8,128)(2,1)}, bf16[4,40,256]{2,1,0:T(8,128)(2,1)}, bf16[4,40,256]{2,1,0:T(8,128)(2,1)}, bf16[4,40,256]{2,1,0:T(8,128)(2,1)}, bf16[4,40,256]{2,1,0:T(8,128)(2,1)}) custom-call(s32[1]{0:T(128)} %bitcast.col_ref, bf16[20,40,128]{2,1,0:T(8,128)(2,1)} %pair_ref.1, bf16[8,128]{1,0:T(8,128)(2,1)} %bitcast.34, ...), custom_call_target="tpu_custom_call" | custom-call | flops 400000000 | bytes 4000000 | tf_op jit(solution)/shard_map/bias/pallas_call | solution.py:490
  3.2 7.3 %all-to-all-start = ((bf16[32,32,128]{2,1,0:T(8,128)(2,1)}), bf16[32,32,128]{2,1,0:T(8,128)(2,1)S(1)}, u32[]{:S(2)}, u32[]{:S(2)}) async-start(bf16[32,32,128]{2,1,0:T(8,128)(2,1)} %get-tuple-element.28), calls=%async_computation | async-start | bytes 524288 | tf_op jit(solution)/shard_map/all_to_all | solution.py:496
  10.6 0.3 collective-permute-start
  10.9 1.6 %collective-permute-start.1 = (bf16[4,40,256]{2,1,0:T(8,128)(2,1)S(1)}, bf16[4,40,256]{2,1,0:T(8,128)(2,1)S(1)}, u32[]{:S(2)}, u32[]{:S(2)}) collective-permute-start(bf16[4,40,256]{2,1,0:T(8,128)(2,1)S(1)} %copy-done.9), channel_id=1, source_target_pairs={{0,2},{1,3},{2,0},{3,1},{4,6},{5,7},{6,4},{7,5},{8,10},{9,11},{10,... | collective-permute-start | bytes 245768 | tf_op jit(solution)/shard_map/ppermute | solution.py:500
  12.5 1.4 %collective-permute-start.2 = (bf16[4,40,256]{2,1,0:T(8,128)(2,1)S(1)}, bf16[4,40,256]{2,1,0:T(8,128)(2,1)S(1)}, u32[]{:S(2)}, u32[]{:S(2)}) collective-permute-start(bf16[4,40,256]{2,1,0:T(8,128)(2,1)S(1)} %copy-done.8), channel_id=1, source_target_pairs={{0,3},{1,0},{2,1},{3,2},{4,7},{5,4},{6,5},{7,6},{8,11},{9,8},{10,9... | collective-permute-start | bytes 245768 | tf_op jit(solution)/shard_map/ppermute | solution.py:500
  14.1 0.2 concatenate.9.ws_ref
  14.3 1.8 %collective-permute-done.refs_1_ = bf16[4,40,256]{2,1,0:T(8,128)(2,1)S(1)} collective-permute-done((bf16[4,40,256]{2,1,0:T(8,128)(2,1)S(1)}, bf16[4,40,256]{2,1,0:T(8,128)(2,1)S(1)}, u32[]{:S(2)}, u32[]{:S(2)}) %collective-permute-start) | collective-permute-done | bytes 81952 | tf_op jit(solution)/shard_map/ppermute | solution.py:500
  16.2 1.8 %collective-permute-done.1.refs_2_ = bf16[4,40,256]{2,1,0:T(8,128)(2,1)S(1)} collective-permute-done((bf16[4,40,256]{2,1,0:T(8,128)(2,1)S(1)}, bf16[4,40,256]{2,1,0:T(8,128)(2,1)S(1)}, u32[]{:S(2)}, u32[]{:S(2)}) %collective-permute-start.1) | collective-permute-done | bytes 81952 | tf_op jit(solution)/shard_map/ppermute | solution.py:500
  18.1 0.8 %project.1 = (bf16[4,96,256]{2,1,0:T(8,128)(2,1)S(1)}, bf16[4,160,256]{2,1,0:T(8,128)(2,1)S(1)}, bf16[4,160,256]{2,1,0:T(8,128)(2,1)S(1)}, f32[4,96,256]{2,1,0:T(8,128)S(1)}, bf16[4,96,256]{2,1,0:T(8,128)(2,1)S(1)}) custom-call(s32[1]{0:T(128)} %bitcast.col_ref, bf16[4,40,256]{2,1,0:T(8,128)(2,1)S(1)} %copy-done.4, ...), custom_call_target="tpu_custom_call" | custom-call | flops 400000000 | bytes 4000000 | tf_op jit(solution)/shard_map/project/pallas_call | solution.py:505
  18.9 2.2 %all-to-all-done.bias_ref = bf16[32,32,128]{2,1,0:T(8,128)(2,1)S(1)} async-done(((bf16[32,32,128]{2,1,0:T(8,128)(2,1)}), bf16[32,32,128]{2,1,0:T(8,128)(2,1)S(1)}, u32[]{:S(2)}, u32[]{:S(2)}) %all-to-all-start) | async-done | bytes 262176 | tf_op jit(solution)/shard_map/all_to_all | solution.py:496
  21.1 3.1 %attend.1 = (bf16[4,4,24,256]{3,2,1,0:T(8,128)(2,1)S(1)}, bf16[32,32,128]{2,1,0:T(8,128)(2,1)}) custom-call(s32[1]{0:T(128)} %bitcast.col_ref, bf16[4,96,256]{2,1,0:T(8,128)(2,1)S(1)} %get-tuple-element.23.q_ref, bf16[4,160,256]{2,1,0:T(8,128)(2,1)S(1)} %get-tuple-element.24.k_ref, bf16[4,160,256]{2,1,0:T(8,128)(2,1)S(1)} %get-tuple-element.25.v_ref, ...), custom_call_target="tpu_custom_call" | custom-call | flops 400000000 | bytes 4000000 | tf_op jit(solution)/shard_map/attend/pallas_call | solution.py:510
  24.2 3.6 %all-to-all-start.1 = ((bf16[32,32,128]{2,1,0:T(8,128)(2,1)}), bf16[32,32,128]{2,1,0:T(8,128)(2,1)S(1)}, u32[]{:S(2)}, u32[]{:S(2)}) async-start(bf16[32,32,128]{2,1,0:T(8,128)(2,1)} %get-tuple-element.29), calls=%async_computation.1 | async-start | bytes 524288 | tf_op jit(solution)/shard_map/all_to_all | solution.py:519
  28.1 0.3 collective-permute-start.3
  28.4 1.6 %collective-permute-start.4 = (bf16[4,24,256]{2,1,0:T(8,128)(2,1)S(1)}, bf16[4,24,256]{2,1,0:T(8,128)(2,1)S(1)}, u32[]{:S(2)}, u32[]{:S(2)}) collective-permute-start(bf16[4,24,256]{2,1,0:T(8,128)(2,1)S(1)} %get-tuple-element.37), channel_id=1, source_target_pairs={{0,2},{1,3},{2,0},{3,1},{4,6},{5,7},{6,4},{7,5},{8,10},{9,11},{10,... | collective-permute-start | bytes 147464 | tf_op jit(solution)/shard_map/ppermute | solution.py:500
  30.0 1.4 %collective-permute-start.5 = (bf16[4,24,256]{2,1,0:T(8,128)(2,1)S(1)}, bf16[4,24,256]{2,1,0:T(8,128)(2,1)S(1)}, u32[]{:S(2)}, u32[]{:S(2)}) collective-permute-start(bf16[4,24,256]{2,1,0:T(8,128)(2,1)S(1)} %get-tuple-element.36), channel_id=1, source_target_pairs={{0,3},{1,0},{2,1},{3,2},{4,7},{5,4},{6,5},{7,6},{8,11},{9,8},{10,9... | collective-permute-start | bytes 147464 | tf_op jit(solution)/shard_map/ppermute | solution.py:500
  31.6 1.0 %collective-permute-done.3.refs_1_ = bf16[4,24,256]{2,1,0:T(8,128)(2,1)S(1)} collective-permute-done((bf16[4,24,256]{2,1,0:T(8,128)(2,1)S(1)}, bf16[4,24,256]{2,1,0:T(8,128)(2,1)S(1)}, u32[]{:S(2)}, u32[]{:S(2)}) %collective-permute-start.3) | collective-permute-done | bytes 49184 | tf_op jit(solution)/shard_map/ppermute | solution.py:500
  32.6 1.6 %collective-permute-done.4.refs_2_ = bf16[4,24,256]{2,1,0:T(8,128)(2,1)S(1)} collective-permute-done((bf16[4,24,256]{2,1,0:T(8,128)(2,1)S(1)}, bf16[4,24,256]{2,1,0:T(8,128)(2,1)S(1)}, u32[]{:S(2)}, u32[]{:S(2)}) %collective-permute-start.4) | collective-permute-done | bytes 49184 | tf_op jit(solution)/shard_map/ppermute | solution.py:500
  34.2 0.7 home.1
  34.9 3.4 %all-to-all-done.1.recv_ref = bf16[32,32,128]{2,1,0:T(8,128)(2,1)S(1)} async-done(((bf16[32,32,128]{2,1,0:T(8,128)(2,1)}), bf16[32,32,128]{2,1,0:T(8,128)(2,1)S(1)}, u32[]{:S(2)}, u32[]{:S(2)}) %all-to-all-start.1) | async-done | bytes 262176 | tf_op jit(solution)/shard_map/all_to_all | solution.py:519
  38.4 2.5 %outer.1 = (bf16[20,40,128]{2,1,0:T(8,128)(2,1)S(1)}, bf16[32,56,128]{2,1,0:T(8,128)(2,1)S(1)}, f32[800,128]{1,0:T(8,128)S(1)}) custom-call(bf16[32,32,128]{2,1,0:T(8,128)(2,1)S(1)} %all-to-all-done.1.recv_ref, bf16[20,40,128]{2,1,0:T(8,128)(2,1)S(1)} %copy-done.2, bf16[1024,128]{1,0:T(8,128)(2,1)S(1)} %bitcast.26, ...), custom_call_target="tpu_custom_call" | custom-call | flops 400000000 | bytes 4000000 | tf_op jit(solution)/shard_map/outer/pallas_call | solution.py:527
  40.9 16.8 %all_to_all.20.recv_ref = bf16[32,56,128]{2,1,0:T(8,128)(2,1)S(1)} all-to-all(bf16[32,56,128]{2,1,0:T(8,128)(2,1)S(1)} %get-tuple-element.33), channel_id=1, replica_groups=mesh['row'=8,'col'=4] {'row','col'}, dimensions={0} | all-to-all | bytes 917504 | tf_op jit(solution)/shard_map/all_to_all | solution.py:538
  57.7 1.1 %triangle.1 = bf16[32,7,4,128]{3,2,1,0:T(4,128)(2,1)S(1)} custom-call(bf16[32,56,128]{2,1,0:T(8,128)(2,1)S(1)} %all_to_all.20.recv_ref), custom_call_target="tpu_custom_call" | custom-call | flops 400000000 | bytes 4000000 | tf_op jit(solution)/shard_map/triangle/pallas_call | solution.py:540
  58.8 12.4 %all_to_all.21.recv_ref = bf16[32,7,4,128]{3,2,1,0:T(4,128)(2,1)S(1)} all-to-all(bf16[32,7,4,128]{3,2,1,0:T(4,128)(2,1)S(1)} %triangle.1), channel_id=1, replica_groups=mesh['row'=8,'col'=4] {'row','col'}, dimensions={0} | all-to-all | bytes 458752 | tf_op jit(solution)/shard_map/all_to_all | solution.py:549
  71.1 1.1 %final.1 = bf16[20,40,128]{2,1,0:T(8,128)(2,1)} custom-call(bf16[32,7,4,128]{3,2,1,0:T(4,128)(2,1)S(1)} %all_to_all.21.recv_ref, bf16[20,40,128]{2,1,0:T(8,128)(2,1)S(1)} %get-tuple-element.34.mid_ref, f32[800,128]{1,0:T(8,128)S(1)} %get-tuple-element.35.gate_ref, bf16[128,128]{1,0:T(8,128)(2,1)S(1)} %copy-done.3), custom_call_target="tpu_custom_call" | custom-call | flops 400000000 | bytes 4000000 | tf_op jit(solution)/shard_map/final/pallas_call | solution.py:550
  (32 shorter events, 0.8 us)
Async XLA Ops:
  3.2 7.4 %copy-start.10 = (bf16[4,40,256]{2,1,0:T(8,128)(2,1)S(1)}, bf16[4,40,256]{2,1,0:T(8,128)(2,1)}, u32[]{:S(2)}) copy-start(bf16[4,40,256]{2,1,0:T(8,128)(2,1)} %get-tuple-element.20) | copy-start | bytes 245764
  3.2 7.7 %copy-start.9 = (bf16[4,40,256]{2,1,0:T(8,128)(2,1)S(1)}, bf16[4,40,256]{2,1,0:T(8,128)(2,1)}, u32[]{:S(2)}) copy-start(bf16[4,40,256]{2,1,0:T(8,128)(2,1)} %get-tuple-element.21) | copy-start | bytes 245764
  3.2 9.3 %copy-start.8 = (bf16[4,40,256]{2,1,0:T(8,128)(2,1)S(1)}, bf16[4,40,256]{2,1,0:T(8,128)(2,1)}, u32[]{:S(2)}) copy-start(bf16[4,40,256]{2,1,0:T(8,128)(2,1)} %get-tuple-element.22) | copy-start | bytes 245764
  3.2 10.7 %copy-start.7 = (bf16[256,64]{0,1:T(8,128)(2,1)S(1)}, bf16[256,64]{0,1:T(8,128)(2,1)}, u32[]{:S(2)}) copy-start(bf16[256,64]{0,1:T(8,128)(2,1)} %param.14) | copy-start | bytes 98308
  3.2 17.9 %all-to-all-start = ((bf16[32,32,128]{2,1,0:T(8,128)(2,1)}), bf16[32,32,128]{2,1,0:T(8,128)(2,1)S(1)}, u32[]{:S(2)}, u32[]{:S(2)}) async-start(bf16[32,32,128]{2,1,0:T(8,128)(2,1)} %get-tuple-element.28), calls=%async_computation | async-start | bytes 524288 | tf_op jit(solution)/shard_map/all_to_all | solution.py:496
  10.6 7.6 %copy-start.1 = (bf16[256,1024]{1,0:T(8,128)(2,1)S(1)}, bf16[256,1024]{1,0:T(8,128)(2,1)}, u32[]{:S(2)}) copy-start(bf16[256,1024]{1,0:T(8,128)(2,1)} %refs_4_.1) | copy-start | bytes 1572868
  10.6 5.6 %collective-permute-start = (bf16[4,40,256]{2,1,0:T(8,128)(2,1)S(1)}, bf16[4,40,256]{2,1,0:T(8,128)(2,1)S(1)}, u32[]{:S(2)}, u32[]{:S(2)}) collective-permute-start(bf16[4,40,256]{2,1,0:T(8,128)(2,1)S(1)} %copy-done.10), channel_id=1, source_target_pairs={{0,1},{1,2},{2,3},{3,0},{4,5},{5,6},{6,7},{7,4},{8,9},{9,10},{10,1... | collective-permute-start | bytes 245768 | tf_op jit(solution)/shard_map/ppermute | solution.py:500
  10.9 7.0 %collective-permute-start.1 = (bf16[4,40,256]{2,1,0:T(8,128)(2,1)S(1)}, bf16[4,40,256]{2,1,0:T(8,128)(2,1)S(1)}, u32[]{:S(2)}, u32[]{:S(2)}) collective-permute-start(bf16[4,40,256]{2,1,0:T(8,128)(2,1)S(1)} %copy-done.9), channel_id=1, source_target_pairs={{0,2},{1,3},{2,0},{3,1},{4,6},{5,7},{6,4},{7,5},{8,10},{9,11},{10,... | collective-permute-start | bytes 245768 | tf_op jit(solution)/shard_map/ppermute | solution.py:500
  12.5 5.6 %collective-permute-start.2 = (bf16[4,40,256]{2,1,0:T(8,128)(2,1)S(1)}, bf16[4,40,256]{2,1,0:T(8,128)(2,1)S(1)}, u32[]{:S(2)}, u32[]{:S(2)}) collective-permute-start(bf16[4,40,256]{2,1,0:T(8,128)(2,1)S(1)} %copy-done.8), channel_id=1, source_target_pairs={{0,3},{1,0},{2,1},{3,2},{4,7},{5,4},{6,5},{7,6},{8,11},{9,8},{10,9... | collective-permute-start | bytes 245768 | tf_op jit(solution)/shard_map/ppermute | solution.py:500
  14.1 4.0 %copy-start.4 = (bf16[4,40,256]{2,1,0:T(8,128)(2,1)S(1)}, bf16[4,40,256]{2,1,0:T(8,128)(2,1)}, u32[]{:S(2)}) copy-start(bf16[4,40,256]{2,1,0:T(8,128)(2,1)} %get-tuple-element.19.refs_0_) | copy-start | bytes 245764
  18.1 3.0 %copy-start = (bf16[256,256]{1,0:T(8,128)(2,1)S(1)}, bf16[256,256]{1,0:T(8,128)(2,1)}, u32[]{:S(2)}) copy-start(bf16[256,256]{1,0:T(8,128)(2,1)} %wf_ref.1) | copy-start | bytes 393220
  24.2 3.6 %copy-start.6 = (bf16[128,640]{1,0:T(8,128)(2,1)S(1)}, bf16[128,640]{1,0:T(8,128)(2,1)}, u32[]{:S(2)}) copy-start(bf16[128,640]{1,0:T(8,128)(2,1)} %param.16) | copy-start | bytes 491524
  24.2 14.1 %all-to-all-start.1 = ((bf16[32,32,128]{2,1,0:T(8,128)(2,1)}), bf16[32,32,128]{2,1,0:T(8,128)(2,1)S(1)}, u32[]{:S(2)}, u32[]{:S(2)}) async-start(bf16[32,32,128]{2,1,0:T(8,128)(2,1)} %get-tuple-element.29), calls=%async_computation.1 | async-start | bytes 524288 | tf_op jit(solution)/shard_map/all_to_all | solution.py:519
  28.1 3.4 %copy-start.5 = (bf16[1024,128]{1,0:T(8,128)(2,1)S(1)}, bf16[1024,128]{1,0:T(8,128)(2,1)}, u32[]{:S(2)}) copy-start(bf16[1024,128]{1,0:T(8,128)(2,1)} %param.15) | copy-start | bytes 786436
  28.1 4.5 %collective-permute-start.3 = (bf16[4,24,256]{2,1,0:T(8,128)(2,1)S(1)}, bf16[4,24,256]{2,1,0:T(8,128)(2,1)S(1)}, u32[]{:S(2)}, u32[]{:S(2)}) collective-permute-start(bf16[4,24,256]{2,1,0:T(8,128)(2,1)S(1)} %get-tuple-element.38), channel_id=1, source_target_pairs={{0,1},{1,2},{2,3},{3,0},{4,5},{5,6},{6,7},{7,4},{8,9},{9,10},{10,1... | collective-permute-start | bytes 147464 | tf_op jit(solution)/shard_map/ppermute | solution.py:500
  28.4 5.8 %collective-permute-start.4 = (bf16[4,24,256]{2,1,0:T(8,128)(2,1)S(1)}, bf16[4,24,256]{2,1,0:T(8,128)(2,1)S(1)}, u32[]{:S(2)}, u32[]{:S(2)}) collective-permute-start(bf16[4,24,256]{2,1,0:T(8,128)(2,1)S(1)} %get-tuple-element.37), channel_id=1, source_target_pairs={{0,2},{1,3},{2,0},{3,1},{4,6},{5,7},{6,4},{7,5},{8,10},{9,11},{10,... | collective-permute-start | bytes 147464 | tf_op jit(solution)/shard_map/ppermute | solution.py:500
  30.0 4.2 %collective-permute-start.5 = (bf16[4,24,256]{2,1,0:T(8,128)(2,1)S(1)}, bf16[4,24,256]{2,1,0:T(8,128)(2,1)S(1)}, u32[]{:S(2)}, u32[]{:S(2)}) collective-permute-start(bf16[4,24,256]{2,1,0:T(8,128)(2,1)S(1)} %get-tuple-element.36), channel_id=1, source_target_pairs={{0,3},{1,0},{2,1},{3,2},{4,7},{5,4},{6,5},{7,6},{8,11},{9,8},{10,9... | collective-permute-start | bytes 147464 | tf_op jit(solution)/shard_map/ppermute | solution.py:500
  34.2 4.2 %copy-start.2 = (bf16[20,40,128]{2,1,0:T(8,128)(2,1)S(1)}, bf16[20,40,128]{2,1,0:T(8,128)(2,1)}, u32[]{:S(2)}) copy-start(bf16[20,40,128]{2,1,0:T(8,128)(2,1)} %pair_ref.1) | copy-start | bytes 614404
  58.8 12.4 %copy-start.3 = (bf16[128,128]{1,0:T(8,128)(2,1)S(1)}, bf16[128,128]{1,0:T(8,128)(2,1)}, u32[]{:S(2)}) copy-start(bf16[128,128]{1,0:T(8,128)(2,1)} %w_ref.1) | copy-start | bytes 98308

commit v6 on v5

--- a/solution.py
+++ b/solution.py
@@ -73,7 +73,7 @@
         self.hd = self.feat // heads
         self.total = self.res * n_col
         self.ok = False
-        if any(size & (size - 1) for size in (heads, outer, self.hd, n_row, n_col)):
+        if any(size & (size - 1) for size in (heads, outer, self.hd, n_row, n_col)) or self.hd * 2 > LANES:
             return
         if self.seqs % n_col or self.width != LANES or heads != SUBLANES or self.cols != self.res:
             return
@@ -247,9 +247,16 @@
         at = lane_iota(step // h, step)
         pick = jnp.where(row_iota(step // h, step) == over(at, wide) * many + modulo(at, many), 1.0, 0.0).astype(BF16)
         blocks += [(own_head, pick)] * count
-    head_lane, low = over(lane_iota(SUBLANES, f), p.hd), row_iota(SUBLANES, f) >= p.i_rem
-    own_lane = [jnp.where(head_lane == g, 1.0, 0.0) for g in range(h)]
+    fit = LANES // p.hd
+    head_lane, low = over(lane_iota(SUBLANES), p.hd), row_iota(SUBLANES) >= p.i_rem
+    own_lane = [jnp.where(head_lane == g % fit, 1.0, 0.0) for g in range(h)]
     own_pair = [jnp.where(low, own_lane[g + 1], own_lane[g]) for g in range(0, h, 2)]
+    empty = jnp.zeros((SUBLANES, LANES), F32)
+
+    def only(rows, mask, tile):
+        return jnp.concatenate([rows[:, n * LANES:(n + 1) * LANES] * mask if n == tile else empty
+                                for n in range(f // LANES)], axis=1)
+
     new, tall, together = [], step // SUBLANES, 4
     for first in range(0, p.own, together):
         jobs = []
@@ -258,11 +265,11 @@
             spread = []
             for r in range(p.n_row):
                 rows = q[r * p.i_main:(r + 1) * p.i_main]
-                spread += [rows * mask for mask in own_lane]
+                spread += [only(rows, mask, g // fit) for g, mask in enumerate(own_lane)]
             for r in range(p.n_row):
                 start = p.n_row * p.i_main + r * p.i_rem
                 rows = jnp.concatenate([q[start:start + p.i_rem]] * 2, axis=0)
-                spread += [rows * mask for mask in own_pair]
+                spread += [only(rows, mask, 2 * g // fit) for g, mask in enumerate(own_pair)]
             for n in range(len(blocks)):
                 jobs.append((s, n, jnp.concatenate(spread[n * tall:(n + 1) * tall], axis=0).astype(BF16)))
         v_t = {s: jnp.transpose(v_ref[s].astype(F32)).astype(BF16) for s in range(first, first + together)
@@ -417,10 +424,12 @@
         for c in range(p.n_col):
             left = flat[c, pl.ds(ch, p.m, stride=SUBLANES), :]
             right = flat[c, pl.ds(p.ch + ch, p.m, stride=SUBLANES), :]
+            both = jnp.concatenate([left, right], axis=0).astype(BF16)
             for a in range(p.q):
                 turn = (-a * p.cols) % LANES
-                lt = pltpu.roll(left, turn, axis=1) if turn else left
-                rt = pltpu.roll(right, turn, axis=1) if turn else right
+                turned = pltpu.roll(both, turn, axis=1).astype(F32) if turn else None
+                lt = turned[:p.m] if turn else left
+                rt = turned[p.m:] if turn else right
                 ls[ch, c, pl.ds(a, p.m, stride=p.q), :] = jnp.where(lane < p.cols, lt, 0.0)
                 for first in range(0, p.n_col, p.q):
                     many = min(p.q, p.n_col - first) * blocks
@@ -439,7 +448,7 @@
             packed = None
             for a in range(p.q):
                 turn = ((a - part) * p.jslot) % LANES
-                piece = pltpu.roll(rows[b][a], turn, axis=1) if turn else rows[b][a]
+                piece = pltpu.roll(rows[b][a].astype(BF16), turn, axis=1).astype(F32) if turn else rows[b][a]
                 packed = piece if packed is None else jnp.where(part_of == a, piece, packed)
             sb[c, pl.ds(ch, p.m, stride=p.ch), :] = packed
     for r in range(p.n_row):

time: 72.6 us -> 72.4 us (level)
  no operation moved by 1% of the time
where the time goes in v6:
time: 72.4 us; the launch traced here: 72.1 us
  blocking collectives  29.1 us (40%)
  starting transfers between devices  17.5 us (24%)
  waiting for transfers between devices  12.1 us (17%)
  Pallas kernels  11.7 us (16%)
  between operations  0.88 us (1%)
  local copies, waits for them, and re-layouts  0.78 us (1%)
    all_to_all x1, blocking collectives, fast(): edges = lax.all_to_all(edges, ALL, 0, 0, tiled=True)  16.8 us
    all_to_all x1, blocking collectives, fast(): back = lax.all_to_all(back, ALL, 0, 0, tiled=True)  12.4 us
    all_to_all x1, starting transfers between devices, fast(): bias = lax.all_to_all(piece, ALL, 0, 0, tiled=True)  7.33 us
    ppermute x6, starting transfers between devices, ring(): lax.ppermute(parts[shift], 'col', [(c, (c + shift) % p.n_col) for c in ra...  6.57 us
    ppermute x6, waiting for transfers between devices, ring(): lax.ppermute(parts[shift], 'col', [(c, (c + shift) % p.n_col) for c in ra...  6.45 us
    all_to_all x1, starting transfers between devices, fast(): sides = lax.all_to_all(sides, ALL, 0, 0, tiled=True)  3.56 us
    all_to_all x1, waiting for transfers between devices, fast(): sides = lax.all_to_all(sides, ALL, 0, 0, tiled=True)  3.43 us
    pallas_call x1, Pallas kernels, fast(): call(functools.partial(attend_kernel, p), (sds((p.n_col, p.own, p.per * p...  3.02 us
  transfers between devices with their start and end apart: 8, of which 7 were waited for; matrix products, arithmetic and copies ran while one was open for 1% of the time, Pallas kernels for 2%

profile of v6, /device:TPU:0, one launch (start us, length us, event | category | flops | bytes accessed | tf_op | source)
XLA Modules:
  0.0 72.1 jit_solution(3354523439992251140)
XLA Ops:
  0.6 2.5 %bias.1 = (bf16[32,32,128]{2,1,0:T(8,128)(2,1)}, bf16[4,40,256]{2,1,0:T(8,128)(2,1)}, bf16[4,40,256]{2,1,0:T(8,128)(2,1)}, bf16[4,40,256]{2,1,0:T(8,128)(2,1)}, bf16[4,40,256]{2,1,0:T(8,128)(2,1)}) custom-call(s32[1]{0:T(128)} %bitcast.col_ref, bf16[20,40,128]{2,1,0:T(8,128)(2,1)} %pair_ref.1, bf16[8,128]{1,0:T(8,128)(2,1)} %bitcast.34, ...), custom_call_target="tpu_custom_call" | custom-call | flops 400000000 | bytes 4000000 | tf_op jit(solution)/shard_map/bias/pallas_call | solution.py:499
  3.2 7.3 %all-to-all-start = ((bf16[32,32,128]{2,1,0:T(8,128)(2,1)}), bf16[32,32,128]{2,1,0:T(8,128)(2,1)S(1)}, u32[]{:S(2)}, u32[]{:S(2)}) async-start(bf16[32,32,128]{2,1,0:T(8,128)(2,1)} %get-tuple-element.28), calls=%async_computation | async-start | bytes 524288 | tf_op jit(solution)/shard_map/all_to_all | solution.py:505
  10.6 0.3 collective-permute-start
  10.9 1.6 %collective-permute-start.1 = (bf16[4,40,256]{2,1,0:T(8,128)(2,1)S(1)}, bf16[4,40,256]{2,1,0:T(8,128)(2,1)S(1)}, u32[]{:S(2)}, u32[]{:S(2)}) collective-permute-start(bf16[4,40,256]{2,1,0:T(8,128)(2,1)S(1)} %copy-done.9), channel_id=1, source_target_pairs={{0,2},{1,3},{2,0},{3,1},{4,6},{5,7},{6,4},{7,5},{8,10},{9,11},{10,... | collective-permute-start | bytes 245768 | tf_op jit(solution)/shard_map/ppermute | solution.py:509
  12.5 1.4 %collective-permute-start.2 = (bf16[4,40,256]{2,1,0:T(8,128)(2,1)S(1)}, bf16[4,40,256]{2,1,0:T(8,128)(2,1)S(1)}, u32[]{:S(2)}, u32[]{:S(2)}) collective-permute-start(bf16[4,40,256]{2,1,0:T(8,128)(2,1)S(1)} %copy-done.8), channel_id=1, source_target_pairs={{0,3},{1,0},{2,1},{3,2},{4,7},{5,4},{6,5},{7,6},{8,11},{9,8},{10,9... | collective-permute-start | bytes 245768 | tf_op jit(solution)/shard_map/ppermute | solution.py:509
  14.1 0.2 concatenate.9.ws_ref
  14.3 1.8 %collective-permute-done.refs_1_ = bf16[4,40,256]{2,1,0:T(8,128)(2,1)S(1)} collective-permute-done((bf16[4,40,256]{2,1,0:T(8,128)(2,1)S(1)}, bf16[4,40,256]{2,1,0:T(8,128)(2,1)S(1)}, u32[]{:S(2)}, u32[]{:S(2)}) %collective-permute-start) | collective-permute-done | bytes 81952 | tf_op jit(solution)/shard_map/ppermute | solution.py:509
  16.2 1.8 %collective-permute-done.1.refs_2_ = bf16[4,40,256]{2,1,0:T(8,128)(2,1)S(1)} collective-permute-done((bf16[4,40,256]{2,1,0:T(8,128)(2,1)S(1)}, bf16[4,40,256]{2,1,0:T(8,128)(2,1)S(1)}, u32[]{:S(2)}, u32[]{:S(2)}) %collective-permute-start.1) | collective-permute-done | bytes 81952 | tf_op jit(solution)/shard_map/ppermute | solution.py:509
  18.1 0.8 %project.1 = (bf16[4,96,256]{2,1,0:T(8,128)(2,1)S(1)}, bf16[4,160,256]{2,1,0:T(8,128)(2,1)S(1)}, bf16[4,160,256]{2,1,0:T(8,128)(2,1)S(1)}, f32[4,96,256]{2,1,0:T(8,128)S(1)}, bf16[4,96,256]{2,1,0:T(8,128)(2,1)S(1)}) custom-call(s32[1]{0:T(128)} %bitcast.col_ref, bf16[4,40,256]{2,1,0:T(8,128)(2,1)S(1)} %copy-done.4, ...), custom_call_target="tpu_custom_call" | custom-call | flops 400000000 | bytes 4000000 | tf_op jit(solution)/shard_map/project/pallas_call | solution.py:514
  18.9 2.2 %all-to-all-done.bias_ref = bf16[32,32,128]{2,1,0:T(8,128)(2,1)S(1)} async-done(((bf16[32,32,128]{2,1,0:T(8,128)(2,1)}), bf16[32,32,128]{2,1,0:T(8,128)(2,1)S(1)}, u32[]{:S(2)}, u32[]{:S(2)}) %all-to-all-start) | async-done | bytes 262176 | tf_op jit(solution)/shard_map/all_to_all | solution.py:505
  21.1 3.0 %attend.1 = (bf16[4,4,24,256]{3,2,1,0:T(8,128)(2,1)S(1)}, bf16[32,32,128]{2,1,0:T(8,128)(2,1)}) custom-call(s32[1]{0:T(128)} %bitcast.col_ref, bf16[4,96,256]{2,1,0:T(8,128)(2,1)S(1)} %get-tuple-element.23.q_ref, bf16[4,160,256]{2,1,0:T(8,128)(2,1)S(1)} %get-tuple-element.24.k_ref, bf16[4,160,256]{2,1,0:T(8,128)(2,1)S(1)} %get-tuple-element.25.v_ref, ...), custom_call_target="tpu_custom_call" | custom-call | flops 400000000 | bytes 4000000 | tf_op jit(solution)/shard_map/attend/pallas_call | solution.py:519
  24.2 3.6 %all-to-all-start.1 = ((bf16[32,32,128]{2,1,0:T(8,128)(2,1)}), bf16[32,32,128]{2,1,0:T(8,128)(2,1)S(1)}, u32[]{:S(2)}, u32[]{:S(2)}) async-start(bf16[32,32,128]{2,1,0:T(8,128)(2,1)} %get-tuple-element.29), calls=%async_computation.1 | async-start | bytes 524288 | tf_op jit(solution)/shard_map/all_to_all | solution.py:528
  28.0 0.3 collective-permute-start.3
  28.3 1.6 %collective-permute-start.4 = (bf16[4,24,256]{2,1,0:T(8,128)(2,1)S(1)}, bf16[4,24,256]{2,1,0:T(8,128)(2,1)S(1)}, u32[]{:S(2)}, u32[]{:S(2)}) collective-permute-start(bf16[4,24,256]{2,1,0:T(8,128)(2,1)S(1)} %get-tuple-element.37), channel_id=1, source_target_pairs={{0,2},{1,3},{2,0},{3,1},{4,6},{5,7},{6,4},{7,5},{8,10},{9,11},{10,... | collective-permute-start | bytes 147464 | tf_op jit(solution)/shard_map/ppermute | solution.py:509
  30.0 1.4 %collective-permute-start.5 = (bf16[4,24,256]{2,1,0:T(8,128)(2,1)S(1)}, bf16[4,24,256]{2,1,0:T(8,128)(2,1)S(1)}, u32[]{:S(2)}, u32[]{:S(2)}) collective-permute-start(bf16[4,24,256]{2,1,0:T(8,128)(2,1)S(1)} %get-tuple-element.36), channel_id=1, source_target_pairs={{0,3},{1,0},{2,1},{3,2},{4,7},{5,4},{6,5},{7,6},{8,11},{9,8},{10,9... | collective-permute-start | bytes 147464 | tf_op jit(solution)/shard_map/ppermute | solution.py:509
  31.5 1.0 %collective-permute-done.3.refs_1_ = bf16[4,24,256]{2,1,0:T(8,128)(2,1)S(1)} collective-permute-done((bf16[4,24,256]{2,1,0:T(8,128)(2,1)S(1)}, bf16[4,24,256]{2,1,0:T(8,128)(2,1)S(1)}, u32[]{:S(2)}, u32[]{:S(2)}) %collective-permute-start.3) | collective-permute-done | bytes 49184 | tf_op jit(solution)/shard_map/ppermute | solution.py:509
  32.6 1.6 %collective-permute-done.4.refs_2_ = bf16[4,24,256]{2,1,0:T(8,128)(2,1)S(1)} collective-permute-done((bf16[4,24,256]{2,1,0:T(8,128)(2,1)S(1)}, bf16[4,24,256]{2,1,0:T(8,128)(2,1)S(1)}, u32[]{:S(2)}, u32[]{:S(2)}) %collective-permute-start.4) | collective-permute-done | bytes 49184 | tf_op jit(solution)/shard_map/ppermute | solution.py:509
  34.2 0.7 home.1
  34.9 3.4 %all-to-all-done.1.recv_ref = bf16[32,32,128]{2,1,0:T(8,128)(2,1)S(1)} async-done(((bf16[32,32,128]{2,1,0:T(8,128)(2,1)}), bf16[32,32,128]{2,1,0:T(8,128)(2,1)S(1)}, u32[]{:S(2)}, u32[]{:S(2)}) %all-to-all-start.1) | async-done | bytes 262176 | tf_op jit(solution)/shard_map/all_to_all | solution.py:528
  38.3 2.5 %outer.1 = (bf16[20,40,128]{2,1,0:T(8,128)(2,1)S(1)}, bf16[32,56,128]{2,1,0:T(8,128)(2,1)S(1)}, f32[800,128]{1,0:T(8,128)S(1)}) custom-call(bf16[32,32,128]{2,1,0:T(8,128)(2,1)S(1)} %all-to-all-done.1.recv_ref, bf16[20,40,128]{2,1,0:T(8,128)(2,1)S(1)} %copy-done.2, bf16[1024,128]{1,0:T(8,128)(2,1)S(1)} %bitcast.26, ...), custom_call_target="tpu_custom_call" | custom-call | flops 400000000 | bytes 4000000 | tf_op jit(solution)/shard_map/outer/pallas_call | solution.py:536
  40.9 16.8 %all_to_all.20.recv_ref = bf16[32,56,128]{2,1,0:T(8,128)(2,1)S(1)} all-to-all(bf16[32,56,128]{2,1,0:T(8,128)(2,1)S(1)} %get-tuple-element.33), channel_id=1, replica_groups=mesh['row'=8,'col'=4] {'row','col'}, dimensions={0} | all-to-all | bytes 917504 | tf_op jit(solution)/shard_map/all_to_all | solution.py:547
  57.6 1.0 %triangle.1 = bf16[32,7,4,128]{3,2,1,0:T(4,128)(2,1)S(1)} custom-call(bf16[32,56,128]{2,1,0:T(8,128)(2,1)S(1)} %all_to_all.20.recv_ref), custom_call_target="tpu_custom_call" | custom-call | flops 400000000 | bytes 4000000 | tf_op jit(solution)/shard_map/triangle/pallas_call | solution.py:549
  58.6 12.4 %all_to_all.21.recv_ref = bf16[32,7,4,128]{3,2,1,0:T(4,128)(2,1)S(1)} all-to-all(bf16[32,7,4,128]{3,2,1,0:T(4,128)(2,1)S(1)} %triangle.1), channel_id=1, replica_groups=mesh['row'=8,'col'=4] {'row','col'}, dimensions={0} | all-to-all | bytes 458752 | tf_op jit(solution)/shard_map/all_to_all | solution.py:558
  71.0 1.1 %final.1 = bf16[20,40,128]{2,1,0:T(8,128)(2,1)} custom-call(bf16[32,7,4,128]{3,2,1,0:T(4,128)(2,1)S(1)} %all_to_all.21.recv_ref, bf16[20,40,128]{2,1,0:T(8,128)(2,1)S(1)} %get-tuple-element.34.mid_ref, f32[800,128]{1,0:T(8,128)S(1)} %get-tuple-element.35.gate_ref, bf16[128,128]{1,0:T(8,128)(2,1)S(1)} %copy-done.3), custom_call_target="tpu_custom_call" | custom-call | flops 400000000 | bytes 4000000 | tf_op jit(solution)/shard_map/final/pallas_call | solution.py:559
  (32 shorter events, 0.8 us)
Async XLA Ops:
  3.2 7.4 %copy-start.10 = (bf16[4,40,256]{2,1,0:T(8,128)(2,1)S(1)}, bf16[4,40,256]{2,1,0:T(8,128)(2,1)}, u32[]{:S(2)}) copy-start(bf16[4,40,256]{2,1,0:T(8,128)(2,1)} %get-tuple-element.20) | copy-start | bytes 245764
  3.2 7.7 %copy-start.9 = (bf16[4,40,256]{2,1,0:T(8,128)(2,1)S(1)}, bf16[4,40,256]{2,1,0:T(8,128)(2,1)}, u32[]{:S(2)}) copy-start(bf16[4,40,256]{2,1,0:T(8,128)(2,1)} %get-tuple-element.21) | copy-start | bytes 245764
  3.2 9.3 %copy-start.8 = (bf16[4,40,256]{2,1,0:T(8,128)(2,1)S(1)}, bf16[4,40,256]{2,1,0:T(8,128)(2,1)}, u32[]{:S(2)}) copy-start(bf16[4,40,256]{2,1,0:T(8,128)(2,1)} %get-tuple-element.22) | copy-start | bytes 245764
  3.2 10.7 %copy-start.7 = (bf16[256,64]{0,1:T(8,128)(2,1)S(1)}, bf16[256,64]{0,1:T(8,128)(2,1)}, u32[]{:S(2)}) copy-start(bf16[256,64]{0,1:T(8,128)(2,1)} %param.14) | copy-start | bytes 98308
  3.2 17.9 %all-to-all-start = ((bf16[32,32,128]{2,1,0:T(8,128)(2,1)}), bf16[32,32,128]{2,1,0:T(8,128)(2,1)S(1)}, u32[]{:S(2)}, u32[]{:S(2)}) async-start(bf16[32,32,128]{2,1,0:T(8,128)(2,1)} %get-tuple-element.28), calls=%async_computation | async-start | bytes 524288 | tf_op jit(solution)/shard_map/all_to_all | solution.py:505
  10.6 7.6 %copy-start.1 = (bf16[256,1024]{1,0:T(8,128)(2,1)S(1)}, bf16[256,1024]{1,0:T(8,128)(2,1)}, u32[]{:S(2)}) copy-start(bf16[256,1024]{1,0:T(8,128)(2,1)} %refs_4_.1) | copy-start | bytes 1572868
  10.6 5.6 %collective-permute-start = (bf16[4,40,256]{2,1,0:T(8,128)(2,1)S(1)}, bf16[4,40,256]{2,1,0:T(8,128)(2,1)S(1)}, u32[]{:S(2)}, u32[]{:S(2)}) collective-permute-start(bf16[4,40,256]{2,1,0:T(8,128)(2,1)S(1)} %copy-done.10), channel_id=1, source_target_pairs={{0,1},{1,2},{2,3},{3,0},{4,5},{5,6},{6,7},{7,4},{8,9},{9,10},{10,1... | collective-permute-start | bytes 245768 | tf_op jit(solution)/shard_map/ppermute | solution.py:509
  10.9 7.0 %collective-permute-start.1 = (bf16[4,40,256]{2,1,0:T(8,128)(2,1)S(1)}, bf16[4,40,256]{2,1,0:T(8,128)(2,1)S(1)}, u32[]{:S(2)}, u32[]{:S(2)}) collective-permute-start(bf16[4,40,256]{2,1,0:T(8,128)(2,1)S(1)} %copy-done.9), channel_id=1, source_target_pairs={{0,2},{1,3},{2,0},{3,1},{4,6},{5,7},{6,4},{7,5},{8,10},{9,11},{10,... | collective-permute-start | bytes 245768 | tf_op jit(solution)/shard_map/ppermute | solution.py:509
  12.5 5.6 %collective-permute-start.2 = (bf16[4,40,256]{2,1,0:T(8,128)(2,1)S(1)}, bf16[4,40,256]{2,1,0:T(8,128)(2,1)S(1)}, u32[]{:S(2)}, u32[]{:S(2)}) collective-permute-start(bf16[4,40,256]{2,1,0:T(8,128)(2,1)S(1)} %copy-done.8), channel_id=1, source_target_pairs={{0,3},{1,0},{2,1},{3,2},{4,7},{5,4},{6,5},{7,6},{8,11},{9,8},{10,9... | collective-permute-start | bytes 245768 | tf_op jit(solution)/shard_map/ppermute | solution.py:509
  14.1 4.0 %copy-start.4 = (bf16[4,40,256]{2,1,0:T(8,128)(2,1)S(1)}, bf16[4,40,256]{2,1,0:T(8,128)(2,1)}, u32[]{:S(2)}) copy-start(bf16[4,40,256]{2,1,0:T(8,128)(2,1)} %get-tuple-element.19.refs_0_) | copy-start | bytes 245764
  18.1 3.0 %copy-start = (bf16[256,256]{1,0:T(8,128)(2,1)S(1)}, bf16[256,256]{1,0:T(8,128)(2,1)}, u32[]{:S(2)}) copy-start(bf16[256,256]{1,0:T(8,128)(2,1)} %wf_ref.1) | copy-start | bytes 393220
  24.2 3.6 %copy-start.6 = (bf16[128,640]{1,0:T(8,128)(2,1)S(1)}, bf16[128,640]{1,0:T(8,128)(2,1)}, u32[]{:S(2)}) copy-start(bf16[128,640]{1,0:T(8,128)(2,1)} %param.16) | copy-start | bytes 491524
  24.2 14.1 %all-to-all-start.1 = ((bf16[32,32,128]{2,1,0:T(8,128)(2,1)}), bf16[32,32,128]{2,1,0:T(8,128)(2,1)S(1)}, u32[]{:S(2)}, u32[]{:S(2)}) async-start(bf16[32,32,128]{2,1,0:T(8,128)(2,1)} %get-tuple-element.29), calls=%async_computation.1 | async-start | bytes 524288 | tf_op jit(solution)/shard_map/all_to_all | solution.py:528
  28.0 3.4 %copy-start.5 = (bf16[1024,128]{1,0:T(8,128)(2,1)S(1)}, bf16[1024,128]{1,0:T(8,128)(2,1)}, u32[]{:S(2)}) copy-start(bf16[1024,128]{1,0:T(8,128)(2,1)} %param.15) | copy-start | bytes 786436
  28.0 4.5 %collective-permute-start.3 = (bf16[4,24,256]{2,1,0:T(8,128)(2,1)S(1)}, bf16[4,24,256]{2,1,0:T(8,128)(2,1)S(1)}, u32[]{:S(2)}, u32[]{:S(2)}) collective-permute-start(bf16[4,24,256]{2,1,0:T(8,128)(2,1)S(1)} %get-tuple-element.38), channel_id=1, source_target_pairs={{0,1},{1,2},{2,3},{3,0},{4,5},{5,6},{6,7},{7,4},{8,9},{9,10},{10,1... | collective-permute-start | bytes 147464 | tf_op jit(solution)/shard_map/ppermute | solution.py:509
  28.3 5.8 %collective-permute-start.4 = (bf16[4,24,256]{2,1,0:T(8,128)(2,1)S(1)}, bf16[4,24,256]{2,1,0:T(8,128)(2,1)S(1)}, u32[]{:S(2)}, u32[]{:S(2)}) collective-permute-start(bf16[4,24,256]{2,1,0:T(8,128)(2,1)S(1)} %get-tuple-element.37), channel_id=1, source_target_pairs={{0,2},{1,3},{2,0},{3,1},{4,6},{5,7},{6,4},{7,5},{8,10},{9,11},{10,... | collective-permute-start | bytes 147464 | tf_op jit(solution)/shard_map/ppermute | solution.py:509
  30.0 4.2 %collective-permute-start.5 = (bf16[4,24,256]{2,1,0:T(8,128)(2,1)S(1)}, bf16[4,24,256]{2,1,0:T(8,128)(2,1)S(1)}, u32[]{:S(2)}, u32[]{:S(2)}) collective-permute-start(bf16[4,24,256]{2,1,0:T(8,128)(2,1)S(1)} %get-tuple-element.36), channel_id=1, source_target_pairs={{0,3},{1,0},{2,1},{3,2},{4,7},{5,4},{6,5},{7,6},{8,11},{9,8},{10,9... | collective-permute-start | bytes 147464 | tf_op jit(solution)/shard_map/ppermute | solution.py:509
  34.2 4.2 %copy-start.2 = (bf16[20,40,128]{2,1,0:T(8,128)(2,1)S(1)}, bf16[20,40,128]{2,1,0:T(8,128)(2,1)}, u32[]{:S(2)}) copy-start(bf16[20,40,128]{2,1,0:T(8,128)(2,1)} %pair_ref.1) | copy-start | bytes 614404
  58.6 12.4 %copy-start.3 = (bf16[128,128]{1,0:T(8,128)(2,1)S(1)}, bf16[128,128]{1,0:T(8,128)(2,1)}, u32[]{:S(2)}) copy-start(bf16[128,128]{1,0:T(8,128)(2,1)} %w_ref.1) | copy-start | bytes 98308

commit v7 on v6

--- a/solution.py
+++ b/solution.py
@@ -419,7 +419,13 @@
     lane = lane_iota(p.m)
     part_of = jnp.broadcast_to(lane_iota(1) // p.jslot, (p.m, LANES))
     blocks = p.per * p.ig
-    rs[...] = jnp.zeros_like(rs)
+    for ch in range(p.ch):
+        for c in range(p.n_col):
+            for first in range(0, p.n_col, p.q):
+                many = min(p.q, p.n_col - first) * blocks * p.q
+                start, end = p.j_base(first) + many // SUBLANES * SUBLANES, p.j_base(first) + LANES
+                if start < end:
+                    rs[ch, c, start:end, :] = jnp.zeros((end - start, LANES), F32)
     for ch in range(p.ch):
         for c in range(p.n_col):
             left = flat[c, pl.ds(ch, p.m, stride=SUBLANES), :]

time: 72.4 us -> 72.4 us (level)
  no operation moved by 1% of the time
where the time goes in v7:
time: 72.4 us; the launch traced here: 72 us
  blocking collectives  29.1 us (40%)
  starting transfers between devices  17.5 us (24%)
  waiting for transfers between devices  12.1 us (17%)
  Pallas kernels  11.6 us (16%)
  between operations  0.88 us (1%)
  local copies, waits for them, and re-layouts  0.78 us (1%)
    all_to_all x1, blocking collectives, fast(): edges = lax.all_to_all(edges, ALL, 0, 0, tiled=True)  16.8 us
    all_to_all x1, blocking collectives, fast(): back = lax.all_to_all(back, ALL, 0, 0, tiled=True)  12.4 us
    all_to_all x1, starting transfers between devices, fast(): bias = lax.all_to_all(piece, ALL, 0, 0, tiled=True)  7.33 us
    ppermute x6, starting transfers between devices, ring(): lax.ppermute(parts[shift], 'col', [(c, (c + shift) % p.n_col) for c in ra...  6.57 us
    ppermute x6, waiting for transfers between devices, ring(): lax.ppermute(parts[shift], 'col', [(c, (c + shift) % p.n_col) for c in ra...  6.45 us
    all_to_all x1, starting transfers between devices, fast(): sides = lax.all_to_all(sides, ALL, 0, 0, tiled=True)  3.56 us
    all_to_all x1, waiting for transfers between devices, fast(): sides = lax.all_to_all(sides, ALL, 0, 0, tiled=True)  3.43 us
    pallas_call x1, Pallas kernels, fast(): call(functools.partial(attend_kernel, p), (sds((p.n_col, p.own, p.per * p...  3.02 us
  transfers between devices with their start and end apart: 8, of which 7 were waited for; matrix products, arithmetic and copies ran while one was open for 1% of the time, Pallas kernels for 2%

profile of v7, /device:TPU:0, one launch (start us, length us, event | category | flops | bytes accessed | tf_op | source)
XLA Modules:
  0.0 72.0 jit_solution(3934950891261209697)
XLA Ops:
  0.6 2.5 %bias.1 = (bf16[32,32,128]{2,1,0:T(8,128)(2,1)}, bf16[4,40,256]{2,1,0:T(8,128)(2,1)}, bf16[4,40,256]{2,1,0:T(8,128)(2,1)}, bf16[4,40,256]{2,1,0:T(8,128)(2,1)}, bf16[4,40,256]{2,1,0:T(8,128)(2,1)}) custom-call(s32[1]{0:T(128)} %bitcast.col_ref, bf16[20,40,128]{2,1,0:T(8,128)(2,1)} %pair_ref.1, bf16[8,128]{1,0:T(8,128)(2,1)} %bitcast.34, ...), custom_call_target="tpu_custom_call" | custom-call | flops 400000000 | bytes 4000000 | tf_op jit(solution)/shard_map/bias/pallas_call | solution.py:505
  3.2 7.3 %all-to-all-start = ((bf16[32,32,128]{2,1,0:T(8,128)(2,1)}), bf16[32,32,128]{2,1,0:T(8,128)(2,1)S(1)}, u32[]{:S(2)}, u32[]{:S(2)}) async-start(bf16[32,32,128]{2,1,0:T(8,128)(2,1)} %get-tuple-element.28), calls=%async_computation | async-start | bytes 524288 | tf_op jit(solution)/shard_map/all_to_all | solution.py:511
  10.6 0.3 collective-permute-start
  10.9 1.6 %collective-permute-start.1 = (bf16[4,40,256]{2,1,0:T(8,128)(2,1)S(1)}, bf16[4,40,256]{2,1,0:T(8,128)(2,1)S(1)}, u32[]{:S(2)}, u32[]{:S(2)}) collective-permute-start(bf16[4,40,256]{2,1,0:T(8,128)(2,1)S(1)} %copy-done.9), channel_id=1, source_target_pairs={{0,2},{1,3},{2,0},{3,1},{4,6},{5,7},{6,4},{7,5},{8,10},{9,11},{10,... | collective-permute-start | bytes 245768 | tf_op jit(solution)/shard_map/ppermute | solution.py:515
  12.5 1.4 %collective-permute-start.2 = (bf16[4,40,256]{2,1,0:T(8,128)(2,1)S(1)}, bf16[4,40,256]{2,1,0:T(8,128)(2,1)S(1)}, u32[]{:S(2)}, u32[]{:S(2)}) collective-permute-start(bf16[4,40,256]{2,1,0:T(8,128)(2,1)S(1)} %copy-done.8), channel_id=1, source_target_pairs={{0,3},{1,0},{2,1},{3,2},{4,7},{5,4},{6,5},{7,6},{8,11},{9,8},{10,9... | collective-permute-start | bytes 245768 | tf_op jit(solution)/shard_map/ppermute | solution.py:515
  14.1 0.2 concatenate.9.ws_ref
  14.3 1.8 %collective-permute-done.refs_1_ = bf16[4,40,256]{2,1,0:T(8,128)(2,1)S(1)} collective-permute-done((bf16[4,40,256]{2,1,0:T(8,128)(2,1)S(1)}, bf16[4,40,256]{2,1,0:T(8,128)(2,1)S(1)}, u32[]{:S(2)}, u32[]{:S(2)}) %collective-permute-start) | collective-permute-done | bytes 81952 | tf_op jit(solution)/shard_map/ppermute | solution.py:515
  16.2 1.8 %collective-permute-done.1.refs_2_ = bf16[4,40,256]{2,1,0:T(8,128)(2,1)S(1)} collective-permute-done((bf16[4,40,256]{2,1,0:T(8,128)(2,1)S(1)}, bf16[4,40,256]{2,1,0:T(8,128)(2,1)S(1)}, u32[]{:S(2)}, u32[]{:S(2)}) %collective-permute-start.1) | collective-permute-done | bytes 81952 | tf_op jit(solution)/shard_map/ppermute | solution.py:515
  18.1 0.8 %project.1 = (bf16[4,96,256]{2,1,0:T(8,128)(2,1)S(1)}, bf16[4,160,256]{2,1,0:T(8,128)(2,1)S(1)}, bf16[4,160,256]{2,1,0:T(8,128)(2,1)S(1)}, f32[4,96,256]{2,1,0:T(8,128)S(1)}, bf16[4,96,256]{2,1,0:T(8,128)(2,1)S(1)}) custom-call(s32[1]{0:T(128)} %bitcast.col_ref, bf16[4,40,256]{2,1,0:T(8,128)(2,1)S(1)} %copy-done.4, ...), custom_call_target="tpu_custom_call" | custom-call | flops 400000000 | bytes 4000000 | tf_op jit(solution)/shard_map/project/pallas_call | solution.py:520
  18.9 2.2 %all-to-all-done.bias_ref = bf16[32,32,128]{2,1,0:T(8,128)(2,1)S(1)} async-done(((bf16[32,32,128]{2,1,0:T(8,128)(2,1)}), bf16[32,32,128]{2,1,0:T(8,128)(2,1)S(1)}, u32[]{:S(2)}, u32[]{:S(2)}) %all-to-all-start) | async-done | bytes 262176 | tf_op jit(solution)/shard_map/all_to_all | solution.py:511
  21.1 3.0 %attend.1 = (bf16[4,4,24,256]{3,2,1,0:T(8,128)(2,1)S(1)}, bf16[32,32,128]{2,1,0:T(8,128)(2,1)}) custom-call(s32[1]{0:T(128)} %bitcast.col_ref, bf16[4,96,256]{2,1,0:T(8,128)(2,1)S(1)} %get-tuple-element.23.q_ref, bf16[4,160,256]{2,1,0:T(8,128)(2,1)S(1)} %get-tuple-element.24.k_ref, bf16[4,160,256]{2,1,0:T(8,128)(2,1)S(1)} %get-tuple-element.25.v_ref, ...), custom_call_target="tpu_custom_call" | custom-call | flops 400000000 | bytes 4000000 | tf_op jit(solution)/shard_map/attend/pallas_call | solution.py:525
  24.2 3.6 %all-to-all-start.1 = ((bf16[32,32,128]{2,1,0:T(8,128)(2,1)}), bf16[32,32,128]{2,1,0:T(8,128)(2,1)S(1)}, u32[]{:S(2)}, u32[]{:S(2)}) async-start(bf16[32,32,128]{2,1,0:T(8,128)(2,1)} %get-tuple-element.29), calls=%async_computation.1 | async-start | bytes 524288 | tf_op jit(solution)/shard_map/all_to_all | solution.py:534
  28.0 0.3 collective-permute-start.3
  28.3 1.6 %collective-permute-start.4 = (bf16[4,24,256]{2,1,0:T(8,128)(2,1)S(1)}, bf16[4,24,256]{2,1,0:T(8,128)(2,1)S(1)}, u32[]{:S(2)}, u32[]{:S(2)}) collective-permute-start(bf16[4,24,256]{2,1,0:T(8,128)(2,1)S(1)} %get-tuple-element.37), channel_id=1, source_target_pairs={{0,2},{1,3},{2,0},{3,1},{4,6},{5,7},{6,4},{7,5},{8,10},{9,11},{10,... | collective-permute-start | bytes 147464 | tf_op jit(solution)/shard_map/ppermute | solution.py:515
  30.0 1.4 %collective-permute-start.5 = (bf16[4,24,256]{2,1,0:T(8,128)(2,1)S(1)}, bf16[4,24,256]{2,1,0:T(8,128)(2,1)S(1)}, u32[]{:S(2)}, u32[]{:S(2)}) collective-permute-start(bf16[4,24,256]{2,1,0:T(8,128)(2,1)S(1)} %get-tuple-element.36), channel_id=1, source_target_pairs={{0,3},{1,0},{2,1},{3,2},{4,7},{5,4},{6,5},{7,6},{8,11},{9,8},{10,9... | collective-permute-start | bytes 147464 | tf_op jit(solution)/shard_map/ppermute | solution.py:515
  31.5 1.0 %collective-permute-done.3.refs_1_ = bf16[4,24,256]{2,1,0:T(8,128)(2,1)S(1)} collective-permute-done((bf16[4,24,256]{2,1,0:T(8,128)(2,1)S(1)}, bf16[4,24,256]{2,1,0:T(8,128)(2,1)S(1)}, u32[]{:S(2)}, u32[]{:S(2)}) %collective-permute-start.3) | collective-permute-done | bytes 49184 | tf_op jit(solution)/shard_map/ppermute | solution.py:515
  32.6 1.6 %collective-permute-done.4.refs_2_ = bf16[4,24,256]{2,1,0:T(8,128)(2,1)S(1)} collective-permute-done((bf16[4,24,256]{2,1,0:T(8,128)(2,1)S(1)}, bf16[4,24,256]{2,1,0:T(8,128)(2,1)S(1)}, u32[]{:S(2)}, u32[]{:S(2)}) %collective-permute-start.4) | collective-permute-done | bytes 49184 | tf_op jit(solution)/shard_map/ppermute | solution.py:515
  34.2 0.7 home.1
  34.9 3.4 %all-to-all-done.1.recv_ref = bf16[32,32,128]{2,1,0:T(8,128)(2,1)S(1)} async-done(((bf16[32,32,128]{2,1,0:T(8,128)(2,1)}), bf16[32,32,128]{2,1,0:T(8,128)(2,1)S(1)}, u32[]{:S(2)}, u32[]{:S(2)}) %all-to-all-start.1) | async-done | bytes 262176 | tf_op jit(solution)/shard_map/all_to_all | solution.py:534
  38.3 2.5 %outer.1 = (bf16[20,40,128]{2,1,0:T(8,128)(2,1)S(1)}, bf16[32,56,128]{2,1,0:T(8,128)(2,1)S(1)}, f32[800,128]{1,0:T(8,128)S(1)}) custom-call(bf16[32,32,128]{2,1,0:T(8,128)(2,1)S(1)} %all-to-all-done.1.recv_ref, bf16[20,40,128]{2,1,0:T(8,128)(2,1)S(1)} %copy-done.2, bf16[1024,128]{1,0:T(8,128)(2,1)S(1)} %bitcast.26, ...), custom_call_target="tpu_custom_call" | custom-call | flops 400000000 | bytes 4000000 | tf_op jit(solution)/shard_map/outer/pallas_call | solution.py:542
  40.9 16.8 %all_to_all.20.recv_ref = bf16[32,56,128]{2,1,0:T(8,128)(2,1)S(1)} all-to-all(bf16[32,56,128]{2,1,0:T(8,128)(2,1)S(1)} %get-tuple-element.33), channel_id=1, replica_groups=mesh['row'=8,'col'=4] {'row','col'}, dimensions={0} | all-to-all | bytes 917504 | tf_op jit(solution)/shard_map/all_to_all | solution.py:553
  57.6 0.9 %triangle.1 = bf16[32,7,4,128]{3,2,1,0:T(4,128)(2,1)S(1)} custom-call(bf16[32,56,128]{2,1,0:T(8,128)(2,1)S(1)} %all_to_all.20.recv_ref), custom_call_target="tpu_custom_call" | custom-call | flops 400000000 | bytes 4000000 | tf_op jit(solution)/shard_map/triangle/pallas_call | solution.py:555
  58.5 12.4 %all_to_all.21.recv_ref = bf16[32,7,4,128]{3,2,1,0:T(4,128)(2,1)S(1)} all-to-all(bf16[32,7,4,128]{3,2,1,0:T(4,128)(2,1)S(1)} %triangle.1), channel_id=1, replica_groups=mesh['row'=8,'col'=4] {'row','col'}, dimensions={0} | all-to-all | bytes 458752 | tf_op jit(solution)/shard_map/all_to_all | solution.py:564
  70.9 1.1 %final.1 = bf16[20,40,128]{2,1,0:T(8,128)(2,1)} custom-call(bf16[32,7,4,128]{3,2,1,0:T(4,128)(2,1)S(1)} %all_to_all.21.recv_ref, bf16[20,40,128]{2,1,0:T(8,128)(2,1)S(1)} %get-tuple-element.34.mid_ref, f32[800,128]{1,0:T(8,128)S(1)} %get-tuple-element.35.gate_ref, bf16[128,128]{1,0:T(8,128)(2,1)S(1)} %copy-done.3), custom_call_target="tpu_custom_call" | custom-call | flops 400000000 | bytes 4000000 | tf_op jit(solution)/shard_map/final/pallas_call | solution.py:565
  (32 shorter events, 0.8 us)
Async XLA Ops:
  3.2 7.4 %copy-start.10 = (bf16[4,40,256]{2,1,0:T(8,128)(2,1)S(1)}, bf16[4,40,256]{2,1,0:T(8,128)(2,1)}, u32[]{:S(2)}) copy-start(bf16[4,40,256]{2,1,0:T(8,128)(2,1)} %get-tuple-element.20) | copy-start | bytes 245764
  3.2 7.7 %copy-start.9 = (bf16[4,40,256]{2,1,0:T(8,128)(2,1)S(1)}, bf16[4,40,256]{2,1,0:T(8,128)(2,1)}, u32[]{:S(2)}) copy-start(bf16[4,40,256]{2,1,0:T(8,128)(2,1)} %get-tuple-element.21) | copy-start | bytes 245764
  3.2 9.3 %copy-start.8 = (bf16[4,40,256]{2,1,0:T(8,128)(2,1)S(1)}, bf16[4,40,256]{2,1,0:T(8,128)(2,1)}, u32[]{:S(2)}) copy-start(bf16[4,40,256]{2,1,0:T(8,128)(2,1)} %get-tuple-element.22) | copy-start | bytes 245764
  3.2 10.7 %copy-start.7 = (bf16[256,64]{0,1:T(8,128)(2,1)S(1)}, bf16[256,64]{0,1:T(8,128)(2,1)}, u32[]{:S(2)}) copy-start(bf16[256,64]{0,1:T(8,128)(2,1)} %param.14) | copy-start | bytes 98308
  3.2 17.9 %all-to-all-start = ((bf16[32,32,128]{2,1,0:T(8,128)(2,1)}), bf16[32,32,128]{2,1,0:T(8,128)(2,1)S(1)}, u32[]{:S(2)}, u32[]{:S(2)}) async-start(bf16[32,32,128]{2,1,0:T(8,128)(2,1)} %get-tuple-element.28), calls=%async_computation | async-start | bytes 524288 | tf_op jit(solution)/shard_map/all_to_all | solution.py:511
  10.6 7.6 %copy-start.1 = (bf16[256,1024]{1,0:T(8,128)(2,1)S(1)}, bf16[256,1024]{1,0:T(8,128)(2,1)}, u32[]{:S(2)}) copy-start(bf16[256,1024]{1,0:T(8,128)(2,1)} %refs_4_.1) | copy-start | bytes 1572868
  10.6 5.6 %collective-permute-start = (bf16[4,40,256]{2,1,0:T(8,128)(2,1)S(1)}, bf16[4,40,256]{2,1,0:T(8,128)(2,1)S(1)}, u32[]{:S(2)}, u32[]{:S(2)}) collective-permute-start(bf16[4,40,256]{2,1,0:T(8,128)(2,1)S(1)} %copy-done.10), channel_id=1, source_target_pairs={{0,1},{1,2},{2,3},{3,0},{4,5},{5,6},{6,7},{7,4},{8,9},{9,10},{10,1... | collective-permute-start | bytes 245768 | tf_op jit(solution)/shard_map/ppermute | solution.py:515
  10.9 7.0 %collective-permute-start.1 = (bf16[4,40,256]{2,1,0:T(8,128)(2,1)S(1)}, bf16[4,40,256]{2,1,0:T(8,128)(2,1)S(1)}, u32[]{:S(2)}, u32[]{:S(2)}) collective-permute-start(bf16[4,40,256]{2,1,0:T(8,128)(2,1)S(1)} %copy-done.9), channel_id=1, source_target_pairs={{0,2},{1,3},{2,0},{3,1},{4,6},{5,7},{6,4},{7,5},{8,10},{9,11},{10,... | collective-permute-start | bytes 245768 | tf_op jit(solution)/shard_map/ppermute | solution.py:515
  12.5 5.6 %collective-permute-start.2 = (bf16[4,40,256]{2,1,0:T(8,128)(2,1)S(1)}, bf16[4,40,256]{2,1,0:T(8,128)(2,1)S(1)}, u32[]{:S(2)}, u32[]{:S(2)}) collective-permute-start(bf16[4,40,256]{2,1,0:T(8,128)(2,1)S(1)} %copy-done.8), channel_id=1, source_target_pairs={{0,3},{1,0},{2,1},{3,2},{4,7},{5,4},{6,5},{7,6},{8,11},{9,8},{10,9... | collective-permute-start | bytes 245768 | tf_op jit(solution)/shard_map/ppermute | solution.py:515
  14.1 4.0 %copy-start.4 = (bf16[4,40,256]{2,1,0:T(8,128)(2,1)S(1)}, bf16[4,40,256]{2,1,0:T(8,128)(2,1)}, u32[]{:S(2)}) copy-start(bf16[4,40,256]{2,1,0:T(8,128)(2,1)} %get-tuple-element.19.refs_0_) | copy-start | bytes 245764
  18.1 3.0 %copy-start = (bf16[256,256]{1,0:T(8,128)(2,1)S(1)}, bf16[256,256]{1,0:T(8,128)(2,1)}, u32[]{:S(2)}) copy-start(bf16[256,256]{1,0:T(8,128)(2,1)} %wf_ref.1) | copy-start | bytes 393220
  24.2 3.6 %copy-start.6 = (bf16[128,640]{1,0:T(8,128)(2,1)S(1)}, bf16[128,640]{1,0:T(8,128)(2,1)}, u32[]{:S(2)}) copy-start(bf16[128,640]{1,0:T(8,128)(2,1)} %param.16) | copy-start | bytes 491524
  24.2 14.1 %all-to-all-start.1 = ((bf16[32,32,128]{2,1,0:T(8,128)(2,1)}), bf16[32,32,128]{2,1,0:T(8,128)(2,1)S(1)}, u32[]{:S(2)}, u32[]{:S(2)}) async-start(bf16[32,32,128]{2,1,0:T(8,128)(2,1)} %get-tuple-element.29), calls=%async_computation.1 | async-start | bytes 524288 | tf_op jit(solution)/shard_map/all_to_all | solution.py:534
  28.0 3.4 %copy-start.5 = (bf16[1024,128]{1,0:T(8,128)(2,1)S(1)}, bf16[1024,128]{1,0:T(8,128)(2,1)}, u32[]{:S(2)}) copy-start(bf16[1024,128]{1,0:T(8,128)(2,1)} %param.15) | copy-start | bytes 786436
  28.0 4.5 %collective-permute-start.3 = (bf16[4,24,256]{2,1,0:T(8,128)(2,1)S(1)}, bf16[4,24,256]{2,1,0:T(8,128)(2,1)S(1)}, u32[]{:S(2)}, u32[]{:S(2)}) collective-permute-start(bf16[4,24,256]{2,1,0:T(8,128)(2,1)S(1)} %get-tuple-element.38), channel_id=1, source_target_pairs={{0,1},{1,2},{2,3},{3,0},{4,5},{5,6},{6,7},{7,4},{8,9},{9,10},{10,1... | collective-permute-start | bytes 147464 | tf_op jit(solution)/shard_map/ppermute | solution.py:515
  28.3 5.8 %collective-permute-start.4 = (bf16[4,24,256]{2,1,0:T(8,128)(2,1)S(1)}, bf16[4,24,256]{2,1,0:T(8,128)(2,1)S(1)}, u32[]{:S(2)}, u32[]{:S(2)}) collective-permute-start(bf16[4,24,256]{2,1,0:T(8,128)(2,1)S(1)} %get-tuple-element.37), channel_id=1, source_target_pairs={{0,2},{1,3},{2,0},{3,1},{4,6},{5,7},{6,4},{7,5},{8,10},{9,11},{10,... | collective-permute-start | bytes 147464 | tf_op jit(solution)/shard_map/ppermute | solution.py:515
  30.0 4.2 %collective-permute-start.5 = (bf16[4,24,256]{2,1,0:T(8,128)(2,1)S(1)}, bf16[4,24,256]{2,1,0:T(8,128)(2,1)S(1)}, u32[]{:S(2)}, u32[]{:S(2)}) collective-permute-start(bf16[4,24,256]{2,1,0:T(8,128)(2,1)S(1)} %get-tuple-element.36), channel_id=1, source_target_pairs={{0,3},{1,0},{2,1},{3,2},{4,7},{5,4},{6,5},{7,6},{8,11},{9,8},{10,9... | collective-permute-start | bytes 147464 | tf_op jit(solution)/shard_map/ppermute | solution.py:515
  34.2 4.2 %copy-start.2 = (bf16[20,40,128]{2,1,0:T(8,128)(2,1)S(1)}, bf16[20,40,128]{2,1,0:T(8,128)(2,1)}, u32[]{:S(2)}) copy-start(bf16[20,40,128]{2,1,0:T(8,128)(2,1)} %pair_ref.1) | copy-start | bytes 614404
  58.5 12.4 %copy-start.3 = (bf16[128,128]{1,0:T(8,128)(2,1)S(1)}, bf16[128,128]{1,0:T(8,128)(2,1)}, u32[]{:S(2)}) copy-start(bf16[128,128]{1,0:T(8,128)(2,1)} %w_ref.1) | copy-start | bytes 98308
